TPU v7x, 32 devices: a whole 2x2x4 slice. The times are simulated.
32 devices in a mesh: dp: 16 (over z, x, core), seq: 2 (over y).
Axes of the slice: x: 2, y: 2, z: 4, core: 2. Of those that a mesh axis runs over, the one named last changes fastest.
Arguments:
- character_codes: int32 [16, 512, 50], P('dp', 'seq'), may hold values from 0 to 262
- word_lengths: int32 [16, 512], P('dp', 'seq'), may hold values from 1 to 50
- sequence_lengths: int32 [16], P('dp'), may hold values from 128 to 512, as said below
- character_table: bfloat16 [263, 16], replicated, may hold values from -6 to 6
- conv_width1: bfloat16 [16, 32], replicated, may hold values from -1.5 to 1.5
- conv_width2: bfloat16 [32, 32], replicated, may hold values from -1 to 1
- conv_width3: bfloat16 [48, 64], replicated, may hold values from -0.875 to 0.875
- conv_width4: bfloat16 [64, 128], replicated, may hold values from -0.75 to 0.75
- conv_width5: bfloat16 [80, 256], replicated, may hold values from -0.625 to 0.625
- conv_width6: bfloat16 [96, 512], replicated, may hold values from -0.625 to 0.625
- conv_width7: bfloat16 [112, 1024], replicated, may hold values from -0.5 to 0.5
- conv_bias: bfloat16 [2048], replicated, may hold values from -2.5 to -0.5
- highway_weight: bfloat16 [2048, 4096], P('dp'), may hold values from -0.125 to 0.125
- highway_bias: bfloat16 [4096], replicated, may hold values from -5 to 5
- projection: bfloat16 [2048, 768], P('dp'), may hold values from -0.125 to 0.125
- position_table: bfloat16 [512, 768], replicated, may hold values from -6 to 6
- attention_in: bfloat16 [768, 2304], P('dp'), may hold values from -0.3125 to 0.3125
- attention_out: bfloat16 [768, 768], P('dp'), may hold values from -0.875 to 0.875
- norm1_gain: bfloat16 [768], replicated, may hold values from 0.5 to 1.5
- norm1_bias: bfloat16 [768], replicated, may hold values from -1.5 to 1.5
- hidden_in: bfloat16 [768, 3072], P('dp'), may hold values from -0.21875 to 0.21875
- hidden_out: bfloat16 [3072, 768], P('dp'), may hold values from -0.15625 to 0.15625
- norm2_gain: bfloat16 [768], replicated, may hold values from 0.5 to 1.5
- norm2_bias: bfloat16 [768], replicated, may hold values from -1.5 to 1.5
- cotangent: bfloat16 [16, 512, 768], P('dp', 'seq'), may hold values from -6 to 6
Outputs:
- layer_out: bfloat16 [16, 512, 768], P('dp', 'seq')
- character_table_gradient: float32 [263, 16], replicated
- conv_width1_gradient: float32 [16, 32], replicated
- conv_width2_gradient: float32 [32, 32], replicated
- conv_width3_gradient: float32 [48, 64], replicated
- conv_width4_gradient: float32 [64, 128], replicated
- conv_width5_gradient: float32 [80, 256], replicated
- conv_width6_gradient: float32 [96, 512], replicated
- conv_width7_gradient: float32 [112, 1024], replicated
- conv_bias_gradient: float32 [2048], replicated
- highway_weight_gradient: float32 [2048, 4096], P('dp')
- highway_bias_gradient: float32 [4096], replicated
- projection_gradient: float32 [2048, 768], P('dp')
- position_table_gradient: float32 [512, 768], replicated
- attention_in_gradient: float32 [768, 2304], P('dp')
- attention_out_gradient: float32 [768, 768], P('dp')
- norm1_gain_gradient: float32 [768], replicated
- norm1_bias_gradient: float32 [768], replicated
- hidden_in_gradient: float32 [768, 3072], P('dp')
- hidden_out_gradient: float32 [3072, 768], P('dp')
- norm2_gain_gradient: float32 [768], replicated
- norm2_bias_gradient: float32 [768], replicated
Inputs may be any that keep to these rules, and one draw needn't show every extreme that they name: `sequence_lengths`: keys at or after a sequence's length take no part in attention; the first sequence has all 512 words.
All inputs are finite; a program needn't handle non-finite values.
Results may differ from a plain program's by a relative error of at most 0.028.
The roundings to bfloat16 on the way count: a program that leaves them out, or rounds other values in their place, can miss the bound.
Values may be sent and summed in bfloat16 or wider, within the bound.
No kernel may reach another device: no remote copies, remote signals or barrier semaphores. Data moves between devices by JAX's collectives and lax.ppermute only.
A program may use at most 256 MiB of HBM per device.

v0:
```python
from functools import partial
import math

import jax
import jax.numpy as jnp
from jax import lax
from jax.sharding import PartitionSpec as P

HEAD_DIM = 64


exact_gelu = partial(jax.nn.gelu, approximate=False)


def layer_norm(value, gain, bias):
    mean = jnp.mean(value, axis=-1, keepdims=True)
    centered = value - mean
    spread = jnp.mean(centered * centered, axis=-1, keepdims=True)
    return centered * lax.rsqrt(spread + 1e-12) * gain + bias


def highway_mix(gates, hidden):
    filters = hidden.shape[1]
    carry = jax.nn.sigmoid(gates[:, filters:])
    return carry * hidden + (1.0 - carry) * jax.nn.relu(gates[:, :filters])


def character_maps(codes, lengths, table, kernels):
    vocab = table.shape[0]
    features = table.shape[1]
    letters = codes.shape[1]
    onehot = (codes[:, :, None] == jnp.arange(vocab, dtype=jnp.int32)[None, None, :]).astype(
        jnp.bfloat16
    )
    embed = jnp.einsum("wcv,ve->wce", onehot, table, preferred_element_type=jnp.float32).astype(
        jnp.bfloat16
    )
    maps = []
    for kernel in kernels:
        width = kernel.shape[0] // features
        count = letters - width + 1
        window = jnp.concatenate(
            [embed[:, shift : shift + count] for shift in range(width)], axis=2
        )
        conv = jnp.einsum("wpk,kc->wpc", window, kernel, preferred_element_type=jnp.float32)
        limit = jnp.maximum(lengths - width + 1, 1)
        valid = jnp.arange(count, dtype=jnp.int32)[None, :] < limit[:, None]
        maps.append((window, jnp.where(valid[:, :, None], conv, -1e30)))
    return (onehot, maps)


def character_pool(codes, lengths, table, kernels):
    onehot, maps = character_maps(codes, lengths, table, kernels)
    return jnp.concatenate([jnp.max(entry[1], axis=1) for entry in maps], axis=1)


def character_back(codes, lengths, grad_block, table, kernels):
    onehot, maps = character_maps(codes, lengths, table, kernels)
    features = table.shape[1]
    letters = codes.shape[1]
    grad_embed = jnp.zeros((codes.shape[0], letters, features), jnp.float32)
    kernel_grads = []
    offset = 0
    for kernel, entry in zip(kernels, maps):
        window, masked = entry
        width = kernel.shape[0] // features
        channels = kernel.shape[1]
        count = letters - width + 1
        top = jnp.max(masked, axis=1, keepdims=True)
        hits = (masked == top).astype(jnp.float32)
        share = (
            grad_block[:, None, offset : offset + channels]
            * hits
            / jnp.sum(hits, axis=1, keepdims=True)
        )
        share = share.astype(jnp.bfloat16)
        offset = offset + channels
        kernel_grads.append(
            jnp.einsum("wpk,wpc->kc", window, share, preferred_element_type=jnp.float32)
        )
        grad_window = jnp.einsum("wpc,kc->wpk", share, kernel, preferred_element_type=jnp.float32)
        for shift in range(width):
            piece = grad_window[:, :, shift * features : (shift + 1) * features]
            grad_embed = grad_embed + jnp.pad(
                piece, ((0, 0), (shift, letters - count - shift), (0, 0))
            )
    table_grad = jnp.einsum(
        "wcv,wce->ve", onehot, grad_embed.astype(jnp.bfloat16), preferred_element_type=jnp.float32
    )
    return (tuple(kernel_grads), table_grad)


def score_heads(query_heads, key_heads, keep):
    raw = (
        jnp.einsum("qhd,khd->hqk", query_heads, key_heads, preferred_element_type=jnp.float32)
        * 0.125
    )
    return jnp.where(keep[None, None, :], raw, -1e30)


def body(
    character_codes,
    word_lengths,
    sequence_lengths,
    character_table,
    conv_width1,
    conv_width2,
    conv_width3,
    conv_width4,
    conv_width5,
    conv_width6,
    conv_width7,
    conv_bias,
    highway_weight,
    highway_bias,
    projection,
    position_table,
    attention_in,
    attention_out,
    norm1_gain,
    norm1_bias,
    hidden_in,
    hidden_out,
    norm2_gain,
    norm2_bias,
    cotangent,
):
    kernels = (
        conv_width1,
        conv_width2,
        conv_width3,
        conv_width4,
        conv_width5,
        conv_width6,
        conv_width7,
    )
    highway_full, projection_full = (
        lax.all_gather(highway_weight, "dp", axis=0, tiled=True),
        lax.all_gather(projection, "dp", axis=0, tiled=True),
    )
    codes = character_codes[0]
    lengths = word_lengths[0]
    words = codes.shape[0]
    letters = codes.shape[1]
    block = math.gcd(words, 32)
    code_blocks = codes.reshape(words // block, block, letters)
    length_blocks = lengths.reshape(words // block, block)
    pooled = lax.map(
        lambda pair: character_pool(pair[0], pair[1], character_table, kernels),
        (code_blocks, length_blocks),
    )
    pooled = pooled.reshape(words, pooled.shape[2])
    biased = pooled + conv_bias.astype(jnp.float32)
    hidden0 = jax.nn.relu(biased)
    hidden0_low = hidden0.astype(jnp.bfloat16)
    attention_full, output_full, inward_full, outward_full = (
        lax.all_gather(attention_in, "dp", axis=0, tiled=True),
        lax.all_gather(attention_out, "dp", axis=0, tiled=True),
        lax.all_gather(hidden_in, "dp", axis=0, tiled=True),
        lax.all_gather(hidden_out, "dp", axis=0, tiled=True),
    )
    gates = jnp.dot(
        hidden0_low, highway_full, preferred_element_type=jnp.float32
    ) + highway_bias.astype(jnp.float32)
    hidden1 = highway_mix(gates, hidden0)
    hidden1_low = hidden1.astype(jnp.bfloat16)
    offset = lax.axis_index("seq") * words
    positions = lax.dynamic_slice_in_dim(position_table, offset, words, 0).astype(jnp.float32)
    embedded = jnp.dot(hidden1_low, projection_full, preferred_element_type=jnp.float32) + positions
    embedded_low = embedded.astype(jnp.bfloat16)
    model = embedded.shape[1]
    heads = model // HEAD_DIM
    projected = jnp.dot(embedded_low, attention_full, preferred_element_type=jnp.float32).astype(
        jnp.bfloat16
    )
    gathered = lax.all_gather(projected[:, model:], "seq", axis=0, tiled=True)
    length = gathered.shape[0]
    query_heads = projected[:, :model].reshape(words, heads, HEAD_DIM)
    key_heads = gathered[:, :model].reshape(length, heads, HEAD_DIM)
    value_heads = gathered[:, model:].reshape(length, heads, HEAD_DIM)
    keep = jnp.arange(length, dtype=jnp.int32) < sequence_lengths[0]
    scores = score_heads(query_heads, key_heads, keep)
    top = jnp.max(scores, axis=-1, keepdims=True)
    unnormalized = jnp.exp(scores - top)
    total = jnp.sum(unnormalized, axis=-1, keepdims=True)
    probs_low = (unnormalized / total).astype(jnp.bfloat16)
    attended = jnp.einsum(
        "hqk,khd->qhd", probs_low, value_heads, preferred_element_type=jnp.float32
    )
    attended = attended.reshape(words, model).astype(jnp.bfloat16)
    joined = embedded + jnp.dot(attended, output_full, preferred_element_type=jnp.float32)
    gain1 = norm1_gain.astype(jnp.float32)
    shift1 = norm1_bias.astype(jnp.float32)
    gain2 = norm2_gain.astype(jnp.float32)
    shift2 = norm2_bias.astype(jnp.float32)
    normed1 = layer_norm(joined, gain1, shift1)
    normed1_low = normed1.astype(jnp.bfloat16)
    inner = jnp.dot(normed1_low, inward_full, preferred_element_type=jnp.float32)
    active = exact_gelu(inner).astype(jnp.bfloat16)
    summed = normed1 + jnp.dot(active, outward_full, preferred_element_type=jnp.float32)
    layer_out = layer_norm(summed, gain2, shift2).astype(jnp.bfloat16)
    seed_grad = cotangent[0].astype(jnp.float32)
    _, norm2_pull = jax.vjp(layer_norm, summed, gain2, shift2)
    grad_summed, norm2_gain_grad, norm2_bias_grad = norm2_pull(seed_grad)
    grad_outer = grad_summed.astype(jnp.bfloat16)
    hidden_out_grad = jnp.einsum(
        "tf,td->fd", active, grad_outer, preferred_element_type=jnp.float32
    )
    grad_active = jnp.einsum(
        "td,fd->tf", grad_outer, outward_full, preferred_element_type=jnp.float32
    )
    _, gelu_pull = jax.vjp(exact_gelu, inner)
    grad_inner = gelu_pull(grad_active)[0].astype(jnp.bfloat16)
    hidden_in_grad = jnp.einsum(
        "td,tf->df", normed1_low, grad_inner, preferred_element_type=jnp.float32
    )
    grad_normed1 = grad_summed + jnp.einsum(
        "tf,df->td", grad_inner, inward_full, preferred_element_type=jnp.float32
    )
    _, norm1_pull = jax.vjp(layer_norm, joined, gain1, shift1)
    grad_joined, norm1_gain_grad, norm1_bias_grad = norm1_pull(grad_normed1)
    grad_branch = grad_joined.astype(jnp.bfloat16)
    attention_out_grad = jnp.einsum(
        "td,te->de", attended, grad_branch, preferred_element_type=jnp.float32
    )
    grad_attended = jnp.einsum(
        "te,de->td", grad_branch, output_full, preferred_element_type=jnp.float32
    ).astype(jnp.bfloat16)
    grad_heads = grad_attended.reshape(words, heads, HEAD_DIM)
    probs = jnp.exp(score_heads(query_heads, key_heads, keep) - top) / total
    probs_again = probs.astype(jnp.bfloat16)
    grad_probs = jnp.einsum(
        "qhd,khd->hqk", grad_heads, value_heads, preferred_element_type=jnp.float32
    )
    grad_scores = (
        probs * (grad_probs - jnp.sum(probs * grad_probs, axis=-1, keepdims=True))
    ).astype(jnp.bfloat16)
    grad_query = (
        jnp.einsum("hqk,khd->qhd", grad_scores, key_heads, preferred_element_type=jnp.float32)
        * 0.125
    )
    count = lax.axis_size("seq") * words
    score_part = lax.slice_in_dim(grad_scores, 0, count, axis=2)
    prob_part = lax.slice_in_dim(probs_again, 0, count, axis=2)
    key_grad = (
        jnp.einsum("hqk,qhd->khd", score_part, query_heads, preferred_element_type=jnp.float32)
        * 0.125
    )
    value_grad = jnp.einsum(
        "hqk,qhd->khd", prob_part, grad_heads, preferred_element_type=jnp.float32
    )
    grad_pairs = lax.psum_scatter(
        jnp.concatenate(
            [key_grad.reshape(count, model), value_grad.reshape(count, model)], axis=1
        ).astype(jnp.bfloat16),
        "seq",
        scatter_dimension=0,
        tiled=True,
    ).astype(jnp.float32)
    grad_projected = jnp.concatenate([grad_query.reshape(words, model), grad_pairs], axis=1).astype(
        jnp.bfloat16
    )
    attention_in_grad = jnp.einsum(
        "td,te->de", embedded_low, grad_projected, preferred_element_type=jnp.float32
    )
    grad_embedded = grad_joined + jnp.einsum(
        "te,de->td", grad_projected, attention_full, preferred_element_type=jnp.float32
    )
    position_grad = lax.dynamic_update_slice_in_dim(
        jnp.zeros((length, model), jnp.float32), grad_embedded, offset, 0
    )
    grad_mapped = grad_embedded.astype(jnp.bfloat16)
    projection_grad = jnp.einsum(
        "tf,td->fd", hidden1_low, grad_mapped, preferred_element_type=jnp.float32
    )
    grad_hidden1 = jnp.einsum(
        "td,fd->tf", grad_mapped, projection_full, preferred_element_type=jnp.float32
    )
    _, highway_pull = jax.vjp(highway_mix, gates, hidden0)
    grad_gates, grad_carry = highway_pull(grad_hidden1)
    grad_gates = grad_gates.astype(jnp.bfloat16)
    highway_grad = jnp.einsum(
        "tf,tg->fg", hidden0_low, grad_gates, preferred_element_type=jnp.float32
    )
    highway_bias_grad = jnp.sum(grad_gates.astype(jnp.float32), axis=0)
    grad_hidden0 = grad_carry + jnp.einsum(
        "tg,fg->tf", grad_gates, highway_full, preferred_element_type=jnp.float32
    )
    grad_pooled = jnp.where(biased > 0, grad_hidden0, 0.0)
    conv_bias_grad = jnp.sum(grad_pooled, axis=0)
    grad_blocks = grad_pooled.reshape(words // block, block, grad_pooled.shape[1])

    def conv_step(carry, item):
        kernel_sum, table_sum = carry
        kernel_part, table_part = character_back(
            item[0], item[1], item[2], character_table, kernels
        )
        return ((jax.tree.map(jnp.add, kernel_sum, kernel_part), table_sum + table_part), None)

    start_sums = (
        tuple((jnp.zeros(kernel.shape, jnp.float32) for kernel in kernels)),
        jnp.zeros(character_table.shape, jnp.float32),
    )
    sums, _ = lax.scan(conv_step, start_sums, (code_blocks, length_blocks, grad_blocks))
    kernel_grads, table_grad = sums
    share_highway, share_projection, share_attention, share_output, share_inward, share_outward = (
        lax.psum_scatter(highway_grad, "dp", scatter_dimension=0, tiled=True),
        lax.psum_scatter(projection_grad, "dp", scatter_dimension=0, tiled=True),
        lax.psum_scatter(attention_in_grad, "dp", scatter_dimension=0, tiled=True),
        lax.psum_scatter(attention_out_grad, "dp", scatter_dimension=0, tiled=True),
        lax.psum_scatter(hidden_in_grad, "dp", scatter_dimension=0, tiled=True),
        lax.psum_scatter(hidden_out_grad, "dp", scatter_dimension=0, tiled=True),
    )
    highway_total, projection_total, attention_total, output_total, inward_total, outward_total = (
        lax.psum(share_highway.astype(jnp.bfloat16), "seq").astype(jnp.float32),
        lax.psum(share_projection.astype(jnp.bfloat16), "seq").astype(jnp.float32),
        lax.psum(share_attention.astype(jnp.bfloat16), "seq").astype(jnp.float32),
        lax.psum(share_output.astype(jnp.bfloat16), "seq").astype(jnp.float32),
        lax.psum(share_inward.astype(jnp.bfloat16), "seq").astype(jnp.float32),
        lax.psum(share_outward.astype(jnp.bfloat16), "seq").astype(jnp.float32),
    )
    small = lax.psum(
        (
            table_grad,
            kernel_grads[0],
            kernel_grads[1],
            kernel_grads[2],
            kernel_grads[3],
            kernel_grads[4],
            kernel_grads[5],
            kernel_grads[6],
            conv_bias_grad,
            highway_bias_grad,
            position_grad,
            norm1_gain_grad,
            norm1_bias_grad,
            norm2_gain_grad,
            norm2_bias_grad,
        ),
        ("dp", "seq"),
    )
    return (
        layer_out[None],
        small[0],
        small[1],
        small[2],
        small[3],
        small[4],
        small[5],
        small[6],
        small[7],
        small[8],
        highway_total,
        small[9],
        projection_total,
        small[10],
        attention_total,
        output_total,
        small[11],
        small[12],
        inward_total,
        outward_total,
        small[13],
        small[14],
    )


def solution(mesh):
    placed = (
        P("dp", "seq", None),
        P("dp", "seq"),
        P("dp"),
        P(),
        P(),
        P(),
        P(),
        P(),
        P(),
        P(),
        P(),
        P(),
        P("dp", None),
        P(),
        P("dp", None),
        P(),
        P("dp", None),
        P("dp", None),
        P(),
        P(),
        P("dp", None),
        P("dp", None),
        P(),
        P(),
        P("dp", "seq", None),
    )
    return jax.shard_map(
        body,
        mesh=mesh,
        in_specs=placed,
        out_specs=(
            P("dp", "seq", None),
            P(),
            P(),
            P(),
            P(),
            P(),
            P(),
            P(),
            P(),
            P(),
            P("dp", None),
            P(),
            P("dp", None),
            P(),
            P("dp", None),
            P("dp", None),
            P(),
            P(),
            P("dp", None),
            P("dp", None),
            P(),
            P(),
        ),
        check_vma=False,
    )
```

profile of v0, /device:TPU:0, one launch (start us, length us, event | category | flops | bytes accessed | tf_op | source)
XLA Modules:
  0.0 2102.8 jit_solution(11255074296748637753)
XLA Ops:
  14.3 119.6 %while.43 = (s32[]{:T(128)}, f32[8,32,2048]{2,1,0:T(8,128)S(1)}, s32[8,32]{1,0:T(8,128)}, s32[8,32,50]{2,1,0:T(8,128)}, bf16[263,16]{0,1:T(8,128)(2,1)}, /*index...) while((s32[]{:T(128)}, f32[8,32,2048]{2,1,0:T(8,128)S(1)}, ...), condition=%wide.region_8.9_spmd, body=%wide.region_0.8_spmd.sunk | while | flops 584907392 | bytes 8470321 | solution.py:148
  134.3 5.5 all-gather.8.cloned.1.call-done
  139.8 8.1 convolution_add_fusion.1
  150.8 34.9 %all-gather.10.cloned.1.call-done = bf16[2048,768]{1,0:T(8,128)(2,1)} async-done(((bf16[128,768]{1,0:T(8,128)(2,1)}), bf16[2048,768]{1,0:T(8,128)(2,1)}) %all-gather.10.cloned.1.call-update) | async-done | bytes 3145744 | tf_op jit(solution)/shard_map/all_gather | solution.py:139
  188.6 45.3 %all-gather.12.cloned.1.call-done = bf16[768,2304]{1,0:T(8,128)(2,1)} async-done(((bf16[48,2304]{1,0:T(8,128)(2,1)}), bf16[768,2304]{1,0:T(8,128)(2,1)}) %all-gather.12.cloned.1.call-update) | async-done | bytes 3538960 | tf_op jit(solution)/shard_map/all_gather | solution.py:157
  244.8 20.6 all-gather.14.cloned.1.call-done
  267.5 5.5 fusion.317
  277.0 28.9 %all-gather.16.cloned.1.call-done = bf16[768,768]{1,0:T(8,128)(2,1)} async-done(((bf16[48,768]{1,0:T(8,128)(2,1)}), bf16[768,768]{1,0:T(8,128)(2,1)}) %all-gather.16.cloned.1.call-update) | async-done | bytes 1179664 | tf_op jit(solution)/shard_map/all_gather | solution.py:158
  308.1 52.2 %all-gather.18.cloned.1.call-done = bf16[768,3072]{1,0:T(8,128)(2,1)} async-done(((bf16[48,3072]{1,0:T(8,128)(2,1)}), bf16[768,3072]{1,0:T(8,128)(2,1)}) %all-gather.18.cloned.1.call-update) | async-done | bytes 4718608 | tf_op jit(solution)/shard_map/all_gather | solution.py:159
  360.3 11.2 multiply_convert_fusion.1
  371.5 42.9 %all-gather.20.cloned.1.call-done = bf16[3072,768]{1,0:T(8,128)(2,1)} async-done(((bf16[192,768]{1,0:T(8,128)(2,1)}), bf16[3072,768]{1,0:T(8,128)(2,1)}) %all-gather.20.cloned.1.call-update) | async-done | bytes 4718608 | tf_op jit(solution)/shard_map/all_gather | solution.py:160
  443.9 18.5 reduce-scatter.8.cloned.1.call-done
  480.2 5.2 fusion.275
  487.0 5.1 fusion.272
  493.7 7.2 fusion.231
  502.9 13.8 fusion.279
  518.3 12.3 fusion.320
  532.1 85.6 %reduce-scatter.12.cloned.1.call-done = f32[128,768]{1,0:T(8,128)} async-done(((f32[2048,768]{1,0:T(8,128)}), f32[128,768]{1,0:T(8,128)}) %reduce-scatter.12.cloned.1.call-update) | async-done | bytes 393232 | tf_op jit(solution)/shard_map/reduce_scatter | solution.py:308
  619.4 92.0 %reduce-scatter.14.cloned.1.call-done = f32[48,2304]{1,0:T(8,128)} async-done(((f32[768,2304]{1,0:T(8,128)}), f32[48,2304]{1,0:T(8,128)}) %reduce-scatter.14.cloned.1.call-update) | async-done | bytes 442384 | tf_op jit(solution)/shard_map/reduce_scatter | solution.py:309
  713.1 113.1 %reduce-scatter.18.cloned.1.call-done = f32[48,3072]{1,0:T(8,128)} async-done(((f32[768,3072]{1,0:T(8,128)}), f32[48,3072]{1,0:T(8,128)}) %reduce-scatter.18.cloned.1.call-update) | async-done | bytes 589840 | tf_op jit(solution)/shard_map/reduce_scatter | solution.py:311
  828.1 114.0 %reduce-scatter.20.cloned.1.call-done = f32[192,768]{1,0:T(8,128)} async-done(((f32[3072,768]{1,0:T(8,128)}), f32[192,768]{1,0:T(8,128)}) %reduce-scatter.20.cloned.1.call-update) | async-done | bytes 589840 | tf_op jit(solution)/shard_map/reduce_scatter | solution.py:312
  943.9 334.8 %reduce-scatter.10.cloned.1.call-done = f32[128,4096]{1,0:T(8,128)} async-done(((f32[2048,4096]{1,0:T(8,128)}), f32[128,4096]{1,0:T(8,128)}) %reduce-scatter.10.cloned.1.call-update) | async-done | bytes 2097168 | tf_op jit(solution)/shard_map/reduce_scatter | solution.py:307
  1281.4 518.9 %while.44 = (s32[]{:T(128)}, f32[16,32]{1,0:T(8,128)}, f32[32,32]{1,0:T(8,128)}, f32[48,64]{1,0:T(8,128)}, f32[64,128]{1,0:T(8,128)}, /*index=5*/f32[80,256]{1,0...) while((s32[]{:T(128)}, f32[16,32]{1,0:T(8,128)}, ...), condition=%wide.region_36.37_spmd.clone, body=%wide.region_21.36_spmd.clone.sunk | while | flops 1773396992 | bytes 44253568 | solution.py:304
  1337.9 5.0 fusion.515
  1403.3 5.0 fusion.515
  1468.6 5.0 fusion.515
  1534.0 5.0 fusion.515
  1599.3 5.0 fusion.515
  1664.7 5.0 fusion.515
  1795.4 5.0 fusion.515
  1810.9 119.0 %all-reduce.36.cloned.1.call-done = (f32[263,16]{0,1:T(8,128)}, f32[16,32]{1,0:T(8,128)}, f32[32,32]{1,0:T(8,128)}, f32[48,64]{1,0:T(8,128)}, f32[64,128]{1,0:T(...) async-done(((f32[263,16]{0,1:T(8,128)}, f32[16,32]{1,0:T(8,128)}, f32[32,32]{1,0:T(8,128)}, ...) | async-done | bytes 104912 | tf_op jit(solution)/shard_map/psum | solution.py:322
  1929.9 146.9 %all-reduce.38.cloned.1.call-done = (f32[80,256]{1,0:T(8,128)}, f32[96,512]{1,0:T(8,128)}, f32[112,1024]{1,0:T(8,128)}, f32[512,768]{1,0:T(8,128)}) async-done(((f32[80,256]{1,0:T(8,128)}, f32[96,512]{1,0:T(8,128)}, f32[112,1024]{1,0:T(8,128)}, f32[512,768]{1,0:T(8,128)}), (f32[80,256]{1,0:T(8,128)}, f32[96,512]{1,0:T(8,128)}, f32[112,1024]{1,0:T(8,128)}, ...) | async-done | bytes 2310160 | tf_op jit(solution)/shard_map/psum | solution.py:322
  (1546 shorter events, 723.8 us)
Async XLA Ops:
  7.2 132.6 %all-gather.8.cloned.1.call-start = ((), (), s32[]{:S(2)}) async-start(), calls=%async_computation.7 | async-start | bytes 17825792 | tf_op jit(solution)/shard_map/all_gather | solution.py:138
  7.9 177.7 %all-gather.10.cloned.1.call-start = ((), (), s32[]{:S(2)}) async-start(), calls=%async_computation.8 | async-start | bytes 3342336 | tf_op jit(solution)/shard_map/all_gather | solution.py:139
  8.7 225.3 %all-gather.12.cloned.1.call-start = ((), (), s32[]{:S(2)}) async-start(), calls=%async_computation.9 | async-start | bytes 3760128 | tf_op jit(solution)/shard_map/all_gather | solution.py:157
  9.4 256.0 %all-gather.14.cloned.1.call-start = ((), (), s32[]{:S(2)}) async-start(), calls=%async_computation.10 | async-start | bytes 2359296 | tf_op jit(solution)/shard_map/all_gather | solution.py:176
  14.3 119.7 %copy-start.68 = (bf16[2048]{0:T(1024)(128)(2,1)S(1)}, bf16[2048]{0:T(1024)(128)(2,1)}, u32[]{:S(2)}) copy-start(bf16[2048]{0:T(1024)(128)(2,1)} %param.40) | copy-start | bytes 12292
  14.3 119.7 %copy-start.65 = (bf16[4096]{0:T(1024)(128)(2,1)S(1)}, bf16[4096]{0:T(1024)(128)(2,1)}, u32[]{:S(2)}) copy-start(bf16[4096]{0:T(1024)(128)(2,1)} %param.42) | copy-start | bytes 24580
  150.8 86.3 %copy-start.8 = (bf16[256,2048]{1,0:T(8,128)(2,1)}, bf16[256,2048]{1,0:T(8,128)(2,1)S(1)}, u32[]{:S(2)}) copy-start(bf16[256,2048]{1,0:T(8,128)(2,1)S(1)} %fusion.230) | copy-start | bytes 3145732
  188.6 117.4 %copy-start.19 = (f32[256,768]{1,0:T(8,128)}, f32[256,768]{1,0:T(8,128)S(1)}, u32[]{:S(2)}) copy-start(f32[256,768]{1,0:T(8,128)S(1)} %convolution_add_fusion.7) | copy-start | bytes 2359300
  188.6 53.3 %copy-start.74 = (bf16[768]{0:T(1024)(128)(2,1)S(1)}, bf16[768]{0:T(1024)(128)(2,1)}, u32[]{:S(2)}) copy-start(bf16[768]{0:T(1024)(128)(2,1)} %param.47) | copy-start | bytes 4612
  188.6 53.3 %copy-start.75 = (bf16[768]{0:T(1024)(128)(2,1)S(1)}, bf16[768]{0:T(1024)(128)(2,1)}, u32[]{:S(2)}) copy-start(bf16[768]{0:T(1024)(128)(2,1)} %param.51) | copy-start | bytes 4612
  188.6 53.9 %copy-start.76 = (bf16[768]{0:T(1024)(128)(2,1)S(1)}, bf16[768]{0:T(1024)(128)(2,1)}, u32[]{:S(2)}) copy-start(bf16[768]{0:T(1024)(128)(2,1)} %param.52) | copy-start | bytes 4612
  239.1 66.9 %all-gather.16.cloned.1.call-start = ((), (), s32[]{:S(2)}) async-start(), calls=%async_computation.11 | async-start | bytes 1253376 | tf_op jit(solution)/shard_map/all_gather | solution.py:158
  239.7 120.6 %all-gather.18.cloned.1.call-start = ((), (), s32[]{:S(2)}) async-start(), calls=%async_computation.12 | async-start | bytes 5013504 | tf_op jit(solution)/shard_map/all_gather | solution.py:159
  240.2 174.2 %all-gather.20.cloned.1.call-start = ((), (), s32[]{:S(2)}) async-start(), calls=%async_computation.13 | async-start | bytes 5013504 | tf_op jit(solution)/shard_map/all_gather | solution.py:160
  241.0 221.4 %reduce-scatter.8.cloned.1.call-start = ((), (), s32[]{:S(2)}) async-start(), calls=%async_computation.14 | async-start | bytes 2359296 | tf_op jit(solution)/shard_map/reduce_scatter | solution.py:252
  307.8 117.4 %copy-start = (f32[256,768]{1,0:T(8,128)}, f32[256,768]{1,0:T(8,128)S(1)}, u32[]{:S(2)}) copy-start(f32[256,768]{1,0:T(8,128)S(1)} %get-tuple-element.978) | copy-start | bytes 2359300
  307.8 106.6 %copy-start.52 = (f32[256]{0:T(256)}, f32[256]{0:T(256)S(1)}, u32[]{:S(2)}) copy-start(f32[256]{0:T(256)S(1)} %broadcast_multiply_fusion.1) | copy-start | bytes 3076
  308.0 63.4 %copy-start.62 = (f32[256]{0:T(256)}, f32[256]{0:T(256)S(1)}, u32[]{:S(2)}) copy-start(f32[256]{0:T(256)S(1)} %multiply_reduce_fusion.4) | copy-start | bytes 3076
  308.1 106.3 %copy-start.59 = (f32[256]{0:T(256)}, f32[256]{0:T(256)S(1)}, u32[]{:S(2)}) copy-start(f32[256]{0:T(256)S(1)} %fusion.266) | copy-start | bytes 3076
  437.6 93.0 %reduce-scatter.16.cloned.1.call-start = ((), (), s32[]{:S(2)}) async-start(), calls=%async_computation.18 | async-start | bytes 2506752 | tf_op jit(solution)/shard_map/reduce_scatter | solution.py:310
  440.9 176.8 %reduce-scatter.12.cloned.1.call-start = ((), (), s32[]{:S(2)}) async-start(), calls=%async_computation.16 | async-start | bytes 6684672 | tf_op jit(solution)/shard_map/reduce_scatter | solution.py:308
  472.8 238.6 %reduce-scatter.14.cloned.1.call-start = ((), (), s32[]{:S(2)}) async-start(), calls=%async_computation.17 | async-start | bytes 7520256 | tf_op jit(solution)/shard_map/reduce_scatter | solution.py:309
  478.5 347.8 %reduce-scatter.18.cloned.1.call-start = ((), (), s32[]{:S(2)}) async-start(), calls=%async_computation.19 | async-start | bytes 10027008 | tf_op jit(solution)/shard_map/reduce_scatter | solution.py:311
  485.4 456.7 %reduce-scatter.20.cloned.1.call-start = ((), (), s32[]{:S(2)}) async-start(), calls=%async_computation.20 | async-start | bytes 10027008 | tf_op jit(solution)/shard_map/reduce_scatter | solution.py:312
  492.1 786.5 %reduce-scatter.10.cloned.1.call-start = ((), (), s32[]{:S(2)}) async-start(), calls=%async_computation.15 | async-start | bytes 35651584 | tf_op jit(solution)/shard_map/reduce_scatter | solution.py:307
  516.7 1287.3 %all-reduce.40.cloned.1.call-start = ((), (), s32[]{:S(2)}) async-start(), calls=%async_computation.23 | async-start | bytes 4259840 | tf_op jit(solution)/shard_map/psum | solution.py:315
  1281.4 648.5 %all-reduce.36.cloned.1.call-start = ((), (), s32[]{:S(2)}) async-start(), calls=%async_computation.21 | async-start | bytes 294912 | tf_op jit(solution)/shard_map/psum | solution.py:322
  1803.4 273.3 %all-reduce.38.cloned.1.call-start = ((), (), s32[]{:S(2)}) async-start(), calls=%async_computation.22 | async-start | bytes 4620288 | tf_op jit(solution)/shard_map/psum | solution.py:322
  1929.9 163.8 %copy-start.72 = (f32[768]{0:T(1024)S(1)}, f32[768]{0:T(1024)}, u32[]{:S(2)}) copy-start(f32[768]{0:T(1024)} %get-tuple-element.1457) | copy-start | bytes 9220
  1929.9 164.4 %copy-start.71 = (f32[768]{0:T(1024)S(1)}, f32[768]{0:T(1024)}, u32[]{:S(2)}) copy-start(f32[768]{0:T(1024)} %get-tuple-element.1458) | copy-start | bytes 9220
  1929.9 165.0 %copy-start.70 = (f32[768]{0:T(1024)S(1)}, f32[768]{0:T(1024)}, u32[]{:S(2)}) copy-start(f32[768]{0:T(1024)} %get-tuple-element.1461) | copy-start | bytes 9220
  1929.9 165.6 %copy-start.69 = (f32[768]{0:T(1024)S(1)}, f32[768]{0:T(1024)}, u32[]{:S(2)}) copy-start(f32[768]{0:T(1024)} %get-tuple-element.1462) | copy-start | bytes 9220
  (268 other events, 885.3 us)
Sparse Core Ops, SparseCore 0:
  10.2 129.5 all-gather.7
  142.1 43.5 all-gather.9
  187.9 45.9 all-gather.11
  239.2 26.2 all-gather.13
  267.6 38.3 all-gather.15
  308.1 52.1 all-gather.17
  362.6 51.7 all-gather.19
  437.7 24.6 reduce-scatter.7
  466.6 62.9 reduce-scatter.15
  533.4 84.2 reduce-scatter.11
  622.2 89.1 reduce-scatter.13
  715.4 110.8 reduce-scatter.17
  830.9 111.1 reduce-scatter.19
  946.2 332.4 reduce-scatter.9
  1282.3 63.6 all-reduce.39
  1803.6 126.2 all-reduce.35
  1938.0 138.7 all-reduce.37
where the time goes:
time: 2120 us; the launch traced here: 2100 us
  waiting for transfers between devices  1260 us (59%)
  matrix products  601 us (28%)
  local copies, waits for them, and re-layouts  170 us (8%)
  other arithmetic  51.1 us (2%)
    reduce_scatter x1, waiting for transfers between devices, body(): lax.psum_scatter(highway_grad, 'dp', scatter_dimension=0, tiled=True)  335 us
    psum x2, waiting for transfers between devices, body(): lax.psum((table_grad, kernel_grads[0], kernel_grads[1], kernel_grads[2],...  266 us
    dot_general x56, matrix products, character_back(): jnp.einsum('wpk,wpc->kc', window, share, preferred_element_type=jnp.float32)  131 us
    eq x56, matrix products, character_back(): hits = (masked == top).astype(jnp.float32)  116 us
    reduce_scatter x1, waiting for transfers between devices, body(): lax.psum_scatter(hidden_out_grad, 'dp', scatter_dimension=0, tiled=True)  114 us
    reduce_scatter x1, waiting for transfers between devices, body(): lax.psum_scatter(hidden_in_grad, 'dp', scatter_dimension=0, tiled=True)  113 us
    dot_general x48, matrix products, character_back(): jnp.einsum('wpc,kc->wpk', share, kernel, preferred_element_type=jnp.float32)  103 us
    reduce_scatter x1, waiting for transfers between devices, body(): lax.psum_scatter(attention_in_grad, 'dp', scatter_dimension=0, tiled=True)  92 us
  transfers between devices with their start and end apart: 17, of which 15 were waited for; matrix products, arithmetic and copies ran while one was open for 35% of the time, Pallas kernels for 0%

commit v1 on v0

--- a/solution.py
+++ b/solution.py
@@ -4,6 +4,8 @@
 import jax
 import jax.numpy as jnp
 from jax import lax
+from jax.experimental import pallas as pl
+from jax.experimental.pallas import tpu as pltpu
 from jax.sharding import PartitionSpec as P
 
 HEAD_DIM = 64
@@ -25,69 +27,162 @@
     return carry * hidden + (1.0 - carry) * jax.nn.relu(gates[:, :filters])
 
 
-def character_maps(codes, lengths, table, kernels):
-    vocab = table.shape[0]
-    features = table.shape[1]
-    letters = codes.shape[1]
-    onehot = (codes[:, :, None] == jnp.arange(vocab, dtype=jnp.int32)[None, None, :]).astype(
-        jnp.bfloat16
-    )
-    embed = jnp.einsum("wcv,ve->wce", onehot, table, preferred_element_type=jnp.float32).astype(
-        jnp.bfloat16
-    )
-    maps = []
+WIDTHS = 7
+LANES = 128
+NEG = -1e30
+
+
+def conv_forward_kernel(spread_ref, lens_ref, weight_ref, pooled_ref, ties_ref, window_ref, flipped_ref, scores_ref):
+    letters, words, _ = spread_ref.shape
+    channels = weight_ref.shape[1]
+    lane = lax.broadcasted_iota(jnp.int32, (words, LANES), 1)
+    slot = lane // 16
+    limit = jnp.maximum(lens_ref[...] - (lane - 16 * WIDTHS), 1)
+    for p in range(letters):
+        window = jnp.zeros((words, LANES), jnp.float32)
+        for j in range(WIDTHS):
+            if p + j < letters:
+                window = jnp.where(slot == j, spread_ref[p + j].astype(jnp.float32), window)
+        flag = jnp.where((lane >= 16 * WIDTHS) & (lane < 17 * WIDTHS) & (p >= limit), 1.0, window)
+        window_ref[p * words:(p + 1) * words] = flag.astype(jnp.bfloat16)
+    flipped_ref[...] = window_ref[...].T
+    tile = 256
+    for c in range(0, channels, tile):
+        scores_ref[...] = jnp.dot(window_ref[...], weight_ref[:, c:c + tile], preferred_element_type=jnp.float32)
+        for r in range(0, words, 16):
+            top = scores_ref[r:r + 16]
+            for p in range(1, letters):
+                top = jnp.maximum(top, scores_ref[p * words + r:p * words + r + 16])
+            count = jnp.zeros((16, tile), jnp.float32)
+            for p in range(letters):
+                count += jnp.where(scores_ref[p * words + r:p * words + r + 16] == top, 1.0, 0.0)
+            pooled_ref[r:r + 16, c:c + tile] = top
+            ties_ref[r:r + 16, c:c + tile] = count
+
+
+def conv_backward_kernel(window_ref, flipped_ref, codes_ref, weight_ref, turned_ref, pooled_ref, share_in_ref,
+                         grad_ref, table_ref, share_ref, scores_ref, spread_ref, letters):
+    rows = window_ref.shape[0]
+    words = rows // letters
+    channels = weight_ref.shape[1]
+    vocab = table_ref.shape[0]
+    tile = 256
+
+    @pl.when(pl.program_id(0) == 0)
+    def _():
+        grad_ref[...] = jnp.zeros_like(grad_ref)
+        table_ref[...] = jnp.zeros_like(table_ref)
+
+    for c in range(0, channels, tile):
+        scores_ref[...] = jnp.dot(window_ref[...], weight_ref[:, c:c + tile], preferred_element_type=jnp.float32)
+        for r in range(0, words, 16):
+            top = pooled_ref[r:r + 16, c:c + tile]
+            part = share_in_ref[r:r + 16, c:c + tile]
+            for p in range(letters):
+                hit = scores_ref[p * words + r:p * words + r + 16] == top
+                share_ref[p * words + r:p * words + r + 16, c:c + tile] = jnp.where(hit, part, 0.0).astype(jnp.bfloat16)
+    grad_ref[...] += jnp.dot(flipped_ref[...], share_ref[...], preferred_element_type=jnp.float32)
+    scores_ref[:, :LANES] = jnp.dot(share_ref[...], turned_ref[...], preferred_element_type=jnp.float32)
+    slot = lax.broadcasted_iota(jnp.int32, (words, LANES), 1) // 16
+    for c in range(letters):
+        spread = jnp.zeros((words, LANES), jnp.float32)
+        for j in range(WIDTHS):
+            if c - j >= 0:
+                spread = jnp.where(slot == j, scores_ref[(c - j) * words:(c - j + 1) * words, :LANES], spread)
+        spread_ref[c * words:(c + 1) * words] = spread.astype(jnp.bfloat16)
+    onehot = jnp.where(lax.broadcasted_iota(jnp.int32, (vocab, rows), 0) == codes_ref[0], 1.0, 0.0).astype(jnp.bfloat16)
+    table_ref[...] += jnp.dot(onehot, spread_ref[...], preferred_element_type=jnp.float32)
+
+
+def conv_forward(spread, lens, weight, block):
+    letters, words, _ = spread.shape
+    channels = weight.shape[1]
+    steps = words // block
+    rows = letters * block
+    f32 = jnp.float32
+    return pl.pallas_call(
+        conv_forward_kernel,
+        grid=(steps,),
+        in_specs=[
+            pl.BlockSpec((letters, block, LANES), lambda i: (0, i, 0)),
+            pl.BlockSpec((block, 1), lambda i: (i, 0)),
+            pl.BlockSpec((LANES, channels), lambda i: (0, 0)),
+        ],
+        out_specs=[
+            pl.BlockSpec((block, channels), lambda i: (i, 0)),
+            pl.BlockSpec((block, channels), lambda i: (i, 0)),
+            pl.BlockSpec((rows, LANES), lambda i: (i, 0)),
+            pl.BlockSpec((LANES, rows), lambda i: (0, i)),
+        ],
+        out_shape=[
+            jax.ShapeDtypeStruct((words, channels), f32),
+            jax.ShapeDtypeStruct((words, channels), f32),
+            jax.ShapeDtypeStruct((steps * rows, LANES), jnp.bfloat16),
+            jax.ShapeDtypeStruct((LANES, steps * rows), jnp.bfloat16),
+        ],
+        scratch_shapes=[pltpu.VMEM((rows, 256), f32)],
+        compiler_params=pltpu.CompilerParams(dimension_semantics=("arbitrary",)),
+        name="conv_forward",
+    )(spread, lens, weight)
+
+
+def conv_backward(window, flipped, codes, weight, turned, pooled, share, vocab, block):
+    words, channels = pooled.shape
+    steps = words // block
+    rows = window.shape[0] // steps
+    letters = rows // block
+    f32 = jnp.float32
+    vocab = -(-vocab // 16) * 16
+
+    def kernel(*refs):
+        conv_backward_kernel(*refs, letters=letters)
+
+    return pl.pallas_call(
+        kernel,
+        grid=(steps,),
+        in_specs=[
+            pl.BlockSpec((rows, LANES), lambda i: (i, 0)),
+            pl.BlockSpec((LANES, rows), lambda i: (0, i)),
+            pl.BlockSpec((1, 1, rows), lambda i: (i, 0, 0)),
+            pl.BlockSpec((LANES, channels), lambda i: (0, 0)),
+            pl.BlockSpec((channels, LANES), lambda i: (0, 0)),
+            pl.BlockSpec((block, channels), lambda i: (i, 0)),
+            pl.BlockSpec((block, channels), lambda i: (i, 0)),
+        ],
+        out_specs=[
+            pl.BlockSpec((LANES, channels), lambda i: (0, 0)),
+            pl.BlockSpec((vocab, LANES), lambda i: (0, 0)),
+        ],
+        out_shape=[
+            jax.ShapeDtypeStruct((LANES, channels), f32),
+            jax.ShapeDtypeStruct((vocab, LANES), f32),
+        ],
+        scratch_shapes=[
+            pltpu.VMEM((rows, channels), jnp.bfloat16),
+            pltpu.VMEM((rows, 256), f32),
+            pltpu.VMEM((rows, LANES), jnp.bfloat16),
+        ],
+        compiler_params=pltpu.CompilerParams(dimension_semantics=("arbitrary",)),
+        name="conv_backward",
+    )(window, flipped, codes, weight, turned, pooled, share)
+
+
+def merged_weight(kernels, features):
+    columns = []
     for kernel in kernels:
         width = kernel.shape[0] // features
-        count = letters - width + 1
-        window = jnp.concatenate(
-            [embed[:, shift : shift + count] for shift in range(width)], axis=2
-        )
-        conv = jnp.einsum("wpk,kc->wpc", window, kernel, preferred_element_type=jnp.float32)
-        limit = jnp.maximum(lengths - width + 1, 1)
-        valid = jnp.arange(count, dtype=jnp.int32)[None, :] < limit[:, None]
-        maps.append((window, jnp.where(valid[:, :, None], conv, -1e30)))
-    return (onehot, maps)
-
-
-def character_pool(codes, lengths, table, kernels):
-    onehot, maps = character_maps(codes, lengths, table, kernels)
-    return jnp.concatenate([jnp.max(entry[1], axis=1) for entry in maps], axis=1)
-
-
-def character_back(codes, lengths, grad_block, table, kernels):
-    onehot, maps = character_maps(codes, lengths, table, kernels)
-    features = table.shape[1]
-    letters = codes.shape[1]
-    grad_embed = jnp.zeros((codes.shape[0], letters, features), jnp.float32)
-    kernel_grads = []
-    offset = 0
-    for kernel, entry in zip(kernels, maps):
-        window, masked = entry
-        width = kernel.shape[0] // features
         channels = kernel.shape[1]
-        count = letters - width + 1
-        top = jnp.max(masked, axis=1, keepdims=True)
-        hits = (masked == top).astype(jnp.float32)
-        share = (
-            grad_block[:, None, offset : offset + channels]
-            * hits
-            / jnp.sum(hits, axis=1, keepdims=True)
-        )
-        share = share.astype(jnp.bfloat16)
-        offset = offset + channels
-        kernel_grads.append(
-            jnp.einsum("wpk,wpc->kc", window, share, preferred_element_type=jnp.float32)
-        )
-        grad_window = jnp.einsum("wpc,kc->wpk", share, kernel, preferred_element_type=jnp.float32)
-        for shift in range(width):
-            piece = grad_window[:, :, shift * features : (shift + 1) * features]
-            grad_embed = grad_embed + jnp.pad(
-                piece, ((0, 0), (shift, letters - count - shift), (0, 0))
-            )
-    table_grad = jnp.einsum(
-        "wcv,wce->ve", onehot, grad_embed.astype(jnp.bfloat16), preferred_element_type=jnp.float32
-    )
-    return (tuple(kernel_grads), table_grad)
+        marks = jnp.zeros((LANES - WIDTHS * features, channels), kernel.dtype).at[width - 1].set(NEG)
+        columns.append(jnp.concatenate([kernel, jnp.zeros(((WIDTHS - width) * features, channels), kernel.dtype), marks], axis=0))
+    return jnp.concatenate(columns, axis=1)
+
+
+def spread_letters(codes, table):
+    vocab, features = table.shape
+    words, letters = codes.shape
+    wide = jnp.tile(table, (1, LANES // features))
+    onehot = (codes.T.reshape(-1, 1) == jnp.arange(vocab, dtype=jnp.int32)[None, :]).astype(jnp.bfloat16)
+    return jnp.dot(onehot, wide, preferred_element_type=jnp.float32).astype(jnp.bfloat16).reshape(letters, words, LANES)
 
 
 def score_heads(query_heads, key_heads, keep):
@@ -142,14 +237,13 @@
     lengths = word_lengths[0]
     words = codes.shape[0]
     letters = codes.shape[1]
-    block = math.gcd(words, 32)
-    code_blocks = codes.reshape(words // block, block, letters)
-    length_blocks = lengths.reshape(words // block, block)
-    pooled = lax.map(
-        lambda pair: character_pool(pair[0], pair[1], character_table, kernels),
-        (code_blocks, length_blocks),
-    )
-    pooled = pooled.reshape(words, pooled.shape[2])
+    block = math.gcd(words, 64)
+    steps = words // block
+    features = character_table.shape[1]
+    conv_weight = merged_weight(kernels, features)
+    pooled, ties, windows, flipped = conv_forward(
+        spread_letters(codes, character_table), lengths[:, None], conv_weight, block
+    )
     biased = pooled + conv_bias.astype(jnp.float32)
     hidden0 = jax.nn.relu(biased)
     hidden0_low = hidden0.astype(jnp.bfloat16)
@@ -288,28 +382,34 @@
     )
     grad_pooled = jnp.where(biased > 0, grad_hidden0, 0.0)
     conv_bias_grad = jnp.sum(grad_pooled, axis=0)
-    grad_blocks = grad_pooled.reshape(words // block, block, grad_pooled.shape[1])
-
-    def conv_step(carry, item):
-        kernel_sum, table_sum = carry
-        kernel_part, table_part = character_back(
-            item[0], item[1], item[2], character_table, kernels
-        )
-        return ((jax.tree.map(jnp.add, kernel_sum, kernel_part), table_sum + table_part), None)
-
-    start_sums = (
-        tuple((jnp.zeros(kernel.shape, jnp.float32) for kernel in kernels)),
-        jnp.zeros(character_table.shape, jnp.float32),
-    )
-    sums, _ = lax.scan(conv_step, start_sums, (code_blocks, length_blocks, grad_blocks))
-    kernel_grads, table_grad = sums
+    code_rows = codes.reshape(steps, block, letters).transpose(0, 2, 1)
+    merged_grad, table_wide = conv_backward(
+        windows,
+        flipped,
+        code_rows.reshape(steps, 1, letters * block),
+        conv_weight,
+        conv_weight.T,
+        pooled,
+        grad_pooled / ties,
+        character_table.shape[0],
+        block,
+    )
+    table_grad = sum(
+        table_wide[: character_table.shape[0], shift * features : (shift + 1) * features]
+        for shift in range(WIDTHS)
+    )
+    kernel_grads = []
+    first = 0
+    for kernel in kernels:
+        kernel_grads.append(merged_grad[: kernel.shape[0], first : first + kernel.shape[1]])
+        first = first + kernel.shape[1]
     share_highway, share_projection, share_attention, share_output, share_inward, share_outward = (
-        lax.psum_scatter(highway_grad, "dp", scatter_dimension=0, tiled=True),
-        lax.psum_scatter(projection_grad, "dp", scatter_dimension=0, tiled=True),
-        lax.psum_scatter(attention_in_grad, "dp", scatter_dimension=0, tiled=True),
-        lax.psum_scatter(attention_out_grad, "dp", scatter_dimension=0, tiled=True),
-        lax.psum_scatter(hidden_in_grad, "dp", scatter_dimension=0, tiled=True),
-        lax.psum_scatter(hidden_out_grad, "dp", scatter_dimension=0, tiled=True),
+        lax.psum_scatter(highway_grad.astype(jnp.bfloat16), "dp", scatter_dimension=0, tiled=True),
+        lax.psum_scatter(projection_grad.astype(jnp.bfloat16), "dp", scatter_dimension=0, tiled=True),
+        lax.psum_scatter(attention_in_grad.astype(jnp.bfloat16), "dp", scatter_dimension=0, tiled=True),
+        lax.psum_scatter(attention_out_grad.astype(jnp.bfloat16), "dp", scatter_dimension=0, tiled=True),
+        lax.psum_scatter(hidden_in_grad.astype(jnp.bfloat16), "dp", scatter_dimension=0, tiled=True),
+        lax.psum_scatter(hidden_out_grad.astype(jnp.bfloat16), "dp", scatter_dimension=0, tiled=True),
     )
     highway_total, projection_total, attention_total, output_total, inward_total, outward_total = (
         lax.psum(share_highway.astype(jnp.bfloat16), "seq").astype(jnp.float32),

time: 2120 us -> 1380 us (0.65)
  matrix products: 601 us -> 117 us
  waiting for transfers between devices: 1260 us -> 1080 us
  local copies, waits for them, and re-layouts: 170 us -> 48.7 us
  Pallas kernels: 0 us -> 85.5 us
  other arithmetic: 51.1 us -> 23.2 us
    dot_general x184 -> x1, matrix products: 371 us -> 4.4 us  [spread_letters(): jnp.dot(onehot, wide, preferred_element_type=jnp.float32)]
    reduce_scatter x6, waiting for transfers between devices: 740 us -> 428 us  [the longest x1 182 us: body(): lax.psum_scatter(highway_grad.astype(jnp.bfloat16), 'dp', scatter_dimensi...]
    eq x56 -> x0, matrix products: 116 us -> none  [character_back(): hits = (masked == top).astype(jnp.float32)]
    pallas_call x0 -> x2, Pallas kernels: none -> 85.5 us  [the longest x1 56.5 us: conv_backward(): pl.pallas_call(kernel, grid=(steps,), in_specs=[pl.BlockSpec((rows, LANES...]
    all_gather x1, waiting for transfers between devices: 5.52 us -> 81.6 us  [body(): lax.all_gather(highway_weight, 'dp', axis=0, tiled=True)]
    psum x1, waiting for transfers between devices: 0.02 us -> 64.6 us  [body(): lax.psum(share_highway.astype(jnp.bfloat16), 'seq').astype(jnp.float32)]
    while x657 -> x0, local copies, waits for them, and re-layouts: 51.4 us -> none
    slice x144 -> x7, local copies, waits for them, and re-layouts: 49.6 us -> 7.65 us  [body(): merged_grad[:kernel.shape[0], first:first + kernel.shape[1]]]
  transfers between devices with their start and end apart: 17 -> 17, of which waited for: 15 -> 16; matrix products, arithmetic and copies ran while one was open for 35% -> 10% of each run, Pallas kernels for 0% -> 6%
where the time goes in v1:
time: 1380 us; the launch traced here: 1370 us
  waiting for transfers between devices  1080 us (78%)
  matrix products  117 us (8%)
  Pallas kernels  85.5 us (6%)
  local copies, waits for them, and re-layouts  48.7 us (4%)
  other arithmetic  23.2 us (2%)
  between operations  15.8 us (1%)
    psum x2, waiting for transfers between devices, body(): lax.psum((table_grad, kernel_grads[0], kernel_grads[1], kernel_grads[2],...  273 us
    reduce_scatter x1, waiting for transfers between devices, body(): lax.psum_scatter(highway_grad.astype(jnp.bfloat16), 'dp', scatter_dimensi...  182 us
    all_gather x1, waiting for transfers between devices, body(): lax.all_gather(highway_weight, 'dp', axis=0, tiled=True)  81.6 us
    reduce_scatter x1, waiting for transfers between devices, body(): lax.psum_scatter(hidden_out_grad.astype(jnp.bfloat16), 'dp', scatter_dime...  78.5 us
    reduce_scatter x1, waiting for transfers between devices, body(): lax.psum_scatter(attention_in_grad.astype(jnp.bfloat16), 'dp', scatter_di...  71.4 us
    reduce_scatter x1, waiting for transfers between devices, body(): lax.psum_scatter(projection_grad.astype(jnp.bfloat16), 'dp', scatter_dime...  69.4 us
    psum x1, waiting for transfers between devices, body(): lax.psum(share_highway.astype(jnp.bfloat16), 'seq').astype(jnp.float32)  64.6 us
    pallas_call x1, Pallas kernels, conv_backward(): pl.pallas_call(kernel, grid=(steps,), in_specs=[pl.BlockSpec((rows, LANES...  56.5 us
  transfers between devices with their start and end apart: 17, of which 16 were waited for; matrix products, arithmetic and copies ran while one was open for 10% of the time, Pallas kernels for 6%

profile of v1, /device:TPU:0, one launch (start us, length us, event | category | flops | bytes accessed | tf_op | source)
XLA Modules:
  0.0 1372.1 jit_solution(10105045287587727624)
XLA Ops:
  24.8 4.4 convolution_convert_fusion
  29.2 29.0 %conv_forward.1 = (f32[256,2048]{1,0:T(8,128)}, f32[256,2048]{1,0:T(8,128)}, bf16[12800,128]{1,0:T(8,128)(2,1)}, bf16[128,12800]{1,0:T(8,128)(2,1)}) custom-call(bf16[50,256,128]{2,1,0:T(8,128)(2,1)} %bitcast.90, s32[256,1]{1,0:T(8,128)} %copy.91.lens_ref, bf16[128,2048]{1,0:T(8,128)(2,1)} %copy.92.weight_ref.refs_3_), custom_call_target="tpu_custom_call" | custom-call | tf_op jit(solution)/shard_map/conv_forward/pallas_call | solution.py:103
  58.2 81.6 %all-gather.8.cloned.1.call-done = bf16[2048,4096]{1,0:T(8,128)(2,1)} async-done(((bf16[128,4096]{1,0:T(8,128)(2,1)}), bf16[2048,4096]{1,0:T(8,128)(2,1)}) %all-gather.8.cloned.1.call-update) | async-done | bytes 16777232 | tf_op jit(solution)/shard_map/all_gather | solution.py:233
  139.8 11.0 convolution_add_fusion
  153.8 31.8 %all-gather.10.cloned.1.call-done = bf16[2048,768]{1,0:T(8,128)(2,1)} async-done(((bf16[128,768]{1,0:T(8,128)(2,1)}), bf16[2048,768]{1,0:T(8,128)(2,1)}) %all-gather.10.cloned.1.call-update) | async-done | bytes 3145744 | tf_op jit(solution)/shard_map/all_gather | solution.py:234
  188.5 45.4 %all-gather.12.cloned.1.call-done = bf16[768,2304]{1,0:T(8,128)(2,1)} async-done(((bf16[48,2304]{1,0:T(8,128)(2,1)}), bf16[768,2304]{1,0:T(8,128)(2,1)}) %all-gather.12.cloned.1.call-update) | async-done | bytes 3538960 | tf_op jit(solution)/shard_map/all_gather | solution.py:251
  233.8 3.1 convolution_convert_fusion.5
  241.4 22.9 %all-gather.14.cloned.1.call-done = bf16[512,1536]{1,0:T(8,128)(2,1)} async-done(((bf16[256,1536]{1,0:T(8,128)(2,1)}), bf16[512,1536]{1,0:T(8,128)(2,1)}) %all-gather.14.cloned.1.call-update) | async-done | bytes 1572880 | tf_op jit(solution)/shard_map/all_gather | solution.py:270
  267.2 4.7 fusion.68
  272.0 4.0 fusion.31
  276.0 28.7 %all-gather.16.cloned.1.call-done = bf16[768,768]{1,0:T(8,128)(2,1)} async-done(((bf16[48,768]{1,0:T(8,128)(2,1)}), bf16[768,768]{1,0:T(8,128)(2,1)}) %all-gather.16.cloned.1.call-update) | async-done | bytes 1179664 | tf_op jit(solution)/shard_map/all_gather | solution.py:252
  307.4 51.7 %all-gather.18.cloned.1.call-done = bf16[768,3072]{1,0:T(8,128)(2,1)} async-done(((bf16[48,3072]{1,0:T(8,128)(2,1)}), bf16[768,3072]{1,0:T(8,128)(2,1)}) %all-gather.18.cloned.1.call-update) | async-done | bytes 4718608 | tf_op jit(solution)/shard_map/all_gather | solution.py:253
  359.1 11.6 multiply_convert_fusion.1
  370.7 42.5 %all-gather.20.cloned.1.call-done = bf16[3072,768]{1,0:T(8,128)(2,1)} async-done(((bf16[192,768]{1,0:T(8,128)(2,1)}), bf16[3072,768]{1,0:T(8,128)(2,1)}) %all-gather.20.cloned.1.call-update) | async-done | bytes 4718608 | tf_op jit(solution)/shard_map/all_gather | solution.py:254
  413.2 4.0 fusion.70
  426.9 3.8 fusion.27
  439.5 5.4 convolution_convert_fusion.3
  445.6 5.3 convolution_convert_fusion.2
  453.9 7.5 reduce-scatter.8.cloned.1.call-done
  462.6 4.6 constant_dynamic-update-slice_fusion.2
  476.1 7.6 fusion.17
  483.7 10.6 convolution_convert_fusion.1
  496.7 13.1 fusion.66
  509.8 56.5 %conv_backward.1 = (f32[128,2048]{1,0:T(8,128)}, f32[272,128]{1,0:T(8,128)}) custom-call(bf16[12800,128]{1,0:T(8,128)(2,1)} %get-tuple-element.113.refs_0_, bf16[128,12800]{1,0:T(8,128)(2,1)} %get-tuple-element.114.refs_1_, s32[4,1,3200]{2,1,0:T(1,128)} %reshape.301.refs_2_, bf16[128,2048]{1,0:T(8,128)(2,1)} %copy.92.weight_ref.refs_3_, ...), custom_call_target="tpu_custom_call" | custom-call | tf_op jit(solution)/shard_map/conv_backward/pallas_call | solution.py:140
  575.5 26.8 %reduce-scatter.18.cloned.1.call-done = bf16[48,3072]{1,0:T(8,128)(2,1)} async-done(((bf16[768,3072]{1,0:T(8,128)(2,1)}), bf16[48,3072]{1,0:T(8,128)(2,1)}) %reduce-scatter.18.cloned.1.call-update) | async-done | bytes 294928 | tf_op jit(solution)/shard_map/reduce_scatter | solution.py:411
  602.3 78.5 %reduce-scatter.20.cloned.1.call-done = bf16[192,768]{1,0:T(8,128)(2,1)} async-done(((bf16[3072,768]{1,0:T(8,128)(2,1)}), bf16[192,768]{1,0:T(8,128)(2,1)}) %reduce-scatter.20.cloned.1.call-update) | async-done | bytes 294928 | tf_op jit(solution)/shard_map/reduce_scatter | solution.py:412
  680.8 69.4 %reduce-scatter.12.cloned.1.call-done = bf16[128,768]{1,0:T(8,128)(2,1)} async-done(((bf16[2048,768]{1,0:T(8,128)(2,1)}), bf16[128,768]{1,0:T(8,128)(2,1)}) %reduce-scatter.12.cloned.1.call-update) | async-done | bytes 196624 | tf_op jit(solution)/shard_map/reduce_scatter | solution.py:408
  750.2 71.4 %reduce-scatter.14.cloned.1.call-done = bf16[48,2304]{1,0:T(8,128)(2,1)} async-done(((bf16[768,2304]{1,0:T(8,128)(2,1)}), bf16[48,2304]{1,0:T(8,128)(2,1)}) %reduce-scatter.14.cloned.1.call-update) | async-done | bytes 221200 | tf_op jit(solution)/shard_map/reduce_scatter | solution.py:409
  821.7 182.0 %reduce-scatter.10.cloned.1.call-done = bf16[128,4096]{1,0:T(8,128)(2,1)} async-done(((bf16[2048,4096]{1,0:T(8,128)(2,1)}), bf16[128,4096]{1,0:T(8,128)(2,1)}) %reduce-scatter.10.cloned.1.call-update) | async-done | bytes 1048592 | tf_op jit(solution)/shard_map/reduce_scatter | solution.py:407
  1005.9 136.5 %all-reduce.9.cloned.1.call-done = (f32[263,16]{1,0:T(8,128)}, f32[16,32]{1,0:T(8,128)}, f32[32,32]{1,0:T(8,128)}, f32[48,64]{1,0:T(8,128)}, f32[64,128]{1,0:T(8...) async-done(((f32[263,16]{1,0:T(8,128)}, f32[16,32]{1,0:T(8,128)}, f32[32,32]{1,0:T(8,128)}, ...) | async-done | bytes 104912 | tf_op jit(solution)/shard_map/psum | solution.py:422
  1144.0 64.6 %all-reduce.13.cloned.1.call-done = (bf16[128,4096]{1,0:T(8,128)(2,1)}, bf16[128,768]{1,0:T(8,128)(2,1)}, bf16[48,2304]{1,0:T(8,128)(2,1)}, bf16[48,768]{1,0:T(8...) async-done(((bf16[128,4096]{1,0:T(8,128)(2,1)}, bf16[128,768]{1,0:T(8,128)(2,1)}, bf16[48,2304]{1,0:T(8,128)(2,1)}, bf16[48,768]{1,0:T(8,128)(2,1)}, ...) | async-done | bytes 2129936 | tf_op jit(solution)/shard_map/psum | solution.py:415
  1215.5 136.1 %all-reduce.11.cloned.1.call-done = (f32[80,256]{1,0:T(8,128)}, f32[96,512]{1,0:T(8,128)}, f32[112,1024]{1,0:T(8,128)}, f32[512,768]{1,0:T(8,128)}) async-done(((f32[80,256]{1,0:T(8,128)}, f32[96,512]{1,0:T(8,128)}, f32[112,1024]{1,0:T(8,128)}, f32[512,768]{1,0:T(8,128)}), (f32[80,256]{1,0:T(8,128)}, f32[96,512]{1,0:T(8,128)}, f32[112,1024]{1,0:T(8,128)}, ...) | async-done | bytes 2310160 | tf_op jit(solution)/shard_map/psum | solution.py:422
  (301 shorter events, 100.3 us)
Async XLA Ops:
  7.2 132.6 %all-gather.8.cloned.1.call-start = ((), (), s32[]{:S(2)}) async-start(), calls=%async_computation.7 | async-start | bytes 17825792 | tf_op jit(solution)/shard_map/all_gather | solution.py:233
  8.0 177.5 %all-gather.10.cloned.1.call-start = ((), (), s32[]{:S(2)}) async-start(), calls=%async_computation.8 | async-start | bytes 3342336 | tf_op jit(solution)/shard_map/all_gather | solution.py:234
  8.7 225.1 %all-gather.12.cloned.1.call-start = ((), (), s32[]{:S(2)}) async-start(), calls=%async_computation.9 | async-start | bytes 3760128 | tf_op jit(solution)/shard_map/all_gather | solution.py:251
  9.5 254.8 %all-gather.14.cloned.1.call-start = ((), (), s32[]{:S(2)}) async-start(), calls=%async_computation.10 | async-start | bytes 2359296 | tf_op jit(solution)/shard_map/all_gather | solution.py:270
  24.8 126.0 %copy-start.37 = (f32[2048]{0:T(1024)}, f32[2048]{0:T(1024)S(1)}, u32[]{:S(2)}) copy-start(f32[2048]{0:T(1024)S(1)} %convert_element_type.129) | copy-start | bytes 24580
  188.4 116.3 %copy-start.11 = (f32[256,768]{1,0:T(8,128)}, f32[256,768]{1,0:T(8,128)S(1)}, u32[]{:S(2)}) copy-start(f32[256,768]{1,0:T(8,128)S(1)} %convolution_add_fusion.6) | copy-start | bytes 2359300
  237.9 66.9 %all-gather.16.cloned.1.call-start = ((), (), s32[]{:S(2)}) async-start(), calls=%async_computation.11 | async-start | bytes 1253376 | tf_op jit(solution)/shard_map/all_gather | solution.py:252
  238.5 120.6 %all-gather.18.cloned.1.call-start = ((), (), s32[]{:S(2)}) async-start(), calls=%async_computation.12 | async-start | bytes 5013504 | tf_op jit(solution)/shard_map/all_gather | solution.py:253
  239.1 174.2 %all-gather.20.cloned.1.call-start = ((), (), s32[]{:S(2)}) async-start(), calls=%async_computation.13 | async-start | bytes 5013504 | tf_op jit(solution)/shard_map/all_gather | solution.py:254
  239.8 221.5 %reduce-scatter.8.cloned.1.call-start = ((), (), s32[]{:S(2)}) async-start(), calls=%async_computation.14 | async-start | bytes 2359296 | tf_op jit(solution)/shard_map/reduce_scatter | solution.py:346
  306.6 117.6 %copy-start.4 = (f32[256,768]{1,0:T(8,128)}, f32[256,768]{1,0:T(8,128)S(1)}, u32[]{:S(2)}) copy-start(f32[256,768]{1,0:T(8,128)S(1)} %get-tuple-element.226) | copy-start | bytes 2359300
  436.5 138.9 %reduce-scatter.16.cloned.1.call-start = ((), (), s32[]{:S(2)}) async-start(), calls=%async_computation.18 | async-start | bytes 1253376 | tf_op jit(solution)/shard_map/reduce_scatter | solution.py:410
  439.4 162.9 %reduce-scatter.18.cloned.1.call-start = ((), (), s32[]{:S(2)}) async-start(), calls=%async_computation.19 | async-start | bytes 5013504 | tf_op jit(solution)/shard_map/reduce_scatter | solution.py:411
  444.9 235.9 %reduce-scatter.20.cloned.1.call-start = ((), (), s32[]{:S(2)}) async-start(), calls=%async_computation.20 | async-start | bytes 5013504 | tf_op jit(solution)/shard_map/reduce_scatter | solution.py:412
  450.9 299.4 %reduce-scatter.12.cloned.1.call-start = ((), (), s32[]{:S(2)}) async-start(), calls=%async_computation.16 | async-start | bytes 3342336 | tf_op jit(solution)/shard_map/reduce_scatter | solution.py:408
  470.1 351.6 %reduce-scatter.14.cloned.1.call-start = ((), (), s32[]{:S(2)}) async-start(), calls=%async_computation.17 | async-start | bytes 3760128 | tf_op jit(solution)/shard_map/reduce_scatter | solution.py:409
  474.5 529.2 %reduce-scatter.10.cloned.1.call-start = ((), (), s32[]{:S(2)}) async-start(), calls=%async_computation.15 | async-start | bytes 17825792 | tf_op jit(solution)/shard_map/reduce_scatter | solution.py:407
  494.3 648.1 %all-reduce.9.cloned.1.call-start = ((), (), s32[]{:S(2)}) async-start(), calls=%async_computation.21 | async-start | bytes 516096 | tf_op jit(solution)/shard_map/psum | solution.py:422
  571.8 431.9 %copy-start.27 = (f32[128,2048]{1,0:T(8,128)S(1)}, f32[128,2048]{1,0:T(8,128)}, u32[]{:S(2)}) copy-start(f32[128,2048]{1,0:T(8,128)} %get-tuple-element.117) | copy-start | bytes 3145732
  575.4 633.2 %all-reduce.13.cloned.1.call-start = ((), (), s32[]{:S(2)}) async-start(), calls=%async_computation.23 | async-start | bytes 4259840 | tf_op jit(solution)/shard_map/psum | solution.py:415
  1003.7 347.9 %all-reduce.11.cloned.1.call-start = ((), (), s32[]{:S(2)}) async-start(), calls=%async_computation.22 | async-start | bytes 4620288 | tf_op jit(solution)/shard_map/psum | solution.py:422
  1208.6 142.9 %copy-start.54 = (f32[16,32]{1,0:T(8,128)S(1)}, f32[16,32]{1,0:T(8,128)}, u32[]{:S(2)}) copy-start(f32[16,32]{1,0:T(8,128)} %get-tuple-element.241) | copy-start | bytes 6148
  1208.6 143.5 %copy-start.43 = (f32[32,32]{1,0:T(8,128)S(1)}, f32[32,32]{1,0:T(8,128)}, u32[]{:S(2)}) copy-start(f32[32,32]{1,0:T(8,128)} %get-tuple-element.242) | copy-start | bytes 12292
  1208.6 144.1 %copy-start.40 = (f32[48,64]{1,0:T(8,128)S(1)}, f32[48,64]{1,0:T(8,128)}, u32[]{:S(2)}) copy-start(f32[48,64]{1,0:T(8,128)} %get-tuple-element.243) | copy-start | bytes 36868
  1208.6 144.7 %copy-start.39 = (f32[64,128]{1,0:T(8,128)S(1)}, f32[64,128]{1,0:T(8,128)}, u32[]{:S(2)}) copy-start(f32[64,128]{1,0:T(8,128)} %get-tuple-element.244) | copy-start | bytes 98308
  1211.5 147.5 %copy-start.53 = (f32[2048]{0:T(1024)S(1)}, f32[2048]{0:T(1024)}, u32[]{:S(2)}) copy-start(f32[2048]{0:T(1024)} %get-tuple-element.248) | copy-start | bytes 24580
  1211.5 148.1 %copy-start.42 = (f32[4096]{0:T(1024)S(1)}, f32[4096]{0:T(1024)}, u32[]{:S(2)}) copy-start(f32[4096]{0:T(1024)} %get-tuple-element.250) | copy-start | bytes 49156
  1213.7 151.5 %copy-start.1 = (bf16[263,16]{0,1:T(8,128)(2,1)S(1)}, bf16[263,16]{0,1:T(8,128)(2,1)}, u32[]{:S(2)}) copy-start(bf16[263,16]{0,1:T(8,128)(2,1)} %param.42) | copy-start | bytes 25252
  1213.7 149.1 %copy-start.59 = (f32[768]{0:T(1024)S(1)}, f32[768]{0:T(1024)}, u32[]{:S(2)}) copy-start(f32[768]{0:T(1024)} %get-tuple-element.255) | copy-start | bytes 9220
  1213.7 149.7 %copy-start.58 = (f32[768]{0:T(1024)S(1)}, f32[768]{0:T(1024)}, u32[]{:S(2)}) copy-start(f32[768]{0:T(1024)} %get-tuple-element.256) | copy-start | bytes 9220
  1213.7 150.3 %copy-start.57 = (f32[768]{0:T(1024)S(1)}, f32[768]{0:T(1024)}, u32[]{:S(2)}) copy-start(f32[768]{0:T(1024)} %get-tuple-element.259) | copy-start | bytes 9220
  1213.7 150.8 %copy-start.56 = (f32[768]{0:T(1024)S(1)}, f32[768]{0:T(1024)}, u32[]{:S(2)}) copy-start(f32[768]{0:T(1024)} %get-tuple-element.260) | copy-start | bytes 9220
  (62 other events, 844.1 us)
Sparse Core Ops, SparseCore 0:
  10.2 129.5 all-gather.7
  142.1 43.3 all-gather.9
  187.8 45.9 all-gather.11
  238.0 26.2 all-gather.13
  266.4 38.3 all-gather.15
  306.9 52.1 all-gather.17
  361.4 51.7 all-gather.19
  436.7 24.6 reduce-scatter.7
  465.4 58.0 reduce-scatter.15
  527.7 74.5 reduce-scatter.17
  606.2 74.5 reduce-scatter.19
  684.9 65.2 reduce-scatter.11
  754.6 67.0 reduce-scatter.13
  826.2 177.4 reduce-scatter.9
  1012.8 129.5 all-reduce.8
  1144.9 63.6 all-reduce.12
  1215.6 135.8 all-reduce.10

commit v2 on v1

v2 whole, which is shorter than its diff:
```python
from functools import partial
import math

import jax
import jax.numpy as jnp
from jax import lax
from jax.experimental import pallas as pl
from jax.experimental.pallas import tpu as pltpu
from jax.sharding import PartitionSpec as P

HEAD_DIM = 64


exact_gelu = partial(jax.nn.gelu, approximate=False)


def layer_norm(value, gain, bias):
    mean = jnp.mean(value, axis=-1, keepdims=True)
    centered = value - mean
    spread = jnp.mean(centered * centered, axis=-1, keepdims=True)
    return centered * lax.rsqrt(spread + 1e-12) * gain + bias


def highway_mix(transform, gate, hidden):
    carry = jax.nn.sigmoid(gate)
    return carry * hidden + (1.0 - carry) * jax.nn.relu(transform)


def place():
    spot = lax.axis_index("dp")
    return (spot // 4, (spot // 2) % 2, spot % 2)


def core_swap(value):
    size = lax.axis_size("dp")
    return lax.ppermute(value, "dp", [(spot, spot ^ 1) for spot in range(size)])


def middle_swap(value):
    size = lax.axis_size("dp")
    return lax.ppermute(value, "dp", [(spot, spot ^ 2) for spot in range(size)])


def outer_shift(value, steps):
    size = lax.axis_size("dp")
    return lax.ppermute(value, "dp", [(spot, (spot - 4 * steps) % size) for spot in range(size)])


def seq_swap(value):
    return lax.ppermute(value, "seq", [(0, 1), (1, 0)])


def after(value, *others):
    return lax.optimization_barrier((value,) + others)[0]


def pick(value, index, axis):
    return lax.dynamic_index_in_dim(value, index, axis, keepdims=False)


def outer_pieces(shard):
    return [shard] + [outer_shift(shard, steps) for steps in range(1, lax.axis_size("dp") // 4)]


def gather_near(pieces):
    outer = place()[0]
    size = len(pieces)
    near = jnp.zeros((size,) + pieces[0].shape, pieces[0].dtype)
    for steps, piece in enumerate(pieces):
        near = lax.dynamic_update_index_in_dim(near, piece, (outer + steps) % size, 0)
    return near


def gather(values, side=None):
    _, middle, core = place()
    size = values[0].shape[0]
    shape = values[0].shape[1:]
    zeros = (0,) * len(shape)
    whole = jnp.zeros(((size, 2, 2) if side is None else (2, size, 2)) + shape, values[0].dtype)
    for flip, value in enumerate(values):
        flip_middle, flip_core = flip % 2, flip // 2
        if side is None:
            start = (0, middle ^ flip_middle, core ^ flip_core) + zeros
            value = value[:, None, None]
        else:
            start = (core ^ side ^ flip_core, 0, middle ^ flip_middle) + zeros
            value = value[None, :, None]
        whole = lax.dynamic_update_slice(whole, value, start)
    return whole


def scatter_core(parts, side=None):
    _, _, core = place()
    axis, slot = (2, core) if side is None else (0, core ^ side)
    other = core_swap(pick(parts, 1 - slot, axis).astype(jnp.bfloat16))
    return pick(parts, slot, axis).astype(jnp.float32) + other.astype(jnp.float32)


def scatter_middle(half):
    _, middle, _ = place()
    other = middle_swap(pick(half, 1 - middle, 1).astype(jnp.bfloat16))
    return pick(half, middle, 1) + other.astype(jnp.float32)


def scatter_outer(quarter):
    outer, _, _ = place()
    size = quarter.shape[0]
    rounded = quarter.astype(jnp.bfloat16)
    total = pick(quarter, outer, 0)
    for steps in range(1, size):
        sent = pick(rounded, (outer + size - steps) % size, 0)
        total = total + outer_shift(sent, steps).astype(jnp.float32)
    return total


def seq_sum(value):
    return value + seq_swap(value.astype(jnp.bfloat16)).astype(jnp.float32)


def own_blocks(value, axis):
    axis = axis % value.ndim
    size = lax.axis_size("dp")
    shape = value.shape
    split = shape[:axis] + (size // 2, 2, shape[axis] // size) + shape[axis + 1 :]
    chosen = pick(value.reshape(split), lax.axis_index("seq"), axis + 1)
    return chosen.reshape(shape[:axis] + (shape[axis] // 2,) + shape[axis + 1 :])


def interleave(own, other, piece):
    first = lax.axis_index("seq") == 0
    blocks = []
    for start in range(0, own.shape[1], piece):
        mine, theirs = own[:, start : start + piece], other[:, start : start + piece]
        blocks += [jnp.where(first, mine, theirs), jnp.where(first, theirs, mine)]
    return jnp.concatenate(blocks, axis=1)


def halves_of(value, piece):
    first = lax.axis_index("seq") == 0
    own, other = [], []
    for start in range(0, value.shape[1], 2 * piece):
        even, odd = value[:, start : start + piece], value[:, start + piece : start + 2 * piece]
        own.append(jnp.where(first, even, odd))
        other.append(jnp.where(first, odd, even))
    return jnp.concatenate(own, axis=1), jnp.concatenate(other, axis=1)


def by_seq(own, other):
    first = lax.axis_index("seq") == 0
    return jnp.stack([jnp.where(first, own, other), jnp.where(first, other, own)])


WIDTHS = 7
LANES = 128
NEG = -1e30


def conv_forward_kernel(spread_ref, lens_ref, weight_ref, pooled_ref, ties_ref, window_ref, flipped_ref, scores_ref):
    letters, words, _ = spread_ref.shape
    channels = weight_ref.shape[1]
    lane = lax.broadcasted_iota(jnp.int32, (words, LANES), 1)
    slot = lane // 16
    limit = jnp.maximum(lens_ref[...] - (lane - 16 * WIDTHS), 1)
    for p in range(letters):
        window = jnp.zeros((words, LANES), jnp.float32)
        for j in range(WIDTHS):
            if p + j < letters:
                window = jnp.where(slot == j, spread_ref[p + j].astype(jnp.float32), window)
        flag = jnp.where((lane >= 16 * WIDTHS) & (lane < 17 * WIDTHS) & (p >= limit), 1.0, window)
        window_ref[p * words:(p + 1) * words] = flag.astype(jnp.bfloat16)
    flipped_ref[...] = window_ref[...].T
    tile = 256

    def one_tile(index, _):
        c = pl.multiple_of(index * tile, tile)
        scores_ref[...] = jnp.dot(window_ref[...], weight_ref[:, pl.ds(c, tile)], preferred_element_type=jnp.float32)
        for r in range(0, words, 16):
            top = scores_ref[r:r + 16]
            for p in range(1, letters):
                top = jnp.maximum(top, scores_ref[p * words + r:p * words + r + 16])
            count = jnp.zeros((16, tile), jnp.float32)
            for p in range(letters):
                count += jnp.where(scores_ref[p * words + r:p * words + r + 16] == top, 1.0, 0.0)
            pooled_ref[r:r + 16, pl.ds(c, tile)] = top
            ties_ref[r:r + 16, pl.ds(c, tile)] = count
        return 0

    lax.fori_loop(0, channels // tile, one_tile, 0)


def conv_backward_kernel(window_ref, flipped_ref, codes_ref, weight_ref, turned_ref, pooled_ref, share_in_ref,
                         grad_ref, table_ref, share_ref, scores_ref, spread_ref, letters):
    rows = window_ref.shape[0]
    words = rows // letters
    channels = weight_ref.shape[1]
    vocab = table_ref.shape[0]
    tile = 256

    @pl.when(pl.program_id(0) == 0)
    def _():
        grad_ref[...] = jnp.zeros_like(grad_ref)
        table_ref[...] = jnp.zeros_like(table_ref)

    def one_tile(index, _):
        c = pl.multiple_of(index * tile, tile)
        scores_ref[...] = jnp.dot(window_ref[...], weight_ref[:, pl.ds(c, tile)], preferred_element_type=jnp.float32)
        for r in range(0, words, 16):
            top = pooled_ref[r:r + 16, pl.ds(c, tile)]
            part = share_in_ref[r:r + 16, pl.ds(c, tile)]
            for p in range(letters):
                hit = scores_ref[p * words + r:p * words + r + 16] == top
                share_ref[p * words + r:p * words + r + 16, pl.ds(c, tile)] = jnp.where(hit, part, 0.0).astype(jnp.bfloat16)
        return 0

    lax.fori_loop(0, channels // tile, one_tile, 0)
    grad_ref[...] += jnp.dot(flipped_ref[...], share_ref[...], preferred_element_type=jnp.float32)
    scores_ref[:, :LANES] = jnp.dot(share_ref[...], turned_ref[...], preferred_element_type=jnp.float32)
    slot = lax.broadcasted_iota(jnp.int32, (words, LANES), 1) // 16
    for c in range(letters):
        spread = jnp.zeros((words, LANES), jnp.float32)
        for j in range(WIDTHS):
            if c - j >= 0:
                spread = jnp.where(slot == j, scores_ref[(c - j) * words:(c - j + 1) * words, :LANES], spread)
        spread_ref[c * words:(c + 1) * words] = spread.astype(jnp.bfloat16)
    onehot = jnp.where(lax.broadcasted_iota(jnp.int32, (vocab, rows), 0) == codes_ref[0], 1.0, 0.0).astype(jnp.bfloat16)
    table_ref[...] += jnp.dot(onehot, spread_ref[...], preferred_element_type=jnp.float32)


def conv_forward(spread, lens, weight, block):
    letters, words, _ = spread.shape
    channels = weight.shape[1]
    steps = words // block
    rows = letters * block
    f32 = jnp.float32
    return pl.pallas_call(
        conv_forward_kernel,
        grid=(steps,),
        in_specs=[
            pl.BlockSpec((letters, block, LANES), lambda i: (0, i, 0)),
            pl.BlockSpec((block, 1), lambda i: (i, 0)),
            pl.BlockSpec((LANES, channels), lambda i: (0, 0)),
        ],
        out_specs=[
            pl.BlockSpec((block, channels), lambda i: (i, 0)),
            pl.BlockSpec((block, channels), lambda i: (i, 0)),
            pl.BlockSpec((rows, LANES), lambda i: (i, 0)),
            pl.BlockSpec((LANES, rows), lambda i: (0, i)),
        ],
        out_shape=[
            jax.ShapeDtypeStruct((words, channels), f32),
            jax.ShapeDtypeStruct((words, channels), f32),
            jax.ShapeDtypeStruct((steps * rows, LANES), jnp.bfloat16),
            jax.ShapeDtypeStruct((LANES, steps * rows), jnp.bfloat16),
        ],
        scratch_shapes=[pltpu.VMEM((rows, 256), f32)],
        compiler_params=pltpu.CompilerParams(dimension_semantics=("arbitrary",)),
        cost_estimate=pl.CostEstimate(
            flops=2 * LANES * steps * rows * channels,
            bytes_accessed=steps * rows * channels * 5,
            transcendentals=0,
        ),
        name="conv_forward",
    )(spread, lens, weight)


def conv_backward(window, flipped, codes, weight, turned, pooled, share, vocab, block, first, steps):
    words, channels = pooled.shape
    rows = window.shape[0] // (words // block)
    letters = rows // block
    f32 = jnp.float32
    vocab = -(-vocab // 16) * 16

    def kernel(*refs):
        conv_backward_kernel(*refs, letters=letters)

    return pl.pallas_call(
        kernel,
        grid=(steps,),
        in_specs=[
            pl.BlockSpec((rows, LANES), lambda i: (first + i, 0)),
            pl.BlockSpec((LANES, rows), lambda i: (0, first + i)),
            pl.BlockSpec((1, 1, rows), lambda i: (first + i, 0, 0)),
            pl.BlockSpec((LANES, channels), lambda i: (0, 0)),
            pl.BlockSpec((channels, LANES), lambda i: (0, 0)),
            pl.BlockSpec((block, channels), lambda i: (first + i, 0)),
            pl.BlockSpec((block, channels), lambda i: (first + i, 0)),
        ],
        out_specs=[
            pl.BlockSpec((LANES, channels), lambda i: (0, 0)),
            pl.BlockSpec((vocab, LANES), lambda i: (0, 0)),
        ],
        out_shape=[
            jax.ShapeDtypeStruct((LANES, channels), f32),
            jax.ShapeDtypeStruct((vocab, LANES), f32),
        ],
        scratch_shapes=[
            pltpu.VMEM((rows, channels), jnp.bfloat16),
            pltpu.VMEM((rows, 256), f32),
            pltpu.VMEM((rows, LANES), jnp.bfloat16),
        ],
        compiler_params=pltpu.CompilerParams(dimension_semantics=("arbitrary",)),
        cost_estimate=pl.CostEstimate(
            flops=6 * LANES * steps * rows * channels,
            bytes_accessed=steps * rows * channels * 8,
            transcendentals=0,
        ),
        name="conv_backward",
    )(window, flipped, codes, weight, turned, pooled, share)


def merge_kernel(*refs):
    whole_ref = refs[-1]
    whole_ref[...] = jnp.zeros_like(whole_ref)
    features = refs[0].shape[0]
    first = 0
    for width, kernel_ref in enumerate(refs[:-1], 1):
        channels = kernel_ref.shape[1]
        whole_ref[: width * features, first : first + channels] = kernel_ref[...]
        marks = lax.broadcasted_iota(jnp.int32, (16, channels), 0) == width - 1
        whole_ref[WIDTHS * features :, first : first + channels] = jnp.where(marks, NEG, 0.0).astype(jnp.bfloat16)
        first = first + channels


def merged_weight(kernels):
    channels = sum(kernel.shape[1] for kernel in kernels)
    return pl.pallas_call(
        merge_kernel, out_shape=jax.ShapeDtypeStruct((LANES, channels), jnp.bfloat16), name="merge_widths"
    )(*kernels)


def spread_letters(codes, table):
    vocab, features = table.shape
    words, letters = codes.shape
    wide = jnp.tile(table, (1, LANES // features))
    onehot = (codes.T.reshape(-1, 1) == jnp.arange(vocab, dtype=jnp.int32)[None, :]).astype(jnp.bfloat16)
    return jnp.dot(onehot, wide, preferred_element_type=jnp.float32).astype(jnp.bfloat16).reshape(letters, words, LANES)


def score_heads(query_heads, key_heads, keep):
    raw = (
        jnp.einsum("qhd,khd->hqk", query_heads, key_heads, preferred_element_type=jnp.float32)
        * 0.125
    )
    return jnp.where(keep[None, None, :], raw, -1e30)


def body(
    character_codes,
    word_lengths,
    sequence_lengths,
    character_table,
    conv_width1,
    conv_width2,
    conv_width3,
    conv_width4,
    conv_width5,
    conv_width6,
    conv_width7,
    conv_bias,
    highway_weight,
    highway_bias,
    projection,
    position_table,
    attention_in,
    attention_out,
    norm1_gain,
    norm1_bias,
    hidden_in,
    hidden_out,
    norm2_gain,
    norm2_bias,
    cotangent,
):
    kernels = (
        conv_width1,
        conv_width2,
        conv_width3,
        conv_width4,
        conv_width5,
        conv_width6,
        conv_width7,
    )
    f32 = jnp.float32
    low = jnp.bfloat16
    side = lax.axis_index("seq")
    outer, middle, core = place()
    size = lax.axis_size("dp")
    chips = size // 2
    words = character_codes.shape[1]
    letters = character_codes.shape[2]
    vocab, features = character_table.shape
    filters = conv_bias.shape[0]
    mine = filters // 2
    piece = filters // size
    half = piece // 2
    model = position_table.shape[1]
    block = math.gcd(words, 64)
    steps = words // block

    highway_shard = own_blocks(highway_weight.reshape(-1, 2, filters), 2)
    held = lax.dynamic_slice_in_dim(projection, core * half, half, 0)
    lent = lax.dynamic_slice_in_dim(projection, (1 - core) * half, half, 0)
    projection_shard = jnp.where(core == side, held, core_swap(lent))
    code_rows = jnp.concatenate([character_codes[0], word_lengths[0][:, None]], axis=1)
    code_rows = [code_rows, seq_swap(code_rows)]

    joint_shard = jnp.concatenate(
        [highway_shard.reshape(piece, filters), projection_shard.reshape(piece, model // 2)], axis=1
    )
    joint_all = lax.all_gather(joint_shard, "dp", axis=0, tiled=True)
    highway_parts = [joint_all[:, :mine], joint_all[:, mine:filters]]
    projection_full = joint_all[:, filters:].reshape(mine, model)
    attention_near = gather_near(outer_pieces(jnp.concatenate([attention_in, attention_out], axis=1)))
    attention_across = middle_swap(attention_near)
    attention_far = [core_swap(attention_near), core_swap(attention_across)]
    attention_all = gather((attention_near, attention_across, *attention_far)).reshape(model, -1)
    attention_full = attention_all[:, : 3 * model]
    output_full = attention_all[:, 3 * model :]

    def cut(grad, slots=False):
        lead = (2, size // 4, 2) if slots else (size // 4, 2, 2)
        return grad.reshape(lead + (grad.shape[0] // size,) + grad.shape[1:])

    codes = [rows[:, :letters] for rows in code_rows]
    conv_weight = own_blocks(merged_weight(kernels), 1)
    conv_shift = own_blocks(conv_bias, 0).astype(f32)
    forwards = [
        conv_forward(spread_letters(codes[0], character_table), code_rows[0][:, letters:], conv_weight, block)
    ]
    rows = hidden_in.shape[0]
    splits = hidden_out.shape[0] // rows
    inner_size = hidden_in.shape[1]
    turned_in = hidden_in.reshape(rows, size, splits, rows).transpose(0, 2, 1, 3).reshape(rows, inner_size)
    forward_shard = jnp.concatenate(
        [turned_in] + [hidden_out[part * rows : (part + 1) * rows] for part in range(splits)], axis=1
    )
    forward_all = lax.all_gather(after(forward_shard, forwards[0][0]), "dp", axis=0, tiled=True)
    inward_full = forward_all[:, :inner_size]
    outward_parts = [
        forward_all[:, inner_size + part * model : inner_size + (part + 1) * model] for part in range(splits)
    ]
    forwards.append(
        conv_forward(spread_letters(codes[1], character_table), code_rows[1][:, letters:], conv_weight, block)
    )
    biased = [forward[0] + conv_shift for forward in forwards]
    hidden0_parts = [jax.nn.relu(value) for value in biased]
    hidden0_low = [value.astype(low) for value in hidden0_parts]
    swapped = [seq_swap(value) for value in hidden0_low]
    hidden0_all = jnp.concatenate(
        [interleave(hidden0_low[0], swapped[1], piece), interleave(hidden0_low[1], swapped[0], piece)], axis=0
    )
    hidden0 = jnp.concatenate(hidden0_parts, axis=0)
    highway_shift = own_blocks(highway_bias.reshape(2, filters), 1).astype(f32)
    transform, gate = [
        jnp.dot(hidden0_all, highway_parts[part], preferred_element_type=f32) + highway_shift[part]
        for part in range(2)
    ]
    hidden1 = highway_mix(transform, gate, hidden0)
    hidden1_low = hidden1.astype(low)
    mapped = jnp.dot(hidden1_low, projection_full, preferred_element_type=f32)
    offset = side * words
    positions = lax.dynamic_slice_in_dim(position_table, offset, words, 0).astype(f32)
    embedded = mapped[:words] + seq_swap(mapped[words:].astype(low)).astype(f32) + positions
    embedded_low = embedded.astype(low)
    heads = model // HEAD_DIM
    projected = jnp.dot(embedded_low, attention_full, preferred_element_type=f32).astype(low)
    pairs = projected[:, model:]
    gathered = jnp.concatenate([pairs, seq_swap(pairs)], axis=0)
    length = gathered.shape[0]
    query_heads = projected[:, :model].reshape(words, heads, HEAD_DIM)
    key_heads = gathered[:, :model].reshape(length, heads, HEAD_DIM)
    value_heads = gathered[:, model:].reshape(length, heads, HEAD_DIM)
    keep = (jnp.arange(length, dtype=jnp.int32) + offset) % length < sequence_lengths[0]
    scores = score_heads(query_heads, key_heads, keep)
    top = jnp.max(scores, axis=-1, keepdims=True)
    unnormalized = jnp.exp(scores - top)
    total = jnp.sum(unnormalized, axis=-1, keepdims=True)
    probs_low = (unnormalized / total).astype(jnp.bfloat16)
    attended = jnp.einsum(
        "hqk,khd->qhd", probs_low, value_heads, preferred_element_type=jnp.float32
    )
    attended = attended.reshape(words, model).astype(jnp.bfloat16)
    joined = embedded + jnp.dot(attended, output_full, preferred_element_type=jnp.float32)
    gain1 = norm1_gain.astype(jnp.float32)
    shift1 = norm1_bias.astype(jnp.float32)
    gain2 = norm2_gain.astype(jnp.float32)
    shift2 = norm2_bias.astype(jnp.float32)
    normed1 = layer_norm(joined, gain1, shift1)
    normed1_low = normed1.astype(jnp.bfloat16)
    inner = jnp.dot(normed1_low, inward_full, preferred_element_type=jnp.float32)
    active = exact_gelu(inner).astype(jnp.bfloat16)
    actives = [active[:, part * model : (part + 1) * model] for part in range(splits)]
    summed = normed1 + sum(
        jnp.dot(actives[part], outward_parts[part], preferred_element_type=f32) for part in range(splits)
    )
    layer_out = layer_norm(summed, gain2, shift2).astype(jnp.bfloat16)
    seed_grad = cotangent[0].astype(jnp.float32)
    _, norm2_pull = jax.vjp(layer_norm, summed, gain2, shift2)
    grad_summed, norm2_gain_grad, norm2_bias_grad = norm2_pull(seed_grad)
    grad_outer = grad_summed.astype(jnp.bfloat16)
    hidden_out_grads = [
        jnp.einsum("tf,td->fd", part, grad_outer, preferred_element_type=f32).astype(low) for part in actives
    ]
    grad_active = jnp.concatenate(
        [jnp.einsum("td,fd->tf", grad_outer, part, preferred_element_type=f32) for part in outward_parts], axis=1
    )
    _, gelu_pull = jax.vjp(exact_gelu, inner)
    grad_inner = gelu_pull(grad_active)[0].astype(jnp.bfloat16)
    hidden_in_grad = jnp.einsum(
        "td,tf->df", normed1_low, grad_inner, preferred_element_type=jnp.float32
    ).astype(low)
    grad_normed1 = grad_summed + jnp.einsum(
        "tf,df->td", grad_inner, inward_full, preferred_element_type=jnp.float32
    )
    _, norm1_pull = jax.vjp(layer_norm, joined, gain1, shift1)
    grad_joined, norm1_gain_grad, norm1_bias_grad = norm1_pull(grad_normed1)
    forward_grad = jnp.concatenate([hidden_in_grad] + hidden_out_grads, axis=1)
    forward_sum = lax.psum_scatter(forward_grad, "dp", scatter_dimension=0, tiled=True)
    grad_branch = after(grad_joined.astype(low), forward_grad)
    attention_out_grad = jnp.einsum(
        "td,te->de", attended, grad_branch, preferred_element_type=jnp.float32
    ).astype(low)
    grad_attended = jnp.einsum(
        "te,de->td", grad_branch, output_full, preferred_element_type=jnp.float32
    ).astype(jnp.bfloat16)
    grad_heads = grad_attended.reshape(words, heads, HEAD_DIM)
    probs = jnp.exp(score_heads(query_heads, key_heads, keep) - top) / total
    probs_again = probs.astype(jnp.bfloat16)
    grad_probs = jnp.einsum(
        "qhd,khd->hqk", grad_heads, value_heads, preferred_element_type=jnp.float32
    )
    grad_scores = (
        probs * (grad_probs - jnp.sum(probs * grad_probs, axis=-1, keepdims=True))
    ).astype(jnp.bfloat16)
    grad_query = (
        jnp.einsum("hqk,khd->qhd", grad_scores, key_heads, preferred_element_type=jnp.float32)
        * 0.125
    )
    key_grad = (
        jnp.einsum("hqk,qhd->khd", grad_scores, query_heads, preferred_element_type=f32) * 0.125
    )
    value_grad = jnp.einsum("hqk,qhd->khd", probs_again, grad_heads, preferred_element_type=f32)
    pair_grads = jnp.concatenate(
        [key_grad.reshape(length, model), value_grad.reshape(length, model)], axis=1
    )
    pairs_lent = pair_grads[words:].astype(low)
    grad_pairs = pair_grads[:words] + seq_swap(pairs_lent).astype(f32)
    grad_projected = jnp.concatenate([grad_query.reshape(words, model), grad_pairs], axis=1).astype(low)
    attention_in_grad = jnp.einsum(
        "td,te->de", embedded_low, grad_projected, preferred_element_type=f32
    ).astype(low)
    grad_embedded = grad_joined + jnp.einsum(
        "te,de->td", grad_projected, attention_full, preferred_element_type=f32
    )
    grad_mapped = grad_embedded.astype(low)
    attention_half = scatter_core(cut(jnp.concatenate([attention_in_grad, attention_out_grad], axis=1)))
    grad_mapped = jnp.concatenate([grad_mapped, seq_swap(grad_mapped)], axis=0)
    grad_mapped = after(grad_mapped, attention_half)
    projection_grad = jnp.einsum(
        "tf,td->fd", hidden1_low, grad_mapped, preferred_element_type=f32
    ).astype(low)
    grad_hidden1 = jnp.einsum("td,fd->tf", grad_mapped, projection_full, preferred_element_type=f32)
    _, highway_pull = jax.vjp(highway_mix, transform, gate, hidden0)
    grad_transform, grad_gate, grad_carry = highway_pull(grad_hidden1)
    grad_gates = [grad_transform.astype(low), grad_gate.astype(low)]
    grad_spread = sum(
        jnp.einsum("tg,fg->tf", grad_gates[part], highway_parts[part], preferred_element_type=f32)
        for part in range(2)
    )
    grad_held, grad_lent = halves_of(grad_spread, piece)
    grad_lent = grad_lent.astype(low)
    lent_back = [seq_swap(grad_lent[words:]), seq_swap(grad_lent[:words])]
    grad_near = grad_carry + grad_held
    grad_pooled = [
        jnp.where(
            biased[part] > 0, grad_near[part * words : (part + 1) * words] + lent_back[part].astype(f32), 0.0
        )
        for part in range(2)
    ]
    highway_grads = [
        jnp.einsum("tf,tg->fg", hidden0_all, grad_gates[part], preferred_element_type=f32).astype(low)
        for part in range(2)
    ]
    highway_bias_grad = jnp.concatenate([jnp.sum(grad.astype(f32), axis=0) for grad in grad_gates])
    conv_bias_grad = jnp.sum(grad_pooled[0], axis=0) + jnp.sum(grad_pooled[1], axis=0)
    position_rows = 2 * words * model // mine // size
    position_low = grad_embedded.astype(low)
    nothing = jnp.zeros_like(position_low)
    position_grad = by_seq(position_low, nothing).reshape(size, position_rows, mine)
    highway_rows = jnp.concatenate(
        [highway_grads[0].reshape(size, piece, mine), position_grad], axis=1
    ).reshape(-1, mine)
    highway_sum = lax.psum_scatter(
        after(highway_rows, forward_sum), "dp", scatter_dimension=0, tiled=True
    )
    joint_half = scatter_core(
        cut(jnp.concatenate([highway_grads[1], projection_grad.reshape(filters, model // 2)], axis=1))
    )
    attention_quarter = scatter_middle(attention_half)
    joint_quarter = scatter_middle(joint_half)
    attention_sum = scatter_outer(attention_quarter)
    turned = conv_weight.T
    shares = [grad_pooled[part] / forwards[part][1] for part in range(2)]
    code_blocks = [
        codes[part].reshape(steps, block, letters).transpose(0, 2, 1).reshape(steps, 1, letters * block)
        for part in range(2)
    ]

    def back(part, first, count, *others):
        return conv_backward(
            forwards[part][2],
            forwards[part][3],
            code_blocks[part],
            conv_weight,
            turned,
            forwards[part][0],
            after(shares[part], *others),
            vocab,
            block,
            first,
            count,
        )

    cuts = steps // 2
    backs = [back(0, 0, cuts, attention_quarter, joint_half)]
    backs.append(back(0, cuts, steps - cuts, *backs[0]))
    backs.append(back(1, 0, cuts, attention_sum, joint_quarter, *backs[1]))
    joint_sum = scatter_outer(joint_quarter)
    backs.append(back(1, cuts, steps - cuts, *backs[2]))
    merged_grad = backs[0][0] + backs[1][0] + backs[2][0] + backs[3][0]
    table_wide = backs[0][1] + backs[1][1] + backs[2][1] + backs[3][1]
    table_grad = sum(
        table_wide[:vocab, shift * features : (shift + 1) * features] for shift in range(WIDTHS)
    )

    forward_total = seq_sum(forward_sum.astype(f32))
    inward_total = (
        forward_total[:, :inner_size].reshape(rows, splits, size, rows).transpose(0, 2, 1, 3).reshape(rows, inner_size)
    )
    outward_total = jnp.concatenate(
        [forward_total[:, inner_size + part * model : inner_size + (part + 1) * model] for part in range(splits)],
        axis=0,
    )
    attention_both = seq_sum(attention_sum)
    attention_total = attention_both[:, : 3 * model]
    output_total = attention_both[:, 3 * model :]
    part0 = highway_sum[:piece]
    position_part = highway_sum[piece:]
    position_part = (position_part.astype(f32) + seq_swap(position_part).astype(f32)).astype(low)
    part1 = joint_sum.astype(low)
    projection_part = part1[:, mine:].reshape(half, model)
    projection_pair = core_swap(projection_part)
    projection_sum = jnp.concatenate(
        [
            jnp.where(core == 0, projection_part, projection_pair),
            jnp.where(core == 0, projection_pair, projection_part),
        ],
        axis=0,
    )
    finals = jnp.concatenate([part0, part1[:, :mine], projection_sum], axis=1)
    finals_other = seq_swap(finals)
    projection_total = jnp.where(core == side, finals[:, 2 * mine :], finals_other[:, 2 * mine :]).astype(f32)
    highway_total = (
        by_seq(
            finals[:, : 2 * mine].reshape(piece, 2, chips, piece),
            finals_other[:, : 2 * mine].reshape(piece, 2, chips, piece),
        )
        .transpose(1, 2, 3, 0, 4)
        .reshape(piece, 2 * filters)
        .astype(f32)
    )

    conv_rows = WIDTHS * features
    table_rows = -(-vocab * features // mine)
    table_flat = jnp.pad(table_grad.reshape(-1), (0, table_rows * mine - vocab * features))
    entries = [
        merged_grad[:conv_rows],
        conv_bias_grad[None],
        highway_bias_grad.reshape(2, mine),
        table_flat.reshape(table_rows, mine),
        jnp.concatenate([norm1_gain_grad, norm1_bias_grad, norm2_gain_grad, norm2_bias_grad]).reshape(-1, mine),
    ]
    starts = [0]
    for row in entries:
        starts.append(starts[-1] + row.shape[0])
    padded = -(-starts[-1] // size) * size
    small = jnp.pad(jnp.concatenate(entries, axis=0), ((0, padded - starts[-1]), (0, 0)))
    small = after(small, joint_sum, attention_both)
    small = scatter_outer(scatter_middle(scatter_core(cut(small)))).astype(low)
    share = small.shape[0]
    small = jnp.concatenate([small, seq_swap(small), position_part], axis=0)
    near = gather_near(outer_pieces(small))
    across = middle_swap(near)
    small = gather((near, across, core_swap(near), core_swap(across))).reshape(size, -1, mine)
    small_own = small[:, :share].reshape(padded, mine)
    small_other = small[:, share : 2 * share].reshape(padded, mine)
    own = [small_own[starts[i] : starts[i + 1]] for i in range(len(entries))]
    other = [small_other[starts[i] : starts[i + 1]] for i in range(len(entries))]
    conv_all = (
        by_seq(own[0].reshape(conv_rows, chips, piece), other[0].reshape(conv_rows, chips, piece))
        .transpose(1, 2, 0, 3)
        .reshape(conv_rows, filters)
        .astype(f32)
    )
    conv_bias_total = (
        by_seq(own[1].reshape(chips, piece), other[1].reshape(chips, piece))
        .transpose(1, 0, 2)
        .reshape(filters)
        .astype(f32)
    )
    highway_bias_total = (
        by_seq(own[2].reshape(2, chips, piece), other[2].reshape(2, chips, piece))
        .transpose(1, 2, 0, 3)
        .reshape(2 * filters)
        .astype(f32)
    )
    table_total = (own[3].astype(f32) + other[3].astype(f32)).reshape(-1)
    table_total = table_total[: vocab * features].reshape(vocab, features)
    norms = (own[4].astype(f32) + other[4].astype(f32)).reshape(4, model)
    position_total = small[:, 2 * share :].reshape(2 * words, model).astype(f32)
    kernel_grads = []
    first = 0
    for kernel in kernels:
        kernel_grads.append(conv_all[: kernel.shape[0], first : first + kernel.shape[1]])
        first = first + kernel.shape[1]
    return (
        layer_out[None],
        table_total,
        *kernel_grads,
        conv_bias_total,
        highway_total,
        highway_bias_total,
        projection_total,
        position_total,
        attention_total,
        output_total,
        norms[0],
        norms[1],
        inward_total,
        outward_total,
        norms[2],
        norms[3],
    )


def solution(mesh):
    placed = (
        P("dp", "seq", None),
        P("dp", "seq"),
        P("dp"),
        P(),
        P(),
        P(),
        P(),
        P(),
        P(),
        P(),
        P(),
        P(),
        P("dp", None),
        P(),
        P("dp", None),
        P(),
        P("dp", None),
        P("dp", None),
        P(),
        P(),
        P("dp", None),
        P("dp", None),
        P(),
        P(),
        P("dp", "seq", None),
    )
    return jax.shard_map(
        body,
        mesh=mesh,
        in_specs=placed,
        out_specs=(
            P("dp", "seq", None),
            P(),
            P(),
            P(),
            P(),
            P(),
            P(),
            P(),
            P(),
            P(),
            P("dp", None),
            P(),
            P("dp", None),
            P(),
            P("dp", None),
            P("dp", None),
            P(),
            P(),
            P("dp", None),
            P("dp", None),
            P(),
            P(),
        ),
        check_vma=False,
    )
```

time: 1380 us -> 595 us (0.43)
  waiting for transfers between devices: 1080 us -> 172 us
  starting transfers between devices: 0.68 us -> 46.2 us
  other arithmetic: 23.2 us -> 63.7 us
  local copies, waits for them, and re-layouts: 48.7 us -> 82.8 us
  Pallas kernels: 85.5 us -> 104 us
  matrix products: 117 us -> 101 us
    reduce_scatter x7 -> x2, waiting for transfers between devices: 436 us -> 0.02 us  [the longest x1 0.02 us: body(): lax.psum_scatter(after(highway_rows, forward_sum), 'dp', scatter_dimensio...]
    psum x3 -> x0, waiting for transfers between devices: 337 us -> none  [the longest x2 273 us: body(): lax.psum((table_grad, kernel_grads[0], kernel_grads[1], kernel_grads[2],...]
    all_gather x7 -> x2, waiting for transfers between devices: 305 us -> 21.3 us  [the longest x1 19.8 us: body(): lax.all_gather(after(forward_shard, forwards[0][0]), 'dp', axis=0, tiled=...]
    ppermute x0 -> x43, waiting for transfers between devices: none -> 151 us  [the longest x14 76.7 us: seq_swap(): return lax.ppermute(value, 'seq', [(0, 1), (1, 0)])]
    ppermute x0 -> x43, starting transfers between devices: none -> 45.8 us  [the longest x15 23.1 us: outer_shift(): lax.ppermute(value, 'dp', [(spot, (spot - 4 * steps) % size) for spot in...]
    add x1 -> x13, other arithmetic: 0.93 us -> 19.3 us  [the longest x3 8.86 us: scatter_core(): pick(parts, slot, axis).astype(jnp.float32) + other.astype(jnp.float32)]
    unnamed x177 -> x197, local copies, waits for them, and re-layouts: 31 us -> 14.9 us
    dot_general x10 -> x22, matrix products: 56.4 us -> 42.5 us  [the longest x2 10 us: body(): jnp.dot(hidden0_all, highway_parts[part], preferred_element_type=f32)]
  transfers between devices with their start and end apart: 17 -> 47, of which waited for: 16 -> 21; matrix products, arithmetic and copies ran while one was open for 10% -> 29% of each run, Pallas kernels for 6% -> 18%
where the time goes in v2:
time: 595 us; the launch traced here: 587 us
  waiting for transfers between devices  172 us (29%)
  Pallas kernels  104 us (17%)
  matrix products  101 us (17%)
  local copies, waits for them, and re-layouts  82.8 us (14%)
  other arithmetic  63.7 us (11%)
  starting transfers between devices  46.2 us (8%)
  between operations  17.3 us (3%)
    ppermute x14, waiting for transfers between devices, seq_swap(): return lax.ppermute(value, 'seq', [(0, 1), (1, 0)])  76.7 us
    pallas_call x4, Pallas kernels, conv_backward(): pl.pallas_call(kernel, grid=(steps,), in_specs=[pl.BlockSpec((rows, LANES...  59.8 us
    ppermute x15, waiting for transfers between devices, outer_shift(): lax.ppermute(value, 'dp', [(spot, (spot - 4 * steps) % size) for spot in...  51.9 us
    pallas_call x2, Pallas kernels, conv_forward(): pl.pallas_call(conv_forward_kernel, grid=(steps,), in_specs=[pl.BlockSpec...  42.4 us
    ppermute x15, starting transfers between devices, outer_shift(): lax.ppermute(value, 'dp', [(spot, (spot - 4 * steps) % size) for spot in...  23.1 us
    ppermute x5, waiting for transfers between devices, middle_swap(): return lax.ppermute(value, 'dp', [(spot, spot ^ 2) for spot in range(size)])  20.5 us
    all_gather x1, waiting for transfers between devices, body(): lax.all_gather(after(forward_shard, forwards[0][0]), 'dp', axis=0, tiled=...  19.8 us
    ppermute x14, starting transfers between devices, seq_swap(): return lax.ppermute(value, 'seq', [(0, 1), (1, 0)])  18.3 us
  transfers between devices with their start and end apart: 47, of which 21 were waited for; matrix products, arithmetic and copies ran while one was open for 29% of the time, Pallas kernels for 18%

profile of v2, /device:TPU:0, one launch (start us, length us, event | category | flops | bytes accessed | tf_op | source)
XLA Modules:
  0.0 587.4 jit_solution(10975835693617723557)
XLA Ops:
  29.7 4.4 convolution_convert_fusion.1
  34.1 21.1 %conv_forward.2 = (f32[256,1024]{1,0:T(8,128)}, f32[256,1024]{1,0:T(8,128)}, bf16[12800,128]{1,0:T(8,128)(2,1)}, bf16[128,12800]{1,0:T(8,128)(2,1)}) custom-call(bf16[50,256,128]{2,1,0:T(8,128)(2,1)} %bitcast.334, s32[256,1]{1,0:T(8,128)} %copy.234.lens_ref, bf16[128,1024]{1,0:T(8,128)(2,1)} %copy.235.weight_ref.refs_3_), custom_call_target="tpu_custom_call" | custom-call | flops 3355443200 | bytes 65536000 | tf_op jit(solution)/shard_map/conv_forward/pallas_call | solution.py:235
  56.7 4.4 convolution_convert_fusion
  61.9 21.2 %conv_forward.3 = (f32[256,1024]{1,0:T(8,128)}, f32[256,1024]{1,0:T(8,128)}, bf16[12800,128]{1,0:T(8,128)(2,1)}, bf16[128,12800]{1,0:T(8,128)(2,1)}) custom-call(bf16[50,256,128]{2,1,0:T(8,128)(2,1)} %bitcast.333, s32[256,1]{1,0:T(8,128)} %slice.528.lens_ref, bf16[128,1024]{1,0:T(8,128)(2,1)} %copy.235.weight_ref.refs_3_), custom_call_target="tpu_custom_call" | custom-call | flops 3355443200 | bytes 65536000 | tf_op jit(solution)/shard_map/conv_forward/pallas_call | solution.py:235
  93.7 16.8 %collective-permute-done.2 = bf16[256,1024]{1,0:T(8,128)(2,1)S(1)} collective-permute-done((bf16[256,1024]{1,0:T(8,128)(2,1)S(1)}, bf16[256,1024]{1,0:T(8,128)(2,1)S(1)}, u32[]{:S(2)}, u32[]{:S(2)}) %collective-permute-start.2) | collective-permute-done | bytes 524320 | tf_op jit(solution)/shard_map/ppermute | solution.py:50
  112.3 11.5 %collective-permute-done.8 = bf16[4,48,3072]{2,1,0:T(8,128)(2,1)} collective-permute-done((bf16[4,48,3072]{2,1,0:T(8,128)(2,1)S(1)}, bf16[4,48,3072]{2,1,0:T(8,128)(2,1)}, u32[]{:S(2)}, u32[]{:S(2)}) %collective-permute-start.8) | collective-permute-done | bytes 1179680 | tf_op jit(solution)/shard_map/ppermute | solution.py:41
  132.0 5.8 fusion.15
  140.2 4.2 fusion.41
  149.6 7.2 %collective-permute-done.4 = bf16[256,768]{1,0:T(8,128)(2,1)S(1)} collective-permute-done((bf16[256,768]{1,0:T(8,128)(2,1)S(1)}, bf16[256,768]{1,0:T(8,128)(2,1)S(1)}, u32[]{:S(2)}, u32[]{:S(2)}) %collective-permute-start.4) | collective-permute-done | bytes 393248 | tf_op jit(solution)/shard_map/ppermute | solution.py:50
  163.2 16.4 %collective-permute-done.11 = bf16[256,1536]{1,0:T(8,128)(2,1)} collective-permute-done((bf16[256,1536]{1,0:T(8,128)(2,1)S(1)}, bf16[256,1536]{1,0:T(8,128)(2,1)}, u32[]{:S(2)}, u32[]{:S(2)}) %collective-permute-start.11) | collective-permute-done | bytes 786464 | tf_op jit(solution)/shard_map/ppermute | solution.py:50
  182.2 4.7 fusion.168
  187.0 4.3 fusion.72
  193.6 19.8 %all-gather.5.cloned.1.call-done = bf16[768,6144]{1,0:T(8,128)(2,1)} async-done(((bf16[48,6144]{1,0:T(8,128)(2,1)}), bf16[768,6144]{1,0:T(8,128)(2,1)}) %all-gather.5.cloned.1.call-update) | async-done | bytes 9437200 | tf_op jit(solution)/shard_map/all_gather | solution.py:437
  213.4 10.2 %multiply_convert_fusion.1 = (bf16[256,3072]{1,0:T(8,128)(2,1)S(1)}, f32[256,3072]{1,0:T(8,128)S(1)}, f32[256,3072]{1,0:T(8,128)S(1)}) fusion(bf16[768,6144]{1,0:T(8,128)(2,1)} %all-gather.5.cloned.1.call-done, f32[256,768]{1,0:T(8,128)S(1)} %get-tuple-element.264, f32[768]{0:T(1024)S(1)} %convert_element_type.353, f32[768]{0:T(1024)S(1)} %convert_element_type.352, ...), kind=kOutput, calls=%fused_computation.46 | convolution fusion | flops 1260060672 | bytes 13377536 | tf_op jit(solution)/shard_map/dot_general | solution.py:490
  264.3 14.6 %collective-permute-done.12 = bf16[256,1536]{0,1:T(8,128)(2,1)} collective-permute-done((bf16[256,1536]{0,1:T(8,128)(2,1)}, bf16[256,1536]{0,1:T(8,128)(2,1)}, u32[]{:S(2)}, u32[]{:S(2)}) %collective-permute-start.12) | collective-permute-done | bytes 786464 | tf_op jit(solution)/shard_map/ppermute | solution.py:50
  294.2 9.3 %collective-permute-done.13 = bf16[256,768]{1,0:T(8,128)(2,1)S(1)} collective-permute-done((bf16[256,768]{1,0:T(8,128)(2,1)S(1)}, bf16[256,768]{1,0:T(8,128)(2,1)S(1)}, u32[]{:S(2)}, u32[]{:S(2)}) %collective-permute-start.13) | collective-permute-done | bytes 393248 | tf_op jit(solution)/shard_map/ppermute | solution.py:50
  303.6 6.2 %convert_add_fusion.1 = f32[4,2,48,3072]{3,2,1,0:T(8,128)} fusion(bf16[4,2,48,3072]{3,2,1,0:T(8,128)(2,1)} %collective-permute-done.14, bf16[4,2,2,48,3072]{4,3,2,1,0:T(8,128)(2,1)} %bitcast.270, s32[]{:T(128)S(6)} %select_n.632), kind=kLoop, calls=%fused_computation.25 | loop fusion | flops 3538944 | bytes 9437188 | tf_op jit(solution)/shard_map/add | solution.py:96
  315.0 7.6 %convert_reduce_fusion = (f32[1024]{0:T(1024)S(1)}, bf16[512,1024]{1,0:T(8,128)(2,1)}, f32[1024]{0:T(1024)S(1)}, bf16[512,1024]{1,0:T(8,128)(2,1)}, f32[512,1024]{1,0:T(8,128)}) fusion(f32[512,1024]{1,0:T(8,128)} %get-tuple-element.260, f32[256,1024]{1,0:T(8,128)S(1)} %copy-done.33, f32[256,1024]{1,0:T(8,128)} %get-tuple-element.258, ...), kind=kOutput, calls=%fused_computation.89 | convolution fusion | flops 815265792 | bytes 12857344 | tf_op jit(solution)/shard_map/td,fd->tf/dot_general | solution.py:562
  325.5 4.4 convolution_convert_fusion.6
  344.8 4.4 convolution_convert_fusion.5
  350.8 5.4 pad_maximum_fusion
  364.7 4.8 collective-permute-start.19
  377.0 8.8 %collective-permute-done.21 = bf16[48,3072]{1,0:T(8,128)(2,1)S(1)} collective-permute-done((bf16[48,3072]{1,0:T(8,128)(2,1)S(1)}, bf16[48,3072]{1,0:T(8,128)(2,1)S(1)}, u32[]{:S(2)}, u32[]{:S(2)}) %collective-permute-start.21) | collective-permute-done | bytes 294944 | tf_op jit(solution)/shard_map/ppermute | solution.py:46
  385.7 23.5 %collective-permute-done.20 = bf16[48,3072]{1,0:T(8,128)(2,1)S(1)} collective-permute-done((bf16[48,3072]{1,0:T(8,128)(2,1)S(1)}, bf16[48,3072]{1,0:T(8,128)(2,1)S(1)}, u32[]{:S(2)}, u32[]{:S(2)}) %collective-permute-start.20) | collective-permute-done | bytes 294944 | tf_op jit(solution)/shard_map/ppermute | solution.py:46
  417.0 14.8 %conv_backward.4 = (f32[128,1024]{1,0:T(8,128)}, f32[272,128]{1,0:T(8,128)}) custom-call(bf16[12800,128]{1,0:T(8,128)(2,1)} %get-tuple-element.50.refs_0_, bf16[128,12800]{1,0:T(8,128)(2,1)} %get-tuple-element.51.refs_1_, s32[4,1,3200]{2,1,0:T(1,128)} %reshape.517.refs_2_, bf16[128,1024]{1,0:T(8,128)(2,1)} %copy.235.weight_ref.refs_3_, ...), custom_call_target="tpu_custom_call" | custom-call | flops 5033164800 | bytes 52428800 | tf_op jit(solution)/shard_map/conv_backward/pallas_call | solution.py:276
  431.8 15.1 %conv_backward.5 = (f32[128,1024]{1,0:T(8,128)}, f32[272,128]{1,0:T(8,128)}) custom-call(bf16[12800,128]{1,0:T(8,128)(2,1)} %get-tuple-element.50.refs_0_, bf16[128,12800]{1,0:T(8,128)(2,1)} %get-tuple-element.51.refs_1_, s32[4,1,3200]{2,1,0:T(1,128)} %reshape.517.refs_2_, bf16[128,1024]{1,0:T(8,128)(2,1)} %copy.235.weight_ref.refs_3_, ...), custom_call_target="tpu_custom_call" | custom-call | flops 5033164800 | bytes 52428800 | tf_op jit(solution)/shard_map/conv_backward/pallas_call | solution.py:276
  455.4 15.0 %conv_backward.6 = (f32[128,1024]{1,0:T(8,128)}, f32[272,128]{1,0:T(8,128)}) custom-call(bf16[12800,128]{1,0:T(8,128)(2,1)} %get-tuple-element.60.refs_0_, bf16[128,12800]{1,0:T(8,128)(2,1)} %get-tuple-element.61.refs_1_, s32[4,1,3200]{2,1,0:T(1,128)} %reshape.518.refs_2_, bf16[128,1024]{1,0:T(8,128)(2,1)} %copy.235.weight_ref.refs_3_, ...), custom_call_target="tpu_custom_call" | custom-call | flops 5033164800 | bytes 52428800 | tf_op jit(solution)/shard_map/conv_backward/pallas_call | solution.py:276
  470.4 14.9 %conv_backward.7 = (f32[128,1024]{1,0:T(8,128)}, f32[272,128]{1,0:T(8,128)}) custom-call(bf16[12800,128]{1,0:T(8,128)(2,1)} %get-tuple-element.60.refs_0_, bf16[128,12800]{1,0:T(8,128)(2,1)} %get-tuple-element.61.refs_1_, s32[4,1,3200]{2,1,0:T(1,128)} %reshape.518.refs_2_, bf16[128,1024]{1,0:T(8,128)(2,1)} %copy.235.weight_ref.refs_3_, ...), custom_call_target="tpu_custom_call" | custom-call | flops 5033164800 | bytes 52428800 | tf_op jit(solution)/shard_map/conv_backward/pallas_call | solution.py:276
  494.8 6.1 %collective-permute-done.24 = bf16[128,1408]{1,0:T(8,128)(2,1)} collective-permute-done((bf16[128,1408]{1,0:T(8,128)(2,1)}, bf16[128,1408]{1,0:T(8,128)(2,1)}, u32[]{:S(2)}, u32[]{:S(2)}) %collective-permute-start.24) | collective-permute-done | bytes 360480 | tf_op jit(solution)/shard_map/ppermute | solution.py:46
  519.7 5.0 collective-permute-done.42
  545.2 6.9 %collective-permute-done.37 = bf16[4,40,1024]{2,1,0:T(8,128)(2,1)} collective-permute-done((bf16[4,40,1024]{2,1,0:T(8,128)(2,1)S(1)}, bf16[4,40,1024]{2,1,0:T(8,128)(2,1)}, u32[]{:S(2)}, u32[]{:S(2)}) %collective-permute-start.37) | collective-permute-done | bytes 327712 | tf_op jit(solution)/shard_map/ppermute | solution.py:41
  553.2 7.4 %collective-permute-done.41 = bf16[128,2816]{1,0:T(8,128)(2,1)S(1)} collective-permute-done((bf16[128,2816]{1,0:T(8,128)(2,1)S(1)}, bf16[128,2816]{1,0:T(8,128)(2,1)S(1)}, u32[]{:S(2)}, u32[]{:S(2)}) %collective-permute-start.41) | collective-permute-done | bytes 720928 | tf_op jit(solution)/shard_map/ppermute | solution.py:50
  (543 shorter events, 243.6 us)
Async XLA Ops:
  7.2 121.6 %all-gather.3.cloned.1.call-start = ((), (), s32[]{:S(2)}) async-start(), calls=%async_computation.2 | async-start | bytes 10584064 | tf_op jit(solution)/shard_map/all_gather | solution.py:410
  11.6 201.8 %all-gather.5.cloned.1.call-start = ((), (), s32[]{:S(2)}) async-start(), calls=%async_computation.3 | async-start | bytes 10027008 | tf_op jit(solution)/shard_map/all_gather | solution.py:437
  11.7 76.5 %collective-permute-start.7 = (bf16[48,3072]{1,0:T(8,128)(2,1)S(1)}, bf16[48,3072]{1,0:T(8,128)(2,1)S(1)}, u32[]{:S(2)}, u32[]{:S(2)}) collective-permute-start(bf16[48,3072]{1,0:T(8,128)(2,1)S(1)} %constant_dynamic-update-slice_fusion.32), channel_id=1, source_target_pairs={{0,8},{2,10},{4,12},{6,14},{8,16},{10,18},{12,20},{14,22},{16,24},... | collective-permute-start | bytes 884744 | tf_op jit(solution)/shard_map/ppermute | solution.py:46
  14.4 73.8 %collective-permute-start.6 = (bf16[48,3072]{1,0:T(8,128)(2,1)S(1)}, bf16[48,3072]{1,0:T(8,128)(2,1)S(1)}, u32[]{:S(2)}, u32[]{:S(2)}) collective-permute-start(bf16[48,3072]{1,0:T(8,128)(2,1)S(1)} %constant_dynamic-update-slice_fusion.32), channel_id=1, source_target_pairs={{0,16},{2,18},{4,20},{6,22},{8,24},{10,26},{12,28},{14,30},{16,0},... | collective-permute-start | bytes 884744 | tf_op jit(solution)/shard_map/ppermute | solution.py:46
  17.0 71.2 %collective-permute-start.5 = (bf16[48,3072]{1,0:T(8,128)(2,1)S(1)}, bf16[48,3072]{1,0:T(8,128)(2,1)S(1)}, u32[]{:S(2)}, u32[]{:S(2)}) collective-permute-start(bf16[48,3072]{1,0:T(8,128)(2,1)S(1)} %constant_dynamic-update-slice_fusion.32), channel_id=1, source_target_pairs={{0,24},{2,26},{4,28},{6,30},{8,0},{10,2},{12,4},{14,6},{16,8},{18,... | collective-permute-start | bytes 884744 | tf_op jit(solution)/shard_map/ppermute | solution.py:46
  18.5 37.5 %collective-permute-start = (s32[256,51]{1,0:T(8,128)S(1)}, s32[256,51]{1,0:T(8,128)S(1)}, u32[]{:S(2)}, u32[]{:S(2)}) collective-permute-start(s32[256,51]{1,0:T(8,128)S(1)} %copy.236), channel_id=1, source_target_pairs={{0,1},{1,0},{2,3},{3,2},{4,5},{5,4},{6,7},{7,6},{8,9},{9,8},{10,11... | collective-permute-start | bytes 156680 | tf_op jit(solution)/shard_map/ppermute | solution.py:50
  55.3 361.6 %reduce-scatter.3.cloned.1.call-start = ((), (), s32[]{:S(2)}) async-start(), calls=%async_computation.4 | async-start | bytes 10027008 | tf_op jit(solution)/shard_map/reduce_scatter | solution.py:518
  86.2 25.2 %collective-permute-start.1 = (bf16[256,1024]{1,0:T(8,128)(2,1)S(1)}, bf16[256,1024]{1,0:T(8,128)(2,1)S(1)}, u32[]{:S(2)}, u32[]{:S(2)}) collective-permute-start(bf16[256,1024]{1,0:T(8,128)(2,1)S(1)} %get-tuple-element.211), channel_id=1, source_target_pairs={{0,1},{1,0},{2,3},{3,2},{4,5},{5,4},{6,7},{7,6},{8,9},{9,8},{10,11... | collective-permute-start | bytes 1572872 | tf_op jit(solution)/shard_map/ppermute | solution.py:50
  86.7 23.9 %collective-permute-start.2 = (bf16[256,1024]{1,0:T(8,128)(2,1)S(1)}, bf16[256,1024]{1,0:T(8,128)(2,1)S(1)}, u32[]{:S(2)}, u32[]{:S(2)}) collective-permute-start(bf16[256,1024]{1,0:T(8,128)(2,1)S(1)} %get-tuple-element.257), channel_id=1, source_target_pairs={{0,1},{1,0},{2,3},{3,2},{4,5},{5,4},{6,7},{7,6},{8,9},{9,8},{10,11... | collective-permute-start | bytes 1572872 | tf_op jit(solution)/shard_map/ppermute | solution.py:50
  88.3 37.9 %collective-permute-start.9 = (bf16[4,48,3072]{2,1,0:T(8,128)(2,1)S(1)}, bf16[4,48,3072]{2,1,0:T(8,128)(2,1)S(1)}, u32[]{:S(2)}, u32[]{:S(2)}) collective-permute-start(bf16[4,48,3072]{2,1,0:T(8,128)(2,1)S(1)} %bitcast_dynamic-update-slice_fusion.8), channel_id=1, source_target_pairs={{0,2},{2,0},{4,6},{6,4},{8,10},{10,8},{12,14},{14,12},{16,18},{18,... | collective-permute-start | bytes 3538952 | tf_op jit(solution)/shard_map/ppermute | solution.py:36
  88.4 35.4 %collective-permute-start.8 = (bf16[4,48,3072]{2,1,0:T(8,128)(2,1)S(1)}, bf16[4,48,3072]{2,1,0:T(8,128)(2,1)}, u32[]{:S(2)}, u32[]{:S(2)}) collective-permute-start(bf16[4,48,3072]{2,1,0:T(8,128)(2,1)S(1)} %bitcast_dynamic-update-slice_fusion.8), channel_id=1, source_target_pairs={{0,4},{2,6},{4,0},{6,2},{8,12},{10,14},{12,8},{14,10},{16,20},{18,... | collective-permute-start | bytes 3538952 | tf_op jit(solution)/shard_map/ppermute | solution.py:41
  123.8 23.4 %collective-permute-start.10 = (bf16[4,48,3072]{2,1,0:T(8,128)(2,1)}, bf16[4,48,3072]{2,1,0:T(8,128)(2,1)}, u32[]{:S(2)}, u32[]{:S(2)}) collective-permute-start(bf16[4,48,3072]{2,1,0:T(8,128)(2,1)} %collective-permute-done.8), channel_id=1, source_target_pairs={{0,2},{2,0},{4,6},{6,4},{8,10},{10,8},{12,14},{14,12},{16,18},{18,... | collective-permute-start | bytes 3538952 | tf_op jit(solution)/shard_map/ppermute | solution.py:36
  160.4 19.2 %collective-permute-start.11 = (bf16[256,1536]{1,0:T(8,128)(2,1)S(1)}, bf16[256,1536]{1,0:T(8,128)(2,1)}, u32[]{:S(2)}, u32[]{:S(2)}) collective-permute-start(bf16[256,1536]{1,0:T(8,128)(2,1)S(1)} %slice.568), channel_id=1, source_target_pairs={{0,1},{1,0},{2,3},{3,2},{4,5},{5,4},{6,7},{7,6},{8,9},{9,8},{10,11... | collective-permute-start | bytes 2359304 | tf_op jit(solution)/shard_map/ppermute | solution.py:50
  258.9 20.0 %collective-permute-start.12 = (bf16[256,1536]{0,1:T(8,128)(2,1)}, bf16[256,1536]{0,1:T(8,128)(2,1)}, u32[]{:S(2)}, u32[]{:S(2)}) collective-permute-start(bf16[256,1536]{0,1:T(8,128)(2,1)} %fusion.49), channel_id=1, source_target_pairs={{0,1},{1,0},{2,3},{3,2},{4,5},{5,4},{6,7},{7,6},{8,9},{9,8},{10,11... | collective-permute-start | bytes 2359304 | tf_op jit(solution)/shard_map/ppermute | solution.py:50
  285.9 17.7 %collective-permute-start.14 = (bf16[4,2,48,3072]{3,2,1,0:T(8,128)(2,1)}, bf16[4,2,48,3072]{3,2,1,0:T(8,128)(2,1)}, u32[]{:S(2)}, u32[]{:S(2)}) collective-permute-start(bf16[4,2,48,3072]{3,2,1,0:T(8,128)(2,1)} %dynamic-slice_bitcast_fusion), channel_id=1, source_target_pairs={{0,2},{2,0},{4,6},{6,4},{8,10},{10,8},{12,14},{14,12},{16,18},{18,... | collective-permute-start | bytes 7077896 | tf_op jit(solution)/shard_map/ppermute | solution.py:36
  286.9 237.9 %reduce-scatter.5.cloned.1.call-start = ((), (), s32[]{:S(2)}) async-start(), calls=%async_computation.5 | async-start | bytes 5292032 | tf_op jit(solution)/shard_map/reduce_scatter | solution.py:593
  291.8 11.7 %collective-permute-start.13 = (bf16[256,768]{1,0:T(8,128)(2,1)S(1)}, bf16[256,768]{1,0:T(8,128)(2,1)S(1)}, u32[]{:S(2)}, u32[]{:S(2)}) collective-permute-start(bf16[256,768]{1,0:T(8,128)(2,1)S(1)} %fusion.68), channel_id=1, source_target_pairs={{0,1},{1,0},{2,3},{3,2},{4,5},{5,4},{6,7},{7,6},{8,9},{9,8},{10,11... | collective-permute-start | bytes 1179656 | tf_op jit(solution)/shard_map/ppermute | solution.py:50
  325.4 37.5 %collective-permute-start.16 = (bf16[4,48,3072]{2,1,0:T(8,128)(2,1)}, bf16[4,48,3072]{2,1,0:T(8,128)(2,1)}, u32[]{:S(2)}, u32[]{:S(2)}) collective-permute-start(bf16[4,48,3072]{2,1,0:T(8,128)(2,1)} %fusion.75), channel_id=1, source_target_pairs={{0,4},{2,6},{4,0},{6,2},{8,12},{10,14},{12,8},{14,10},{16,20},{18,... | collective-permute-start | bytes 3538952 | tf_op jit(solution)/shard_map/ppermute | solution.py:41
  331.9 79.1 %collective-permute-start.17 = (bf16[4,2,128,1408]{3,2,1,0:T(8,128)(2,1)}, bf16[4,2,128,1408]{3,2,1,0:T(8,128)(2,1)}, u32[]{:S(2)}, u32[]{:S(2)}) collective-permute-start(bf16[4,2,128,1408]{3,2,1,0:T(8,128)(2,1)} %fusion.37), channel_id=1, source_target_pairs={{0,2},{2,0},{4,6},{6,4},{8,10},{10,8},{12,14},{14,12},{16,18},{18,... | collective-permute-start | bytes 8650760 | tf_op jit(solution)/shard_map/ppermute | solution.py:36
  339.0 30.5 %collective-permute-start.15 = (bf16[256,1024]{1,0:T(8,128)(2,1)}, bf16[256,1024]{1,0:T(8,128)(2,1)S(1)}, u32[]{:S(2)}, u32[]{:S(2)}) collective-permute-start(bf16[256,1024]{1,0:T(8,128)(2,1)} %get-tuple-element.237), channel_id=1, source_target_pairs={{0,1},{1,0},{2,3},{3,2},{4,5},{5,4},{6,7},{7,6},{8,9},{9,8},{10,11... | collective-permute-start | bytes 1572872 | tf_op jit(solution)/shard_map/ppermute | solution.py:50
  340.3 29.9 %collective-permute-start.18 = (bf16[256,1024]{1,0:T(8,128)(2,1)}, bf16[256,1024]{1,0:T(8,128)(2,1)}, u32[]{:S(2)}, u32[]{:S(2)}) collective-permute-start(bf16[256,1024]{1,0:T(8,128)(2,1)} %get-tuple-element.238), channel_id=1, source_target_pairs={{0,1},{1,0},{2,3},{3,2},{4,5},{5,4},{6,7},{7,6},{8,9},{9,8},{10,11... | collective-permute-start | bytes 1572872 | tf_op jit(solution)/shard_map/ppermute | solution.py:50
  364.7 12.3 %collective-permute-start.19 = (bf16[48,3072]{1,0:T(8,128)(2,1)S(1)}, bf16[48,3072]{1,0:T(8,128)(2,1)S(1)}, u32[]{:S(2)}, u32[]{:S(2)}) collective-permute-start(bf16[48,3072]{1,0:T(8,128)(2,1)S(1)} %get-tuple-element.234), channel_id=1, source_target_pairs={{0,24},{2,26},{4,28},{6,30},{8,0},{10,2},{12,4},{14,6},{16,8},{18,... | collective-permute-start | bytes 884744 | tf_op jit(solution)/shard_map/ppermute | solution.py:46
  369.5 16.2 %collective-permute-start.21 = (bf16[48,3072]{1,0:T(8,128)(2,1)S(1)}, bf16[48,3072]{1,0:T(8,128)(2,1)S(1)}, u32[]{:S(2)}, u32[]{:S(2)}) collective-permute-start(bf16[48,3072]{1,0:T(8,128)(2,1)S(1)} %get-tuple-element.235), channel_id=1, source_target_pairs={{0,8},{2,10},{4,12},{6,14},{8,16},{10,18},{12,20},{14,22},{16,24},... | collective-permute-start | bytes 884744 | tf_op jit(solution)/shard_map/ppermute | solution.py:46
  369.5 39.8 %collective-permute-start.20 = (bf16[48,3072]{1,0:T(8,128)(2,1)S(1)}, bf16[48,3072]{1,0:T(8,128)(2,1)S(1)}, u32[]{:S(2)}, u32[]{:S(2)}) collective-permute-start(bf16[48,3072]{1,0:T(8,128)(2,1)S(1)} %get-tuple-element.236), channel_id=1, source_target_pairs={{0,16},{2,18},{4,20},{6,22},{8,24},{10,26},{12,28},{14,30},{16,0},... | collective-permute-start | bytes 884744 | tf_op jit(solution)/shard_map/ppermute | solution.py:46
  416.3 30.7 %collective-permute-start.22 = (bf16[4,128,1408]{2,1,0:T(8,128)(2,1)S(1)}, bf16[4,128,1408]{2,1,0:T(8,128)(2,1)}, u32[]{:S(2)}, u32[]{:S(2)}) collective-permute-start(bf16[4,128,1408]{2,1,0:T(8,128)(2,1)S(1)} %fusion.60), channel_id=1, source_target_pairs={{0,4},{2,6},{4,0},{6,2},{8,12},{10,14},{12,8},{14,10},{16,20},{18,... | collective-permute-start | bytes 4325384 | tf_op jit(solution)/shard_map/ppermute | solution.py:41
  451.1 43.7 %collective-permute-start.23 = (bf16[128,1408]{1,0:T(8,128)(2,1)}, bf16[128,1408]{1,0:T(8,128)(2,1)}, u32[]{:S(2)}, u32[]{:S(2)}) collective-permute-start(bf16[128,1408]{1,0:T(8,128)(2,1)} %get-tuple-element.221), channel_id=1, source_target_pairs={{0,24},{2,26},{4,28},{6,30},{8,0},{10,2},{12,4},{14,6},{16,8},{18,... | collective-permute-start | bytes 1081352 | tf_op jit(solution)/shard_map/ppermute | solution.py:46
  454.8 40.0 %collective-permute-start.25 = (bf16[128,1408]{1,0:T(8,128)(2,1)}, bf16[128,1408]{1,0:T(8,128)(2,1)}, u32[]{:S(2)}, u32[]{:S(2)}) collective-permute-start(bf16[128,1408]{1,0:T(8,128)(2,1)} %get-tuple-element.222), channel_id=1, source_target_pairs={{0,8},{2,10},{4,12},{6,14},{8,16},{10,18},{12,20},{14,22},{16,24},... | collective-permute-start | bytes 1081352 | tf_op jit(solution)/shard_map/ppermute | solution.py:46
  454.8 46.1 %collective-permute-start.24 = (bf16[128,1408]{1,0:T(8,128)(2,1)}, bf16[128,1408]{1,0:T(8,128)(2,1)}, u32[]{:S(2)}, u32[]{:S(2)}) collective-permute-start(bf16[128,1408]{1,0:T(8,128)(2,1)} %get-tuple-element.223), channel_id=1, source_target_pairs={{0,16},{2,18},{4,20},{6,22},{8,24},{10,26},{12,28},{14,30},{16,0},... | collective-permute-start | bytes 1081352 | tf_op jit(solution)/shard_map/ppermute | solution.py:46
  508.8 15.9 %collective-permute-start.42 = (bf16[48,6144]{1,0:T(8,128)(2,1)S(1)}, bf16[48,6144]{1,0:T(8,128)(2,1)S(1)}, u32[]{:S(2)}, u32[]{:S(2)}) collective-permute-start(bf16[48,6144]{1,0:T(8,128)(2,1)S(1)} %copy-done.41), channel_id=1, source_target_pairs={{0,1},{1,0},{2,3},{3,2},{4,5},{5,4},{6,7},{7,6},{8,9},{9,8},{10,11... | collective-permute-start | bytes 1769480 | tf_op jit(solution)/shard_map/ppermute | solution.py:50
  519.0 15.7 %collective-permute-start.32 = (bf16[8,1024]{1,0:T(8,128)(2,1)S(1)}, bf16[8,1024]{1,0:T(8,128)(2,1)S(1)}, u32[]{:S(2)}, u32[]{:S(2)}) collective-permute-start(bf16[8,1024]{1,0:T(8,128)(2,1)S(1)} %fusion.131), channel_id=1, source_target_pairs={{0,1},{1,0},{2,3},{3,2},{4,5},{5,4},{6,7},{7,6},{8,9},{9,8},{10,11... | collective-permute-start | bytes 49160 | tf_op jit(solution)/shard_map/ppermute | solution.py:50
  544.6 15.9 %collective-permute-start.41 = (bf16[128,2816]{1,0:T(8,128)(2,1)S(1)}, bf16[128,2816]{1,0:T(8,128)(2,1)S(1)}, u32[]{:S(2)}, u32[]{:S(2)}) collective-permute-start(bf16[128,2816]{1,0:T(8,128)(2,1)S(1)} %maximum_maximum_fusion), channel_id=1, source_target_pairs={{0,1},{1,0},{2,3},{3,2},{4,5},{5,4},{6,7},{7,6},{8,9},{9,8},{10,11... | collective-permute-start | bytes 2162696 | tf_op jit(solution)/shard_map/ppermute | solution.py:50
  552.1 15.8 %collective-permute-start.39 = (bf16[4,40,1024]{2,1,0:T(8,128)(2,1)}, bf16[4,40,1024]{2,1,0:T(8,128)(2,1)}, u32[]{:S(2)}, u32[]{:S(2)}) collective-permute-start(bf16[4,40,1024]{2,1,0:T(8,128)(2,1)} %collective-permute-done.37), channel_id=1, source_target_pairs={{0,2},{2,0},{4,6},{6,4},{8,10},{10,8},{12,14},{14,12},{16,18},{18,... | collective-permute-start | bytes 983048 | tf_op jit(solution)/shard_map/ppermute | solution.py:36
  (109 other events, 1002.3 us)
Sparse Core Ops, SparseCore 0:
  11.7 117.0 all-gather.2
  131.7 81.6 all-gather.4
  287.0 126.4 reduce-scatter.2
  417.8 99.2 reduce-scatter.4

commit v3 on v2

--- a/solution.py
+++ b/solution.py
@@ -96,20 +96,24 @@
     return pick(parts, slot, axis).astype(jnp.float32) + other.astype(jnp.float32)
 
 
-def scatter_middle(half):
+def scatter_middle(half, first=(), last=()):
     _, middle, _ = place()
-    other = middle_swap(pick(half, 1 - middle, 1).astype(jnp.bfloat16))
-    return pick(half, middle, 1) + other.astype(jnp.float32)
-
-
-def scatter_outer(quarter):
+    sent = after(pick(half, 1 - middle, 1).astype(jnp.bfloat16), *first)
+    return pick(half, middle, 1) + after(middle_swap(sent), *last).astype(jnp.float32)
+
+
+def scatter_outer(quarter, first=(), last=()):
     outer, _, _ = place()
     size = quarter.shape[0]
-    rounded = quarter.astype(jnp.bfloat16)
+    rounded = after(quarter.astype(jnp.bfloat16), *first)
+    pieces = [
+        outer_shift(pick(rounded, (outer + size - steps) % size, 0), steps) for steps in range(1, size)
+    ]
+    if last:
+        pieces = lax.optimization_barrier(tuple(pieces) + tuple(last))[: size - 1]
     total = pick(quarter, outer, 0)
-    for steps in range(1, size):
-        sent = pick(rounded, (outer + size - steps) % size, 0)
-        total = total + outer_shift(sent, steps).astype(jnp.float32)
+    for value in pieces:
+        total = total + value.astype(jnp.float32)
     return total
 
 
@@ -464,8 +468,13 @@
     embedded_low = embedded.astype(low)
     heads = model // HEAD_DIM
     projected = jnp.dot(embedded_low, attention_full, preferred_element_type=f32).astype(low)
-    pairs = projected[:, model:]
-    gathered = jnp.concatenate([pairs, seq_swap(pairs)], axis=0)
+    gathered = jnp.concatenate(
+        [
+            jnp.concatenate([pair, seq_swap(pair)], axis=0)
+            for pair in (projected[:, model : 2 * model], projected[:, 2 * model :])
+        ],
+        axis=1,
+    )
     length = gathered.shape[0]
     query_heads = projected[:, :model].reshape(words, heads, HEAD_DIM)
     key_heads = gathered[:, :model].reshape(length, heads, HEAD_DIM)
@@ -526,6 +535,7 @@
     grad_heads = grad_attended.reshape(words, heads, HEAD_DIM)
     probs = jnp.exp(score_heads(query_heads, key_heads, keep) - top) / total
     probs_again = probs.astype(jnp.bfloat16)
+    value_grad = jnp.einsum("hqk,qhd->khd", probs_again, grad_heads, preferred_element_type=f32)
     grad_probs = jnp.einsum(
         "qhd,khd->hqk", grad_heads, value_heads, preferred_element_type=jnp.float32
     )
@@ -539,12 +549,13 @@
     key_grad = (
         jnp.einsum("hqk,qhd->khd", grad_scores, query_heads, preferred_element_type=f32) * 0.125
     )
-    value_grad = jnp.einsum("hqk,qhd->khd", probs_again, grad_heads, preferred_element_type=f32)
-    pair_grads = jnp.concatenate(
-        [key_grad.reshape(length, model), value_grad.reshape(length, model)], axis=1
-    )
-    pairs_lent = pair_grads[words:].astype(low)
-    grad_pairs = pair_grads[:words] + seq_swap(pairs_lent).astype(f32)
+    value_grad = value_grad.reshape(length, model)
+    key_grad = key_grad.reshape(length, model)
+    value_back = seq_swap(value_grad[words:].astype(low))
+    key_back = seq_swap(key_grad[words:].astype(low))
+    grad_pairs = jnp.concatenate(
+        [key_grad[:words] + key_back.astype(f32), value_grad[:words] + value_back.astype(f32)], axis=1
+    )
     grad_projected = jnp.concatenate([grad_query.reshape(words, model), grad_pairs], axis=1).astype(low)
     attention_in_grad = jnp.einsum(
         "td,te->de", embedded_low, grad_projected, preferred_element_type=f32
@@ -597,8 +608,6 @@
         cut(jnp.concatenate([highway_grads[1], projection_grad.reshape(filters, model // 2)], axis=1))
     )
     attention_quarter = scatter_middle(attention_half)
-    joint_quarter = scatter_middle(joint_half)
-    attention_sum = scatter_outer(attention_quarter)
     turned = conv_weight.T
     shares = [grad_pooled[part] / forwards[part][1] for part in range(2)]
     code_blocks = [
@@ -622,18 +631,22 @@
         )
 
     cuts = steps // 2
-    backs = [back(0, 0, cuts, attention_quarter, joint_half)]
-    backs.append(back(0, cuts, steps - cuts, *backs[0]))
-    backs.append(back(1, 0, cuts, attention_sum, joint_quarter, *backs[1]))
-    joint_sum = scatter_outer(joint_quarter)
-    backs.append(back(1, cuts, steps - cuts, *backs[2]))
+    backs = [back(0, 0, cuts, attention_quarter, joint_half, highway_rows)]
+    attention_sum = scatter_outer(attention_quarter, grad_pooled, backs[0])
+    joint_quarter = scatter_middle(joint_half, grad_pooled, backs[0])
+    backs.append(back(0, cuts, steps - cuts, attention_sum, joint_quarter, *backs[0]))
+    forward_both = forward_sum.astype(f32) + after(seq_swap(after(forward_sum, *backs[0])), *backs[1]).astype(f32)
+    backs.append(back(1, 0, cuts, forward_sum, *backs[1]))
+    attention_both = attention_sum + after(seq_swap(after(attention_sum.astype(low), *backs[1])), *backs[2]).astype(f32)
+    backs.append(back(1, cuts, steps - cuts, forward_both, *backs[2]))
+    joint_sum = scatter_outer(joint_quarter, backs[0], backs[3])
     merged_grad = backs[0][0] + backs[1][0] + backs[2][0] + backs[3][0]
     table_wide = backs[0][1] + backs[1][1] + backs[2][1] + backs[3][1]
     table_grad = sum(
         table_wide[:vocab, shift * features : (shift + 1) * features] for shift in range(WIDTHS)
     )
 
-    forward_total = seq_sum(forward_sum.astype(f32))
+    forward_total = forward_both
     inward_total = (
         forward_total[:, :inner_size].reshape(rows, splits, size, rows).transpose(0, 2, 1, 3).reshape(rows, inner_size)
     )
@@ -641,7 +654,6 @@
         [forward_total[:, inner_size + part * model : inner_size + (part + 1) * model] for part in range(splits)],
         axis=0,
     )
-    attention_both = seq_sum(attention_sum)
     attention_total = attention_both[:, : 3 * model]
     output_total = attention_both[:, 3 * model :]
     part0 = highway_sum[:piece]
@@ -685,10 +697,10 @@
         starts.append(starts[-1] + row.shape[0])
     padded = -(-starts[-1] // size) * size
     small = jnp.pad(jnp.concatenate(entries, axis=0), ((0, padded - starts[-1]), (0, 0)))
-    small = after(small, joint_sum, attention_both)
+    small = after(small, joint_sum, attention_both, highway_sum)
     small = scatter_outer(scatter_middle(scatter_core(cut(small)))).astype(low)
     share = small.shape[0]
-    small = jnp.concatenate([small, seq_swap(small), position_part], axis=0)
+    small = after(jnp.concatenate([small, seq_swap(small), position_part], axis=0), finals_other)
     near = gather_near(outer_pieces(small))
     across = middle_swap(near)
     small = gather((near, across, core_swap(near), core_swap(across))).reshape(size, -1, mine)

time: 595 us -> 544 us (0.914)
  waiting for transfers between devices: 172 us -> 128 us
  starting transfers between devices: 46.2 us -> 54.5 us
  matrix products: 101 us -> 95 us
    ppermute x15, waiting for transfers between devices: 51.9 us -> 4.88 us  [outer_shift(): lax.ppermute(value, 'dp', [(spot, (spot - 4 * steps) % size) for spot in...]
    unnamed x197 -> x175, local copies, waits for them, and re-layouts: 14.9 us -> 14.2 us
    ppermute x14 -> x16, starting transfers between devices: 18.3 us -> 18.8 us  [seq_swap(): return lax.ppermute(value, 'seq', [(0, 1), (1, 0)])]
    ppermute x14 -> x16, waiting for transfers between devices: 76.7 us -> 76.9 us  [seq_swap(): return lax.ppermute(value, 'seq', [(0, 1), (1, 0)])]
  transfers between devices with their start and end apart: 47 -> 49, of which waited for: 21 -> 20; matrix products, arithmetic and copies ran while one was open for 29% -> 33% of each run, Pallas kernels for 18% -> 19%
where the time goes in v3:
time: 544 us; the launch traced here: 536 us
  waiting for transfers between devices  128 us (24%)
  Pallas kernels  104 us (19%)
  matrix products  95 us (17%)
  local copies, waits for them, and re-layouts  77 us (14%)
  other arithmetic  60.5 us (11%)
  starting transfers between devices  54.5 us (10%)
  between operations  17.2 us (3%)
    ppermute x16, waiting for transfers between devices, seq_swap(): return lax.ppermute(value, 'seq', [(0, 1), (1, 0)])  76.9 us
    pallas_call x4, Pallas kernels, conv_backward(): pl.pallas_call(kernel, grid=(steps,), in_specs=[pl.BlockSpec((rows, LANES...  60 us
    pallas_call x2, Pallas kernels, conv_forward(): pl.pallas_call(conv_forward_kernel, grid=(steps,), in_specs=[pl.BlockSpec...  42.4 us
    ppermute x15, starting transfers between devices, outer_shift(): lax.ppermute(value, 'dp', [(spot, (spot - 4 * steps) % size) for spot in...  27 us
    ppermute x5, waiting for transfers between devices, middle_swap(): return lax.ppermute(value, 'dp', [(spot, spot ^ 2) for spot in range(size)])  24 us
    ppermute x16, starting transfers between devices, seq_swap(): return lax.ppermute(value, 'seq', [(0, 1), (1, 0)])  18.8 us
    all_gather x1, waiting for transfers between devices, body(): lax.all_gather(after(forward_shard, forwards[0][0]), 'dp', axis=0, tiled=...  18.2 us
    unnamed x175, local copies, waits for them, and re-layouts  14.2 us
  transfers between devices with their start and end apart: 49, of which 20 were waited for; matrix products, arithmetic and copies ran while one was open for 33% of the time, Pallas kernels for 19%

profile of v3, /device:TPU:0, one launch (start us, length us, event | category | flops | bytes accessed | tf_op | source)
XLA Modules:
  0.0 536.2 jit_solution(4149371781816179128)
XLA Ops:
  29.7 4.4 convolution_convert_fusion.1
  34.1 21.2 %conv_forward.2 = (f32[256,1024]{1,0:T(8,128)}, f32[256,1024]{1,0:T(8,128)}, bf16[12800,128]{1,0:T(8,128)(2,1)}, bf16[128,12800]{1,0:T(8,128)(2,1)}) custom-call(bf16[50,256,128]{2,1,0:T(8,128)(2,1)} %bitcast.338, s32[256,1]{1,0:T(8,128)} %copy.234.lens_ref, bf16[128,1024]{1,0:T(8,128)(2,1)} %copy.235.weight_ref.refs_3_), custom_call_target="tpu_custom_call" | custom-call | flops 3355443200 | bytes 65536000 | tf_op jit(solution)/shard_map/conv_forward/pallas_call | solution.py:239
  56.8 4.4 convolution_convert_fusion
  62.0 21.2 %conv_forward.3 = (f32[256,1024]{1,0:T(8,128)}, f32[256,1024]{1,0:T(8,128)}, bf16[12800,128]{1,0:T(8,128)(2,1)}, bf16[128,12800]{1,0:T(8,128)(2,1)}) custom-call(bf16[50,256,128]{2,1,0:T(8,128)(2,1)} %bitcast.337, s32[256,1]{1,0:T(8,128)} %slice.543.lens_ref, bf16[128,1024]{1,0:T(8,128)(2,1)} %copy.235.weight_ref.refs_3_), custom_call_target="tpu_custom_call" | custom-call | flops 3355443200 | bytes 65536000 | tf_op jit(solution)/shard_map/conv_forward/pallas_call | solution.py:239
  93.7 16.8 %collective-permute-done.2 = bf16[256,1024]{1,0:T(8,128)(2,1)S(1)} collective-permute-done((bf16[256,1024]{1,0:T(8,128)(2,1)S(1)}, bf16[256,1024]{1,0:T(8,128)(2,1)S(1)}, u32[]{:S(2)}, u32[]{:S(2)}) %collective-permute-start.2) | collective-permute-done | bytes 524320 | tf_op jit(solution)/shard_map/ppermute | solution.py:50
  112.3 11.6 %collective-permute-done.8 = bf16[4,48,3072]{2,1,0:T(8,128)(2,1)} collective-permute-done((bf16[4,48,3072]{2,1,0:T(8,128)(2,1)S(1)}, bf16[4,48,3072]{2,1,0:T(8,128)(2,1)}, u32[]{:S(2)}, u32[]{:S(2)}) %collective-permute-start.8) | collective-permute-done | bytes 1179680 | tf_op jit(solution)/shard_map/ppermute | solution.py:41
  132.8 5.0 fusion.15
  139.5 4.2 fusion.41
  149.0 7.1 %collective-permute-done.4 = bf16[256,768]{1,0:T(8,128)(2,1)S(1)} collective-permute-done((bf16[256,768]{1,0:T(8,128)(2,1)S(1)}, bf16[256,768]{1,0:T(8,128)(2,1)S(1)}, u32[]{:S(2)}, u32[]{:S(2)}) %collective-permute-start.4) | collective-permute-done | bytes 393248 | tf_op jit(solution)/shard_map/ppermute | solution.py:50
  164.7 8.7 %collective-permute-done.12 = bf16[256,768]{1,0:T(8,128)(2,1)} collective-permute-done((bf16[256,768]{1,0:T(8,128)(2,1)S(1)}, bf16[256,768]{1,0:T(8,128)(2,1)}, u32[]{:S(2)}, u32[]{:S(2)}) %collective-permute-start.12) | collective-permute-done | bytes 393248 | tf_op jit(solution)/shard_map/ppermute | solution.py:50
  174.8 5.6 %collective-permute-done.11 = bf16[256,768]{1,0:T(8,128)(2,1)} collective-permute-done((bf16[256,768]{1,0:T(8,128)(2,1)}, bf16[256,768]{1,0:T(8,128)(2,1)}, u32[]{:S(2)}, u32[]{:S(2)}) %collective-permute-start.11) | collective-permute-done | bytes 393248 | tf_op jit(solution)/shard_map/ppermute | solution.py:50
  182.7 6.1 %fusion.169 = (f32[12,256]{1,0:T(8,128)}, f32[12,256,512]{2,1,0:T(8,128)}) fusion(pred[512]{0:T(512)(128)(4,1)} %fusion.139, bf16[256,12,64]{0,2,1:T(8,128)(2,1)S(1)} %bitcast.301, bf16[512,12,64]{0,2,1:T(8,128)(2,1)S(1)} %bitcast.293), kind=kOutput, calls=%fused_computation.390 | convolution fusion | flops 207618560 | bytes 7483904 | tf_op jit(solution)/shard_map/sub | solution.py:485
  188.7 4.2 fusion.71
  195.2 18.2 %all-gather.5.cloned.1.call-done = bf16[768,6144]{1,0:T(8,128)(2,1)} async-done(((bf16[48,6144]{1,0:T(8,128)(2,1)}), bf16[768,6144]{1,0:T(8,128)(2,1)}) %all-gather.5.cloned.1.call-update) | async-done | bytes 9437200 | tf_op jit(solution)/shard_map/all_gather | solution.py:441
  213.4 10.2 %multiply_convert_fusion.1 = (bf16[256,3072]{1,0:T(8,128)(2,1)S(1)}, f32[256,3072]{1,0:T(8,128)S(1)}, f32[256,3072]{1,0:T(8,128)S(1)}) fusion(bf16[768,6144]{1,0:T(8,128)(2,1)} %all-gather.5.cloned.1.call-done, f32[256,768]{1,0:T(8,128)S(1)} %get-tuple-element.297, f32[768]{0:T(1024)S(1)} %convert_element_type.362, f32[768]{0:T(1024)S(1)} %convert_element_type.361, ...), kind=kOutput, calls=%fused_computation.44 | convolution fusion | flops 1260060672 | bytes 13377536 | tf_op jit(solution)/shard_map/dot_general | solution.py:499
  249.2 4.6 fusion.56
  263.5 5.7 %collective-permute-done.14 = bf16[256,768]{0,1:T(8,128)(2,1)S(1)} collective-permute-done((bf16[256,768]{0,1:T(8,128)(2,1)S(1)}, bf16[256,768]{0,1:T(8,128)(2,1)S(1)}, u32[]{:S(2)}, u32[]{:S(2)}) %collective-permute-start.14) | collective-permute-done | bytes 393248 | tf_op jit(solution)/shard_map/ppermute | solution.py:50
  269.4 7.5 %collective-permute-done.13 = bf16[256,768]{0,1:T(8,128)(2,1)S(1)} collective-permute-done((bf16[256,768]{0,1:T(8,128)(2,1)S(1)}, bf16[256,768]{0,1:T(8,128)(2,1)S(1)}, u32[]{:S(2)}, u32[]{:S(2)}) %collective-permute-start.13) | collective-permute-done | bytes 393248 | tf_op jit(solution)/shard_map/ppermute | solution.py:50
  290.1 9.1 %collective-permute-done.15 = bf16[256,768]{1,0:T(8,128)(2,1)S(1)} collective-permute-done((bf16[256,768]{1,0:T(8,128)(2,1)S(1)}, bf16[256,768]{1,0:T(8,128)(2,1)S(1)}, u32[]{:S(2)}, u32[]{:S(2)}) %collective-permute-start.15) | collective-permute-done | bytes 393248 | tf_op jit(solution)/shard_map/ppermute | solution.py:50
  299.3 5.8 %convert_add_fusion.1 = f32[4,2,48,3072]{3,2,1,0:T(8,128)} fusion(bf16[4,2,48,3072]{3,2,1,0:T(8,128)(2,1)} %collective-permute-done.16, bf16[4,2,2,48,3072]{4,3,2,1,0:T(8,128)(2,1)} %bitcast.278, s32[]{:T(128)S(6)} %select_n.632), kind=kLoop, calls=%fused_computation.25 | loop fusion | flops 3538944 | bytes 9437188 | tf_op jit(solution)/shard_map/add | solution.py:96
  313.6 6.4 %convert_reduce_fusion = (f32[1024]{0:T(1024)S(1)}, bf16[512,1024]{1,0:T(8,128)(2,1)S(1)}, f32[1024]{0:T(1024)S(1)}, bf16[512,1024]{1,0:T(8,128)(2,1)S(1)}, f32[512,1024]{1,0:T(8,128)}) fusion(f32[512,1024]{1,0:T(8,128)} %get-tuple-element.293, f32[256,1024]{1,0:T(8,128)S(1)} %copy-done.31, f32[256,1024]{1,0:T(8,128)} %get-tuple-element.291, ...), kind=kOutput, calls=%fused_computation.87 | convolution fusion | flops 815265792 | bytes 12857344 | tf_op jit(solution)/shard_map/td,fd->tf/dot_general | solution.py:573
  339.3 3.9 multiply_add_fusion
  346.6 10.8 %collective-permute-done.20 = bf16[256,1024]{1,0:T(8,128)(2,1)} collective-permute-done((bf16[256,1024]{1,0:T(8,128)(2,1)S(1)}, bf16[256,1024]{1,0:T(8,128)(2,1)}, u32[]{:S(2)}, u32[]{:S(2)}) %collective-permute-start.20) | collective-permute-done | bytes 524320 | tf_op jit(solution)/shard_map/ppermute | solution.py:50
  377.3 15.1 %conv_backward.4 = (f32[128,1024]{1,0:T(8,128)}, f32[272,128]{1,0:T(8,128)}) custom-call(bf16[12800,128]{1,0:T(8,128)(2,1)} %get-tuple-element.65.refs_0_, bf16[128,12800]{1,0:T(8,128)(2,1)} %get-tuple-element.66.refs_1_, s32[4,1,3200]{2,1,0:T(1,128)} %reshape.517.refs_2_, bf16[128,1024]{1,0:T(8,128)(2,1)} %copy.235.weight_ref.refs_3_, ...), custom_call_target="tpu_custom_call" | custom-call | flops 5033164800 | bytes 52428800 | tf_op jit(solution)/shard_map/conv_backward/pallas_call | solution.py:280
  392.3 3.8 collective-permute-done.22
  397.4 9.6 %collective-permute-done.24 = bf16[4,128,1408]{2,1,0:T(8,128)(2,1)} collective-permute-done((bf16[4,128,1408]{2,1,0:T(8,128)(2,1)S(1)}, bf16[4,128,1408]{2,1,0:T(8,128)(2,1)}, u32[]{:S(2)}, u32[]{:S(2)}) %collective-permute-start.24) | collective-permute-done | bytes 1441824 | tf_op jit(solution)/shard_map/ppermute | solution.py:41
  407.0 4.3 fusion.151
  411.2 14.9 %conv_backward.5 = (f32[128,1024]{1,0:T(8,128)}, f32[272,128]{1,0:T(8,128)}) custom-call(bf16[12800,128]{1,0:T(8,128)(2,1)} %get-tuple-element.65.refs_0_, bf16[128,12800]{1,0:T(8,128)(2,1)} %get-tuple-element.66.refs_1_, s32[4,1,3200]{2,1,0:T(1,128)} %reshape.517.refs_2_, bf16[128,1024]{1,0:T(8,128)(2,1)} %copy.235.weight_ref.refs_3_, ...), custom_call_target="tpu_custom_call" | custom-call | flops 5033164800 | bytes 52428800 | tf_op jit(solution)/shard_map/conv_backward/pallas_call | solution.py:280
  433.0 15.0 %conv_backward.6 = (f32[128,1024]{1,0:T(8,128)}, f32[272,128]{1,0:T(8,128)}) custom-call(bf16[12800,128]{1,0:T(8,128)(2,1)} %get-tuple-element.81.refs_0_, bf16[128,12800]{1,0:T(8,128)(2,1)} %get-tuple-element.82.refs_1_, s32[4,1,3200]{2,1,0:T(1,128)} %reshape.518.refs_2_, bf16[128,1024]{1,0:T(8,128)(2,1)} %copy.235.weight_ref.refs_3_, ...), custom_call_target="tpu_custom_call" | custom-call | flops 5033164800 | bytes 52428800 | tf_op jit(solution)/shard_map/conv_backward/pallas_call | solution.py:280
  450.7 14.9 %conv_backward.7 = (f32[128,1024]{1,0:T(8,128)}, f32[272,128]{1,0:T(8,128)}) custom-call(bf16[12800,128]{1,0:T(8,128)(2,1)} %get-tuple-element.81.refs_0_, bf16[128,12800]{1,0:T(8,128)(2,1)} %get-tuple-element.82.refs_1_, s32[4,1,3200]{2,1,0:T(1,128)} %reshape.518.refs_2_, bf16[128,1024]{1,0:T(8,128)(2,1)} %copy.235.weight_ref.refs_3_, ...), custom_call_target="tpu_custom_call" | custom-call | flops 5033164800 | bytes 52428800 | tf_op jit(solution)/shard_map/conv_backward/pallas_call | solution.py:280
  479.2 4.6 collective-permute-start.32
  496.7 4.1 collective-permute-start.41
  (530 shorter events, 230.0 us)
Async XLA Ops:
  7.2 121.6 %all-gather.3.cloned.1.call-start = ((), (), s32[]{:S(2)}) async-start(), calls=%async_computation.2 | async-start | bytes 10584064 | tf_op jit(solution)/shard_map/all_gather | solution.py:414
  11.6 201.7 %all-gather.5.cloned.1.call-start = ((), (), s32[]{:S(2)}) async-start(), calls=%async_computation.3 | async-start | bytes 10027008 | tf_op jit(solution)/shard_map/all_gather | solution.py:441
  11.7 76.5 %collective-permute-start.7 = (bf16[48,3072]{1,0:T(8,128)(2,1)S(1)}, bf16[48,3072]{1,0:T(8,128)(2,1)S(1)}, u32[]{:S(2)}, u32[]{:S(2)}) collective-permute-start(bf16[48,3072]{1,0:T(8,128)(2,1)S(1)} %constant_dynamic-update-slice_fusion.32), channel_id=1, source_target_pairs={{0,8},{2,10},{4,12},{6,14},{8,16},{10,18},{12,20},{14,22},{16,24},... | collective-permute-start | bytes 884744 | tf_op jit(solution)/shard_map/ppermute | solution.py:46
  14.4 73.8 %collective-permute-start.6 = (bf16[48,3072]{1,0:T(8,128)(2,1)S(1)}, bf16[48,3072]{1,0:T(8,128)(2,1)S(1)}, u32[]{:S(2)}, u32[]{:S(2)}) collective-permute-start(bf16[48,3072]{1,0:T(8,128)(2,1)S(1)} %constant_dynamic-update-slice_fusion.32), channel_id=1, source_target_pairs={{0,16},{2,18},{4,20},{6,22},{8,24},{10,26},{12,28},{14,30},{16,0},... | collective-permute-start | bytes 884744 | tf_op jit(solution)/shard_map/ppermute | solution.py:46
  17.0 71.2 %collective-permute-start.5 = (bf16[48,3072]{1,0:T(8,128)(2,1)S(1)}, bf16[48,3072]{1,0:T(8,128)(2,1)S(1)}, u32[]{:S(2)}, u32[]{:S(2)}) collective-permute-start(bf16[48,3072]{1,0:T(8,128)(2,1)S(1)} %constant_dynamic-update-slice_fusion.32), channel_id=1, source_target_pairs={{0,24},{2,26},{4,28},{6,30},{8,0},{10,2},{12,4},{14,6},{16,8},{18,... | collective-permute-start | bytes 884744 | tf_op jit(solution)/shard_map/ppermute | solution.py:46
  18.5 37.5 %collective-permute-start = (s32[256,51]{1,0:T(8,128)S(1)}, s32[256,51]{1,0:T(8,128)S(1)}, u32[]{:S(2)}, u32[]{:S(2)}) collective-permute-start(s32[256,51]{1,0:T(8,128)S(1)} %copy.236), channel_id=1, source_target_pairs={{0,1},{1,0},{2,3},{3,2},{4,5},{5,4},{6,7},{7,6},{8,9},{9,8},{10,11... | collective-permute-start | bytes 156680 | tf_op jit(solution)/shard_map/ppermute | solution.py:50
  55.3 316.9 %reduce-scatter.3.cloned.1.call-start = ((), (), s32[]{:S(2)}) async-start(), calls=%async_computation.4 | async-start | bytes 10027008 | tf_op jit(solution)/shard_map/reduce_scatter | solution.py:527
  86.2 25.2 %collective-permute-start.1 = (bf16[256,1024]{1,0:T(8,128)(2,1)S(1)}, bf16[256,1024]{1,0:T(8,128)(2,1)S(1)}, u32[]{:S(2)}, u32[]{:S(2)}) collective-permute-start(bf16[256,1024]{1,0:T(8,128)(2,1)S(1)} %get-tuple-element.243), channel_id=1, source_target_pairs={{0,1},{1,0},{2,3},{3,2},{4,5},{5,4},{6,7},{7,6},{8,9},{9,8},{10,11... | collective-permute-start | bytes 1572872 | tf_op jit(solution)/shard_map/ppermute | solution.py:50
  86.6 23.9 %collective-permute-start.2 = (bf16[256,1024]{1,0:T(8,128)(2,1)S(1)}, bf16[256,1024]{1,0:T(8,128)(2,1)S(1)}, u32[]{:S(2)}, u32[]{:S(2)}) collective-permute-start(bf16[256,1024]{1,0:T(8,128)(2,1)S(1)} %get-tuple-element.290), channel_id=1, source_target_pairs={{0,1},{1,0},{2,3},{3,2},{4,5},{5,4},{6,7},{7,6},{8,9},{9,8},{10,11... | collective-permute-start | bytes 1572872 | tf_op jit(solution)/shard_map/ppermute | solution.py:50
  88.3 37.9 %collective-permute-start.9 = (bf16[4,48,3072]{2,1,0:T(8,128)(2,1)S(1)}, bf16[4,48,3072]{2,1,0:T(8,128)(2,1)S(1)}, u32[]{:S(2)}, u32[]{:S(2)}) collective-permute-start(bf16[4,48,3072]{2,1,0:T(8,128)(2,1)S(1)} %bitcast_dynamic-update-slice_fusion.8), channel_id=1, source_target_pairs={{0,2},{2,0},{4,6},{6,4},{8,10},{10,8},{12,14},{14,12},{16,18},{18,... | collective-permute-start | bytes 3538952 | tf_op jit(solution)/shard_map/ppermute | solution.py:36
  88.4 35.4 %collective-permute-start.8 = (bf16[4,48,3072]{2,1,0:T(8,128)(2,1)S(1)}, bf16[4,48,3072]{2,1,0:T(8,128)(2,1)}, u32[]{:S(2)}, u32[]{:S(2)}) collective-permute-start(bf16[4,48,3072]{2,1,0:T(8,128)(2,1)S(1)} %bitcast_dynamic-update-slice_fusion.8), channel_id=1, source_target_pairs={{0,4},{2,6},{4,0},{6,2},{8,12},{10,14},{12,8},{14,10},{16,20},{18,... | collective-permute-start | bytes 3538952 | tf_op jit(solution)/shard_map/ppermute | solution.py:41
  123.8 22.8 %collective-permute-start.10 = (bf16[4,48,3072]{2,1,0:T(8,128)(2,1)}, bf16[4,48,3072]{2,1,0:T(8,128)(2,1)}, u32[]{:S(2)}, u32[]{:S(2)}) collective-permute-start(bf16[4,48,3072]{2,1,0:T(8,128)(2,1)} %collective-permute-done.8), channel_id=1, source_target_pairs={{0,2},{2,0},{4,6},{6,4},{8,10},{10,8},{12,14},{14,12},{16,18},{18,... | collective-permute-start | bytes 3538952 | tf_op jit(solution)/shard_map/ppermute | solution.py:36
  161.3 12.2 %collective-permute-start.12 = (bf16[256,768]{1,0:T(8,128)(2,1)S(1)}, bf16[256,768]{1,0:T(8,128)(2,1)}, u32[]{:S(2)}, u32[]{:S(2)}) collective-permute-start(bf16[256,768]{1,0:T(8,128)(2,1)S(1)} %get-tuple-element.267), channel_id=1, source_target_pairs={{0,1},{1,0},{2,3},{3,2},{4,5},{5,4},{6,7},{7,6},{8,9},{9,8},{10,11... | collective-permute-start | bytes 1179656 | tf_op jit(solution)/shard_map/ppermute | solution.py:50
  163.0 17.4 %collective-permute-start.11 = (bf16[256,768]{1,0:T(8,128)(2,1)}, bf16[256,768]{1,0:T(8,128)(2,1)}, u32[]{:S(2)}, u32[]{:S(2)}) collective-permute-start(bf16[256,768]{1,0:T(8,128)(2,1)} %get-tuple-element.269), channel_id=1, source_target_pairs={{0,1},{1,0},{2,3},{3,2},{4,5},{5,4},{6,7},{7,6},{8,9},{9,8},{10,11... | collective-permute-start | bytes 1179656 | tf_op jit(solution)/shard_map/ppermute | solution.py:50
  243.7 226.9 %reduce-scatter.5.cloned.1.call-start = ((), (), s32[]{:S(2)}) async-start(), calls=%async_computation.5 | async-start | bytes 5292032 | tf_op jit(solution)/shard_map/reduce_scatter | solution.py:604
  262.4 14.6 %collective-permute-start.13 = (bf16[256,768]{0,1:T(8,128)(2,1)S(1)}, bf16[256,768]{0,1:T(8,128)(2,1)S(1)}, u32[]{:S(2)}, u32[]{:S(2)}) collective-permute-start(bf16[256,768]{0,1:T(8,128)(2,1)S(1)} %bitcast.320), channel_id=1, source_target_pairs={{0,1},{1,0},{2,3},{3,2},{4,5},{5,4},{6,7},{7,6},{8,9},{9,8},{10,11... | collective-permute-start | bytes 1179656 | tf_op jit(solution)/shard_map/ppermute | solution.py:50
  282.5 16.8 %collective-permute-start.16 = (bf16[4,2,48,3072]{3,2,1,0:T(8,128)(2,1)}, bf16[4,2,48,3072]{3,2,1,0:T(8,128)(2,1)}, u32[]{:S(2)}, u32[]{:S(2)}) collective-permute-start(bf16[4,2,48,3072]{3,2,1,0:T(8,128)(2,1)} %dynamic-slice_bitcast_fusion), channel_id=1, source_target_pairs={{0,2},{2,0},{4,6},{6,4},{8,10},{10,8},{12,14},{14,12},{16,18},{18,... | collective-permute-start | bytes 7077896 | tf_op jit(solution)/shard_map/ppermute | solution.py:36
  313.2 48.7 %collective-permute-start.18 = (bf16[4,48,3072]{2,1,0:T(8,128)(2,1)}, bf16[4,48,3072]{2,1,0:T(8,128)(2,1)}, u32[]{:S(2)}, u32[]{:S(2)}) collective-permute-start(bf16[4,48,3072]{2,1,0:T(8,128)(2,1)} %fusion.74), channel_id=1, source_target_pairs={{0,4},{2,6},{4,0},{6,2},{8,12},{10,14},{12,8},{14,10},{16,20},{18,... | collective-permute-start | bytes 3538952 | tf_op jit(solution)/shard_map/ppermute | solution.py:41
  325.3 39.9 %collective-permute-start.19 = (bf16[4,2,128,1408]{3,2,1,0:T(8,128)(2,1)}, bf16[4,2,128,1408]{3,2,1,0:T(8,128)(2,1)}, u32[]{:S(2)}, u32[]{:S(2)}) collective-permute-start(bf16[4,2,128,1408]{3,2,1,0:T(8,128)(2,1)} %fusion.37), channel_id=1, source_target_pairs={{0,2},{2,0},{4,6},{6,4},{8,10},{10,8},{12,14},{14,12},{16,18},{18,... | collective-permute-start | bytes 8650760 | tf_op jit(solution)/shard_map/ppermute | solution.py:36
  331.5 15.0 %collective-permute-start.17 = (bf16[256,1024]{1,0:T(8,128)(2,1)}, bf16[256,1024]{1,0:T(8,128)(2,1)}, u32[]{:S(2)}, u32[]{:S(2)}) collective-permute-start(bf16[256,1024]{1,0:T(8,128)(2,1)} %get-tuple-element.270), channel_id=1, source_target_pairs={{0,1},{1,0},{2,3},{3,2},{4,5},{5,4},{6,7},{7,6},{8,9},{9,8},{10,11... | collective-permute-start | bytes 1572872 | tf_op jit(solution)/shard_map/ppermute | solution.py:50
  333.0 24.4 %collective-permute-start.20 = (bf16[256,1024]{1,0:T(8,128)(2,1)S(1)}, bf16[256,1024]{1,0:T(8,128)(2,1)}, u32[]{:S(2)}, u32[]{:S(2)}) collective-permute-start(bf16[256,1024]{1,0:T(8,128)(2,1)S(1)} %get-tuple-element.271), channel_id=1, source_target_pairs={{0,1},{1,0},{2,3},{3,2},{4,5},{5,4},{6,7},{7,6},{8,9},{9,8},{10,11... | collective-permute-start | bytes 1572872 | tf_op jit(solution)/shard_map/ppermute | solution.py:50
  370.4 36.6 %collective-permute-start.24 = (bf16[4,128,1408]{2,1,0:T(8,128)(2,1)S(1)}, bf16[4,128,1408]{2,1,0:T(8,128)(2,1)}, u32[]{:S(2)}, u32[]{:S(2)}) collective-permute-start(bf16[4,128,1408]{2,1,0:T(8,128)(2,1)S(1)} %fusion.59), channel_id=1, source_target_pairs={{0,4},{2,6},{4,0},{6,2},{8,12},{10,14},{12,8},{14,10},{16,20},{18,... | collective-permute-start | bytes 4325384 | tf_op jit(solution)/shard_map/ppermute | solution.py:41
  373.0 19.3 %collective-permute-start.23 = (bf16[48,3072]{1,0:T(8,128)(2,1)}, bf16[48,3072]{1,0:T(8,128)(2,1)S(1)}, u32[]{:S(2)}, u32[]{:S(2)}) collective-permute-start(bf16[48,3072]{1,0:T(8,128)(2,1)} %get-tuple-element.264), channel_id=1, source_target_pairs={{0,8},{2,10},{4,12},{6,14},{8,16},{10,18},{12,20},{14,22},{16,24},... | collective-permute-start | bytes 884744 | tf_op jit(solution)/shard_map/ppermute | solution.py:46
  373.4 22.8 %collective-permute-start.22 = (bf16[48,3072]{1,0:T(8,128)(2,1)S(1)}, bf16[48,3072]{1,0:T(8,128)(2,1)S(1)}, u32[]{:S(2)}, u32[]{:S(2)}) collective-permute-start(bf16[48,3072]{1,0:T(8,128)(2,1)S(1)} %get-tuple-element.265), channel_id=1, source_target_pairs={{0,16},{2,18},{4,20},{6,22},{8,24},{10,26},{12,28},{14,30},{16,0},... | collective-permute-start | bytes 884744 | tf_op jit(solution)/shard_map/ppermute | solution.py:46
  374.7 21.4 %collective-permute-start.21 = (bf16[48,3072]{1,0:T(8,128)(2,1)S(1)}, bf16[48,3072]{1,0:T(8,128)(2,1)S(1)}, u32[]{:S(2)}, u32[]{:S(2)}) collective-permute-start(bf16[48,3072]{1,0:T(8,128)(2,1)S(1)} %get-tuple-element.266), channel_id=1, source_target_pairs={{0,24},{2,26},{4,28},{6,30},{8,0},{10,2},{12,4},{14,6},{16,8},{18,... | collective-permute-start | bytes 884744 | tf_op jit(solution)/shard_map/ppermute | solution.py:46
  426.1 21.9 %collective-permute-start.29 = (bf16[48,3072]{1,0:T(8,128)(2,1)S(1)}, bf16[48,3072]{1,0:T(8,128)(2,1)}, u32[]{:S(2)}, u32[]{:S(2)}) collective-permute-start(bf16[48,3072]{1,0:T(8,128)(2,1)S(1)} %get-tuple-element.97), channel_id=1, source_target_pairs={{0,1},{1,0},{2,3},{3,2},{4,5},{5,4},{6,7},{7,6},{8,9},{9,8},{10,11... | collective-permute-start | bytes 884744 | tf_op jit(solution)/shard_map/ppermute | solution.py:50
  428.6 37.1 %collective-permute-start.28 = (bf16[128,1408]{1,0:T(8,128)(2,1)}, bf16[128,1408]{1,0:T(8,128)(2,1)}, u32[]{:S(2)}, u32[]{:S(2)}) collective-permute-start(bf16[128,1408]{1,0:T(8,128)(2,1)} %get-tuple-element.251), channel_id=1, source_target_pairs={{0,8},{2,10},{4,12},{6,14},{8,16},{10,18},{12,20},{14,22},{16,24},... | collective-permute-start | bytes 1081352 | tf_op jit(solution)/shard_map/ppermute | solution.py:46
  428.6 37.1 %collective-permute-start.27 = (bf16[128,1408]{1,0:T(8,128)(2,1)}, bf16[128,1408]{1,0:T(8,128)(2,1)}, u32[]{:S(2)}, u32[]{:S(2)}) collective-permute-start(bf16[128,1408]{1,0:T(8,128)(2,1)} %get-tuple-element.252), channel_id=1, source_target_pairs={{0,16},{2,18},{4,20},{6,22},{8,24},{10,26},{12,28},{14,30},{16,0},... | collective-permute-start | bytes 1081352 | tf_op jit(solution)/shard_map/ppermute | solution.py:46
  428.7 36.9 %collective-permute-start.26 = (bf16[128,1408]{1,0:T(8,128)(2,1)}, bf16[128,1408]{1,0:T(8,128)(2,1)}, u32[]{:S(2)}, u32[]{:S(2)}) collective-permute-start(bf16[128,1408]{1,0:T(8,128)(2,1)} %get-tuple-element.253), channel_id=1, source_target_pairs={{0,24},{2,26},{4,28},{6,30},{8,0},{10,2},{12,4},{14,6},{16,8},{18,... | collective-permute-start | bytes 1081352 | tf_op jit(solution)/shard_map/ppermute | solution.py:46
  432.4 18.1 %collective-permute-start.25 = (bf16[48,6144]{1,0:T(8,128)(2,1)S(1)}, bf16[48,6144]{1,0:T(8,128)(2,1)S(1)}, u32[]{:S(2)}, u32[]{:S(2)}) collective-permute-start(bf16[48,6144]{1,0:T(8,128)(2,1)S(1)} %copy-done.39), channel_id=1, source_target_pairs={{0,1},{1,0},{2,3},{3,2},{4,5},{5,4},{6,7},{7,6},{8,9},{9,8},{10,11... | collective-permute-start | bytes 1769480 | tf_op jit(solution)/shard_map/ppermute | solution.py:50
  476.4 20.2 %collective-permute-start.38 = (bf16[128,2816]{1,0:T(8,128)(2,1)}, bf16[128,2816]{1,0:T(8,128)(2,1)}, u32[]{:S(2)}, u32[]{:S(2)}) collective-permute-start(bf16[128,2816]{1,0:T(8,128)(2,1)} %maximum_maximum_fusion), channel_id=1, source_target_pairs={{0,1},{1,0},{2,3},{3,2},{4,5},{5,4},{6,7},{7,6},{8,9},{9,8},{10,11... | collective-permute-start | bytes 2162696 | tf_op jit(solution)/shard_map/ppermute | solution.py:50
  479.2 12.6 %collective-permute-start.32 = (bf16[8,1024]{1,0:T(8,128)(2,1)}, bf16[8,1024]{1,0:T(8,128)(2,1)}, u32[]{:S(2)}, u32[]{:S(2)}) collective-permute-start(bf16[8,1024]{1,0:T(8,128)(2,1)} %get-tuple-element.283), channel_id=1, source_target_pairs={{0,24},{2,26},{4,28},{6,30},{8,0},{10,2},{12,4},{14,6},{16,8},{18,... | collective-permute-start | bytes 49160 | tf_op jit(solution)/shard_map/ppermute | solution.py:46
  (100 other events, 899.6 us)
Sparse Core Ops, SparseCore 0:
  11.7 117.0 all-gather.2
  131.7 81.6 all-gather.4
  243.8 120.9 reduce-scatter.2
  372.3 95.2 reduce-scatter.4

commit v4 on v3

--- a/solution.py
+++ b/solution.py
@@ -408,23 +408,20 @@
     code_rows = jnp.concatenate([character_codes[0], word_lengths[0][:, None]], axis=1)
     code_rows = [code_rows, seq_swap(code_rows)]
 
-    joint_shard = jnp.concatenate(
-        [highway_shard.reshape(piece, filters), projection_shard.reshape(piece, model // 2)], axis=1
-    )
-    joint_all = lax.all_gather(joint_shard, "dp", axis=0, tiled=True)
-    highway_parts = [joint_all[:, :mine], joint_all[:, mine:filters]]
-    projection_full = joint_all[:, filters:].reshape(mine, model)
-    attention_near = gather_near(outer_pieces(jnp.concatenate([attention_in, attention_out], axis=1)))
-    attention_across = middle_swap(attention_near)
-    attention_far = [core_swap(attention_near), core_swap(attention_across)]
-    attention_all = gather((attention_near, attention_across, *attention_far)).reshape(model, -1)
-    attention_full = attention_all[:, : 3 * model]
-    output_full = attention_all[:, 3 * model :]
-
+    highway_all = lax.all_gather(highway_shard.reshape(piece, filters), "dp", axis=0, tiled=True)
+    highway_parts = [highway_all[:, :mine], highway_all[:, mine:]]
+    projection_near = gather_near(outer_pieces(projection_shard))
+    projection_across = middle_swap(projection_near)
+    projection_far = [core_swap(projection_near), core_swap(projection_across)]
+    projection_full = gather((projection_near, projection_across, *projection_far)).reshape(mine, model)
+    attention_near = gather_near(
+        outer_pieces(after(jnp.concatenate([attention_in, attention_out], axis=1), projection_near))
+    )
     def cut(grad, slots=False):
         lead = (2, size // 4, 2) if slots else (size // 4, 2, 2)
         return grad.reshape(lead + (grad.shape[0] // size,) + grad.shape[1:])
 
+    code_rows[1] = after(code_rows[1], projection_near)
     codes = [rows[:, :letters] for rows in code_rows]
     conv_weight = own_blocks(merged_weight(kernels), 1)
     conv_shift = own_blocks(conv_bias, 0).astype(f32)
@@ -461,6 +458,11 @@
     ]
     hidden1 = highway_mix(transform, gate, hidden0)
     hidden1_low = hidden1.astype(low)
+    attention_across = after(middle_swap(attention_near), hidden1_low)
+    attention_far = [core_swap(attention_near), core_swap(attention_across)]
+    attention_all = gather((attention_near, attention_across, *attention_far)).reshape(model, -1)
+    attention_full = attention_all[:, : 3 * model]
+    output_full = attention_all[:, 3 * model :]
     mapped = jnp.dot(hidden1_low, projection_full, preferred_element_type=f32)
     offset = side * words
     positions = lax.dynamic_slice_in_dim(position_table, offset, words, 0).astype(f32)
@@ -581,15 +583,20 @@
     grad_held, grad_lent = halves_of(grad_spread, piece)
     grad_lent = grad_lent.astype(low)
     lent_back = [seq_swap(grad_lent[words:]), seq_swap(grad_lent[:words])]
+    highway_grads = [
+        jnp.einsum("tf,tg->fg", hidden0_all, grad_gates[part], preferred_element_type=f32).astype(low)
+        for part in range(2)
+    ]
+    joint_half = scatter_core(
+        cut(jnp.concatenate([highway_grads[1], projection_grad.reshape(filters, model // 2)], axis=1))
+    )
+    attention_quarter = scatter_middle(attention_half)
+    lent_back[1] = after(lent_back[1], joint_half, attention_quarter)
     grad_near = grad_carry + grad_held
     grad_pooled = [
         jnp.where(
             biased[part] > 0, grad_near[part * words : (part + 1) * words] + lent_back[part].astype(f32), 0.0
         )
-        for part in range(2)
-    ]
-    highway_grads = [
-        jnp.einsum("tf,tg->fg", hidden0_all, grad_gates[part], preferred_element_type=f32).astype(low)
         for part in range(2)
     ]
     highway_bias_grad = jnp.concatenate([jnp.sum(grad.astype(f32), axis=0) for grad in grad_gates])
@@ -604,10 +611,6 @@
     highway_sum = lax.psum_scatter(
         after(highway_rows, forward_sum), "dp", scatter_dimension=0, tiled=True
     )
-    joint_half = scatter_core(
-        cut(jnp.concatenate([highway_grads[1], projection_grad.reshape(filters, model // 2)], axis=1))
-    )
-    attention_quarter = scatter_middle(attention_half)
     turned = conv_weight.T
     shares = [grad_pooled[part] / forwards[part][1] for part in range(2)]
     code_blocks = [
@@ -633,7 +636,7 @@
     cuts = steps // 2
     backs = [back(0, 0, cuts, attention_quarter, joint_half, highway_rows)]
     attention_sum = scatter_outer(attention_quarter, grad_pooled, backs[0])
-    joint_quarter = scatter_middle(joint_half, grad_pooled, backs[0])
+    joint_quarter = scatter_middle(joint_half, (), backs[0])
     backs.append(back(0, cuts, steps - cuts, attention_sum, joint_quarter, *backs[0]))
     forward_both = forward_sum.astype(f32) + after(seq_swap(after(forward_sum, *backs[0])), *backs[1]).astype(f32)
     backs.append(back(1, 0, cuts, forward_sum, *backs[1]))

time: 544 us -> 536 us (0.985)
  waiting for transfers between devices: 128 us -> 94.9 us
  starting transfers between devices: 54.5 us -> 71 us
  matrix products: 95 us -> 103 us
    ppermute x5 -> x6, waiting for transfers between devices: 24 us -> 4.23 us  [middle_swap(): return lax.ppermute(value, 'dp', [(spot, spot ^ 2) for spot in range(size)])]
    ppermute x15 -> x18, starting transfers between devices: 27 us -> 45.5 us  [outer_shift(): lax.ppermute(value, 'dp', [(spot, (spot - 4 * steps) % size) for spot in...]
    ppermute x15 -> x18, waiting for transfers between devices: 4.88 us -> 19.9 us  [outer_shift(): lax.ppermute(value, 'dp', [(spot, (spot - 4 * steps) % size) for spot in...]
    all_gather x1, waiting for transfers between devices: 18.2 us -> 3.24 us  [body(): lax.all_gather(after(forward_shard, forwards[0][0]), 'dp', axis=0, tiled=...]
    ppermute x16, waiting for transfers between devices: 76.9 us -> 65.3 us  [seq_swap(): return lax.ppermute(value, 'seq', [(0, 1), (1, 0)])]
    unnamed x175 -> x188, local copies, waits for them, and re-layouts: 14.2 us -> 13.2 us
  transfers between devices with their start and end apart: 49 -> 55, of which waited for: 20 -> 20; matrix products, arithmetic and copies ran while one was open for 33% -> 35% of each run, Pallas kernels for 19% -> 20%
where the time goes in v4:
time: 536 us; the launch traced here: 528 us
  Pallas kernels  104 us (19%)
  matrix products  103 us (19%)
  waiting for transfers between devices  94.9 us (18%)
  local copies, waits for them, and re-layouts  72.1 us (13%)
  starting transfers between devices  71 us (13%)
  other arithmetic  65.3 us (12%)
  between operations  16.9 us (3%)
    ppermute x16, waiting for transfers between devices, seq_swap(): return lax.ppermute(value, 'seq', [(0, 1), (1, 0)])  65.3 us
    pallas_call x4, Pallas kernels, conv_backward(): pl.pallas_call(kernel, grid=(steps,), in_specs=[pl.BlockSpec((rows, LANES...  60.1 us
    ppermute x18, starting transfers between devices, outer_shift(): lax.ppermute(value, 'dp', [(spot, (spot - 4 * steps) % size) for spot in...  45.5 us
    pallas_call x2, Pallas kernels, conv_forward(): pl.pallas_call(conv_forward_kernel, grid=(steps,), in_specs=[pl.BlockSpec...  42.3 us
    ppermute x18, waiting for transfers between devices, outer_shift(): lax.ppermute(value, 'dp', [(spot, (spot - 4 * steps) % size) for spot in...  19.9 us
    ppermute x16, starting transfers between devices, seq_swap(): return lax.ppermute(value, 'seq', [(0, 1), (1, 0)])  18.4 us
    unnamed x188, local copies, waits for them, and re-layouts  13.2 us
    dot_general x2, matrix products, body(): jnp.dot(hidden0_all, highway_parts[part], preferred_element_type=f32)  13 us
  transfers between devices with their start and end apart: 55, of which 20 were waited for; matrix products, arithmetic and copies ran while one was open for 35% of the time, Pallas kernels for 20%

profile of v4, /device:TPU:0, one launch (start us, length us, event | category | flops | bytes accessed | tf_op | source)
XLA Modules:
  0.0 527.7 jit_solution(14476749293451889764)
XLA Ops:
  21.8 4.4 convolution_convert_fusion.1
  26.2 21.2 %conv_forward.2 = (f32[256,1024]{1,0:T(8,128)}, f32[256,1024]{1,0:T(8,128)}, bf16[12800,128]{1,0:T(8,128)(2,1)}, bf16[128,12800]{1,0:T(8,128)(2,1)}) custom-call(bf16[50,256,128]{2,1,0:T(8,128)(2,1)} %bitcast.369, s32[256,1]{1,0:T(8,128)} %copy.240.lens_ref, bf16[128,1024]{1,0:T(8,128)(2,1)} %copy.241.weight_ref.refs_3_), custom_call_target="tpu_custom_call" | custom-call | flops 3355443200 | bytes 65536000 | tf_op jit(solution)/shard_map/conv_forward/pallas_call | solution.py:239
  53.0 4.1 collective-permute-done.2
  57.2 13.4 %collective-permute-done.3 = bf16[64,768]{1,0:T(8,128)(2,1)S(1)} collective-permute-done((bf16[64,768]{1,0:T(8,128)(2,1)S(1)}, bf16[64,768]{1,0:T(8,128)(2,1)S(1)}, u32[]{:S(2)}, u32[]{:S(2)}) %collective-permute-start.3) | collective-permute-done | bytes 98336 | tf_op jit(solution)/shard_map/ppermute | solution.py:46
  72.1 5.5 %collective-permute-start.12 = (bf16[48,3072]{1,0:T(8,128)(2,1)S(1)}, bf16[48,3072]{1,0:T(8,128)(2,1)}, u32[]{:S(2)}, u32[]{:S(2)}) collective-permute-start(bf16[48,3072]{1,0:T(8,128)(2,1)S(1)} %pad_maximum_fusion.14), channel_id=1, source_target_pairs={{0,16},{2,18},{4,20},{6,22},{8,24},{10,26},{12,28},{14,30},{16,0},... | collective-permute-start | bytes 884744 | tf_op jit(solution)/shard_map/ppermute | solution.py:46
  82.9 4.4 convolution_convert_fusion
  87.3 21.2 %conv_forward.3 = (f32[256,1024]{1,0:T(8,128)}, f32[256,1024]{1,0:T(8,128)}, bf16[12800,128]{1,0:T(8,128)(2,1)}, bf16[128,12800]{1,0:T(8,128)(2,1)}) custom-call(bf16[50,256,128]{2,1,0:T(8,128)(2,1)} %bitcast.368, s32[256,1]{1,0:T(8,128)} %slice.408.lens_ref, bf16[128,1024]{1,0:T(8,128)(2,1)} %copy.241.weight_ref.refs_3_), custom_call_target="tpu_custom_call" | custom-call | flops 3355443200 | bytes 65536000 | tf_op jit(solution)/shard_map/conv_forward/pallas_call | solution.py:239
  120.8 16.2 %collective-permute-done.6 = bf16[256,1024]{1,0:T(8,128)(2,1)S(1)} collective-permute-done((bf16[256,1024]{1,0:T(8,128)(2,1)S(1)}, bf16[256,1024]{1,0:T(8,128)(2,1)S(1)}, u32[]{:S(2)}, u32[]{:S(2)}) %collective-permute-start.6) | collective-permute-done | bytes 524320 | tf_op jit(solution)/shard_map/ppermute | solution.py:50
  140.0 5.8 %fusion.15 = f32[512,1024]{1,0:T(8,128)S(1)} fusion(bf16[2048,2048]{0,1:T(8,128)(2,1)} %all-gather.3.cloned.1.call-done, bf16[256,2048]{1,0:T(8,128)(2,1)} %copy-done.62, bf16[256,2048]{1,0:T(8,128)(2,1)} %copy-done.65), kind=kOutput, calls=%fused_computation.35 | convolution fusion | flops 2151677952 | bytes 8388608 | tf_op jit(solution)/shard_map/dot_general | solution.py:456
  145.9 7.2 %fusion.41 = (bf16[512,1024]{1,0:T(8,128)(2,1)S(1)}, f32[512,1024]{1,0:T(8,128)}) fusion(f32[512,1024]{1,0:T(8,128)S(1)} %fusion.15, f32[256,1024]{1,0:T(8,128)S(1)} %copy-done.30, f32[256,1024]{1,0:T(8,128)S(1)} %copy-done.32, f32[1024]{0:T(1024)S(1)} %bitcast.363, f32[1024]{0:T(1024)S(1)} %bitcast.365, ...), kind=kOutput, calls=%fused_computation.79 | convolution fusion | flops 2157969408 | bytes 13639680 | tf_op jit(solution)/shard_map/dot_general | solution.py:456
  157.9 9.4 %collective-permute-done.10 = bf16[256,768]{1,0:T(8,128)(2,1)S(1)} collective-permute-done((bf16[256,768]{1,0:T(8,128)(2,1)S(1)}, bf16[256,768]{1,0:T(8,128)(2,1)S(1)}, u32[]{:S(2)}, u32[]{:S(2)}) %collective-permute-start.10) | collective-permute-done | bytes 393248 | tf_op jit(solution)/shard_map/ppermute | solution.py:50
  174.1 8.6 %collective-permute-done.18 = bf16[256,768]{1,0:T(8,128)(2,1)S(1)} collective-permute-done((bf16[256,768]{1,0:T(8,128)(2,1)S(1)}, bf16[256,768]{1,0:T(8,128)(2,1)S(1)}, u32[]{:S(2)}, u32[]{:S(2)}) %collective-permute-start.18) | collective-permute-done | bytes 393248 | tf_op jit(solution)/shard_map/ppermute | solution.py:50
  183.0 6.6 %collective-permute-done.17 = bf16[256,768]{1,0:T(8,128)(2,1)} collective-permute-done((bf16[256,768]{1,0:T(8,128)(2,1)}, bf16[256,768]{1,0:T(8,128)(2,1)}, u32[]{:S(2)}, u32[]{:S(2)}) %collective-permute-start.17) | collective-permute-done | bytes 393248 | tf_op jit(solution)/shard_map/ppermute | solution.py:50
  192.0 6.2 %fusion.169 = (f32[12,256]{1,0:T(8,128)}, f32[12,256,512]{2,1,0:T(8,128)}) fusion(pred[512]{0:T(512)(128)(4,1)} %fusion.139, bf16[256,12,64]{0,2,1:T(8,128)(2,1)S(1)} %bitcast.330, bf16[512,12,64]{0,2,1:T(8,128)(2,1)S(1)} %bitcast.320), kind=kOutput, calls=%fused_computation.396 | convolution fusion | flops 207618560 | bytes 7483904 | tf_op jit(solution)/shard_map/sub | solution.py:487
  207.9 9.7 %multiply_convert_fusion.1 = (bf16[256,3072]{1,0:T(8,128)(2,1)S(1)}, f32[256,3072]{1,0:T(8,128)S(1)}, f32[256,3072]{1,0:T(8,128)S(1)}) fusion(bf16[768,6144]{1,0:T(8,128)(2,1)} %all-gather.5.cloned.1.call-done, f32[256,768]{1,0:T(8,128)S(1)} %get-tuple-element.305, f32[768]{0:T(1024)S(1)} %convert_element_type.362, f32[768]{0:T(1024)S(1)} %convert_element_type.361, ...), kind=kOutput, calls=%fused_computation.44 | convolution fusion | flops 1260060672 | bytes 13377536 | tf_op jit(solution)/shard_map/dot_general | solution.py:501
  243.3 4.2 fusion.56
  257.4 5.7 %collective-permute-done.20 = bf16[256,768]{0,1:T(8,128)(2,1)S(1)} collective-permute-done((bf16[256,768]{0,1:T(8,128)(2,1)S(1)}, bf16[256,768]{0,1:T(8,128)(2,1)S(1)}, u32[]{:S(2)}, u32[]{:S(2)}) %collective-permute-start.20) | collective-permute-done | bytes 393248 | tf_op jit(solution)/shard_map/ppermute | solution.py:50
  263.2 7.7 %collective-permute-done.19 = bf16[256,768]{0,1:T(8,128)(2,1)S(1)} collective-permute-done((bf16[256,768]{0,1:T(8,128)(2,1)S(1)}, bf16[256,768]{0,1:T(8,128)(2,1)S(1)}, u32[]{:S(2)}, u32[]{:S(2)}) %collective-permute-start.19) | collective-permute-done | bytes 393248 | tf_op jit(solution)/shard_map/ppermute | solution.py:50
  284.3 8.9 %collective-permute-done.21 = bf16[256,768]{1,0:T(8,128)(2,1)S(1)} collective-permute-done((bf16[256,768]{1,0:T(8,128)(2,1)S(1)}, bf16[256,768]{1,0:T(8,128)(2,1)S(1)}, u32[]{:S(2)}, u32[]{:S(2)}) %collective-permute-start.21) | collective-permute-done | bytes 393248 | tf_op jit(solution)/shard_map/ppermute | solution.py:50
  293.3 5.8 %convert_add_fusion.1 = f32[4,2,48,3072]{3,2,1,0:T(8,128)} fusion(bf16[4,2,48,3072]{3,2,1,0:T(8,128)(2,1)} %collective-permute-done.22, bf16[4,2,2,48,3072]{4,3,2,1,0:T(8,128)(2,1)} %bitcast.301, s32[]{:T(128)S(6)} %select_n.658), kind=kLoop, calls=%fused_computation.25 | loop fusion | flops 3538944 | bytes 9437188 | tf_op jit(solution)/shard_map/add | solution.py:96
  304.0 7.1 %convert_reduce_fusion = (f32[1024]{0:T(1024)S(1)}, bf16[512,1024]{1,0:T(8,128)(2,1)}, f32[1024]{0:T(1024)S(1)}, bf16[512,1024]{1,0:T(8,128)(2,1)}, f32[512,1024]{1,0:T(8,128)}) fusion(f32[512,1024]{1,0:T(8,128)} %get-tuple-element.301, f32[256,1024]{1,0:T(8,128)S(1)} %copy-done.31, f32[256,1024]{1,0:T(8,128)} %get-tuple-element.299, ...), kind=kOutput, calls=%fused_computation.87 | convolution fusion | flops 815265792 | bytes 12857344 | tf_op jit(solution)/shard_map/td,fd->tf/dot_general | solution.py:575
  314.1 4.4 convolution_convert_fusion.6
  319.7 4.9 fusion.13
  336.8 4.4 convolution_convert_fusion.5
  341.2 5.4 %pad_maximum_fusion = bf16[16,152,1024]{2,1,0:T(8,128)(2,1)} fusion(bf16[16,24,1024]{2,1,0:T(8,128)(2,1)S(1)} %reshape.489, bf16[16,128,1024]{2,1,0:T(8,128)(2,1)} %bitcast.318), kind=kLoop, calls=%fused_computation.21 | loop fusion | flops 9961472 | bytes 9961472 | tf_op jit(solution)/shard_map/concatenate | solution.py:608
  372.3 15.1 %conv_backward.4 = (f32[128,1024]{1,0:T(8,128)}, f32[272,128]{1,0:T(8,128)}) custom-call(bf16[12800,128]{1,0:T(8,128)(2,1)} %get-tuple-element.71.refs_0_, bf16[128,12800]{1,0:T(8,128)(2,1)} %get-tuple-element.72.refs_1_, s32[4,1,3200]{2,1,0:T(1,128)} %reshape.513.refs_2_, bf16[128,1024]{1,0:T(8,128)(2,1)} %copy.241.weight_ref.refs_3_, ...), custom_call_target="tpu_custom_call" | custom-call | flops 5033164800 | bytes 52428800 | tf_op jit(solution)/shard_map/conv_backward/pallas_call | solution.py:280
  391.0 4.2 fusion.151
  395.2 14.9 %conv_backward.5 = (f32[128,1024]{1,0:T(8,128)}, f32[272,128]{1,0:T(8,128)}) custom-call(bf16[12800,128]{1,0:T(8,128)(2,1)} %get-tuple-element.71.refs_0_, bf16[128,12800]{1,0:T(8,128)(2,1)} %get-tuple-element.72.refs_1_, s32[4,1,3200]{2,1,0:T(1,128)} %reshape.513.refs_2_, bf16[128,1024]{1,0:T(8,128)(2,1)} %copy.241.weight_ref.refs_3_, ...), custom_call_target="tpu_custom_call" | custom-call | flops 5033164800 | bytes 52428800 | tf_op jit(solution)/shard_map/conv_backward/pallas_call | solution.py:280
  412.7 6.5 %collective-permute-start.34 = (bf16[128,1408]{1,0:T(8,128)(2,1)}, bf16[128,1408]{1,0:T(8,128)(2,1)}, u32[]{:S(2)}, u32[]{:S(2)}) collective-permute-start(bf16[128,1408]{1,0:T(8,128)(2,1)} %get-tuple-element.259), channel_id=1, source_target_pairs={{0,8},{2,10},{4,12},{6,14},{8,16},{10,18},{12,20},{14,22},{16,24},... | collective-permute-start | bytes 1081352 | tf_op jit(solution)/shard_map/ppermute | solution.py:46
  422.1 15.2 %conv_backward.6 = (f32[128,1024]{1,0:T(8,128)}, f32[272,128]{1,0:T(8,128)}) custom-call(bf16[12800,128]{1,0:T(8,128)(2,1)} %get-tuple-element.87.refs_0_, bf16[128,12800]{1,0:T(8,128)(2,1)} %get-tuple-element.88.refs_1_, s32[4,1,3200]{2,1,0:T(1,128)} %reshape.514.refs_2_, bf16[128,1024]{1,0:T(8,128)(2,1)} %copy.241.weight_ref.refs_3_, ...), custom_call_target="tpu_custom_call" | custom-call | flops 5033164800 | bytes 52428800 | tf_op jit(solution)/shard_map/conv_backward/pallas_call | solution.py:280
  440.0 14.9 %conv_backward.7 = (f32[128,1024]{1,0:T(8,128)}, f32[272,128]{1,0:T(8,128)}) custom-call(bf16[12800,128]{1,0:T(8,128)(2,1)} %get-tuple-element.87.refs_0_, bf16[128,12800]{1,0:T(8,128)(2,1)} %get-tuple-element.88.refs_1_, s32[4,1,3200]{2,1,0:T(1,128)} %reshape.514.refs_2_, bf16[128,1024]{1,0:T(8,128)(2,1)} %copy.241.weight_ref.refs_3_, ...), custom_call_target="tpu_custom_call" | custom-call | flops 5033164800 | bytes 52428800 | tf_op jit(solution)/shard_map/conv_backward/pallas_call | solution.py:280
  467.8 9.6 %collective-permute-start.38 = (bf16[8,1024]{1,0:T(8,128)(2,1)}, bf16[8,1024]{1,0:T(8,128)(2,1)}, u32[]{:S(2)}, u32[]{:S(2)}) collective-permute-start(bf16[8,1024]{1,0:T(8,128)(2,1)} %get-tuple-element.291), channel_id=1, source_target_pairs={{0,24},{2,26},{4,28},{6,30},{8,0},{10,2},{12,4},{14,6},{16,8},{18,... | collective-permute-start | bytes 49160 | tf_op jit(solution)/shard_map/ppermute | solution.py:46
  (558 shorter events, 228.2 us)
Async XLA Ops:
  7.2 132.7 %all-gather.3.cloned.1.call-start = ((), (), s32[]{:S(2)}) async-start(), calls=%async_computation.2 | async-start | bytes 8912896 | tf_op jit(solution)/shard_map/all_gather | solution.py:411
  9.8 198.1 %all-gather.5.cloned.1.call-start = ((), (), s32[]{:S(2)}) async-start(), calls=%async_computation.3 | async-start | bytes 10027008 | tf_op jit(solution)/shard_map/all_gather | solution.py:438
  9.9 38.2 %collective-permute-start.1 = (bf16[64,768]{1,0:T(8,128)(2,1)S(1)}, bf16[64,768]{1,0:T(8,128)(2,1)S(1)}, u32[]{:S(2)}, u32[]{:S(2)}) collective-permute-start(bf16[64,768]{1,0:T(8,128)(2,1)S(1)} %constant_dynamic-slice_fusion.2), channel_id=1, source_target_pairs={{0,2},{2,0},{4,6},{6,4},{8,10},{10,8},{12,14},{14,12},{16,18},{18,... | collective-permute-start | bytes 294920 | tf_op jit(solution)/shard_map/ppermute | solution.py:36
  10.6 60.0 %collective-permute-start = (s32[256,51]{1,0:T(8,128)S(1)}, s32[256,51]{1,0:T(8,128)S(1)}, u32[]{:S(2)}, u32[]{:S(2)}) collective-permute-start(s32[256,51]{1,0:T(8,128)S(1)} %copy.242), channel_id=1, source_target_pairs={{0,1},{1,0},{2,3},{3,2},{4,5},{5,4},{6,7},{7,6},{8,9},{9,8},{10,11... | collective-permute-start | bytes 156680 | tf_op jit(solution)/shard_map/ppermute | solution.py:50
  47.4 317.2 %reduce-scatter.3.cloned.1.call-start = ((), (), s32[]{:S(2)}) async-start(), calls=%async_computation.4 | async-start | bytes 10027008 | tf_op jit(solution)/shard_map/reduce_scatter | solution.py:529
  51.9 18.7 %collective-permute-start.3 = (bf16[64,768]{1,0:T(8,128)(2,1)S(1)}, bf16[64,768]{1,0:T(8,128)(2,1)S(1)}, u32[]{:S(2)}, u32[]{:S(2)}) collective-permute-start(bf16[64,768]{1,0:T(8,128)(2,1)S(1)} %get-tuple-element.252), channel_id=1, source_target_pairs={{0,16},{2,18},{4,20},{6,22},{8,24},{10,26},{12,28},{14,30},{16,0},... | collective-permute-start | bytes 294920 | tf_op jit(solution)/shard_map/ppermute | solution.py:46
  52.0 18.6 %collective-permute-start.4 = (bf16[64,768]{1,0:T(8,128)(2,1)S(1)}, bf16[64,768]{1,0:T(8,128)(2,1)S(1)}, u32[]{:S(2)}, u32[]{:S(2)}) collective-permute-start(bf16[64,768]{1,0:T(8,128)(2,1)S(1)} %get-tuple-element.252), channel_id=1, source_target_pairs={{0,8},{2,10},{4,12},{6,14},{8,16},{10,18},{12,20},{14,22},{16,24},... | collective-permute-start | bytes 294920 | tf_op jit(solution)/shard_map/ppermute | solution.py:46
  72.1 43.8 %collective-permute-start.13 = (bf16[48,3072]{1,0:T(8,128)(2,1)S(1)}, bf16[48,3072]{1,0:T(8,128)(2,1)}, u32[]{:S(2)}, u32[]{:S(2)}) collective-permute-start(bf16[48,3072]{1,0:T(8,128)(2,1)S(1)} %pad_maximum_fusion.14), channel_id=1, source_target_pairs={{0,8},{2,10},{4,12},{6,14},{8,16},{10,18},{12,20},{14,22},{16,24},... | collective-permute-start | bytes 884744 | tf_op jit(solution)/shard_map/ppermute | solution.py:46
  72.1 41.2 %collective-permute-start.12 = (bf16[48,3072]{1,0:T(8,128)(2,1)S(1)}, bf16[48,3072]{1,0:T(8,128)(2,1)}, u32[]{:S(2)}, u32[]{:S(2)}) collective-permute-start(bf16[48,3072]{1,0:T(8,128)(2,1)S(1)} %pad_maximum_fusion.14), channel_id=1, source_target_pairs={{0,16},{2,18},{4,20},{6,22},{8,24},{10,26},{12,28},{14,30},{16,0},... | collective-permute-start | bytes 884744 | tf_op jit(solution)/shard_map/ppermute | solution.py:46
  77.6 34.2 %collective-permute-start.11 = (bf16[48,3072]{1,0:T(8,128)(2,1)S(1)}, bf16[48,3072]{1,0:T(8,128)(2,1)}, u32[]{:S(2)}, u32[]{:S(2)}) collective-permute-start(bf16[48,3072]{1,0:T(8,128)(2,1)S(1)} %pad_maximum_fusion.14), channel_id=1, source_target_pairs={{0,24},{2,26},{4,28},{6,30},{8,0},{10,2},{12,4},{14,6},{16,8},{18,... | collective-permute-start | bytes 884744 | tf_op jit(solution)/shard_map/ppermute | solution.py:46
  80.9 38.3 %collective-permute-start.8 = (bf16[4,64,768]{2,1,0:T(8,128)(2,1)S(1)}, bf16[4,64,768]{2,1,0:T(8,128)(2,1)}, u32[]{:S(2)}, u32[]{:S(2)}) collective-permute-start(bf16[4,64,768]{2,1,0:T(8,128)(2,1)S(1)} %bitcast_dynamic-update-slice_fusion.16), channel_id=1, source_target_pairs={{0,2},{2,0},{4,6},{6,4},{8,10},{10,8},{12,14},{14,12},{16,18},{18,... | collective-permute-start | bytes 1179656 | tf_op jit(solution)/shard_map/ppermute | solution.py:36
  80.9 36.8 %collective-permute-start.7 = (bf16[4,64,768]{2,1,0:T(8,128)(2,1)S(1)}, bf16[4,64,768]{2,1,0:T(8,128)(2,1)}, u32[]{:S(2)}, u32[]{:S(2)}) collective-permute-start(bf16[4,64,768]{2,1,0:T(8,128)(2,1)S(1)} %bitcast_dynamic-update-slice_fusion.16), channel_id=1, source_target_pairs={{0,4},{2,6},{4,0},{6,2},{8,12},{10,14},{12,8},{14,10},{16,20},{18,... | collective-permute-start | bytes 1179656 | tf_op jit(solution)/shard_map/ppermute | solution.py:41
  111.7 26.1 %collective-permute-start.5 = (bf16[256,1024]{1,0:T(8,128)(2,1)S(1)}, bf16[256,1024]{1,0:T(8,128)(2,1)S(1)}, u32[]{:S(2)}, u32[]{:S(2)}) collective-permute-start(bf16[256,1024]{1,0:T(8,128)(2,1)S(1)} %get-tuple-element.249), channel_id=1, source_target_pairs={{0,1},{1,0},{2,3},{3,2},{4,5},{5,4},{6,7},{7,6},{8,9},{9,8},{10,11... | collective-permute-start | bytes 1572872 | tf_op jit(solution)/shard_map/ppermute | solution.py:50
  113.3 23.7 %collective-permute-start.6 = (bf16[256,1024]{1,0:T(8,128)(2,1)S(1)}, bf16[256,1024]{1,0:T(8,128)(2,1)S(1)}, u32[]{:S(2)}, u32[]{:S(2)}) collective-permute-start(bf16[256,1024]{1,0:T(8,128)(2,1)S(1)} %get-tuple-element.298), channel_id=1, source_target_pairs={{0,1},{1,0},{2,3},{3,2},{4,5},{5,4},{6,7},{7,6},{8,9},{9,8},{10,11... | collective-permute-start | bytes 1572872 | tf_op jit(solution)/shard_map/ppermute | solution.py:50
  116.9 39.6 %collective-permute-start.15 = (bf16[4,48,3072]{2,1,0:T(8,128)(2,1)S(1)}, bf16[4,48,3072]{2,1,0:T(8,128)(2,1)}, u32[]{:S(2)}, u32[]{:S(2)}) collective-permute-start(bf16[4,48,3072]{2,1,0:T(8,128)(2,1)S(1)} %bitcast_dynamic-update-slice_fusion.12), channel_id=1, source_target_pairs={{0,2},{2,0},{4,6},{6,4},{8,10},{10,8},{12,14},{14,12},{16,18},{18,... | collective-permute-start | bytes 3538952 | tf_op jit(solution)/shard_map/ppermute | solution.py:36
  117.7 35.4 %collective-permute-start.14 = (bf16[4,48,3072]{2,1,0:T(8,128)(2,1)S(1)}, bf16[4,48,3072]{2,1,0:T(8,128)(2,1)}, u32[]{:S(2)}, u32[]{:S(2)}) collective-permute-start(bf16[4,48,3072]{2,1,0:T(8,128)(2,1)S(1)} %bitcast_dynamic-update-slice_fusion.12), channel_id=1, source_target_pairs={{0,4},{2,6},{4,0},{6,2},{8,12},{10,14},{12,8},{14,10},{16,20},{18,... | collective-permute-start | bytes 3538952 | tf_op jit(solution)/shard_map/ppermute | solution.py:41
  119.3 19.6 %collective-permute-start.9 = (bf16[4,64,768]{2,1,0:T(8,128)(2,1)}, bf16[4,64,768]{2,1,0:T(8,128)(2,1)S(1)}, u32[]{:S(2)}, u32[]{:S(2)}) collective-permute-start(bf16[4,64,768]{2,1,0:T(8,128)(2,1)} %collective-permute-done.7), channel_id=1, source_target_pairs={{0,2},{2,0},{4,6},{6,4},{8,10},{10,8},{12,14},{14,12},{16,18},{18,... | collective-permute-start | bytes 1179656 | tf_op jit(solution)/shard_map/ppermute | solution.py:36
  171.1 18.6 %collective-permute-start.17 = (bf16[256,768]{1,0:T(8,128)(2,1)}, bf16[256,768]{1,0:T(8,128)(2,1)}, u32[]{:S(2)}, u32[]{:S(2)}) collective-permute-start(bf16[256,768]{1,0:T(8,128)(2,1)} %get-tuple-element.277), channel_id=1, source_target_pairs={{0,1},{1,0},{2,3},{3,2},{4,5},{5,4},{6,7},{7,6},{8,9},{9,8},{10,11... | collective-permute-start | bytes 1179656 | tf_op jit(solution)/shard_map/ppermute | solution.py:50
  237.8 222.1 %reduce-scatter.5.cloned.1.call-start = ((), (), s32[]{:S(2)}) async-start(), calls=%async_computation.5 | async-start | bytes 5292032 | tf_op jit(solution)/shard_map/reduce_scatter | solution.py:611
  314.0 37.2 %collective-permute-start.24 = (bf16[4,48,3072]{2,1,0:T(8,128)(2,1)}, bf16[4,48,3072]{2,1,0:T(8,128)(2,1)S(1)}, u32[]{:S(2)}, u32[]{:S(2)}) collective-permute-start(bf16[4,48,3072]{2,1,0:T(8,128)(2,1)} %fusion.74), channel_id=1, source_target_pairs={{0,4},{2,6},{4,0},{6,2},{8,12},{10,14},{12,8},{14,10},{16,20},{18,... | collective-permute-start | bytes 3538952 | tf_op jit(solution)/shard_map/ppermute | solution.py:41
  318.8 34.6 %collective-permute-start.25 = (bf16[4,2,128,1408]{3,2,1,0:T(8,128)(2,1)S(1)}, bf16[4,2,128,1408]{3,2,1,0:T(8,128)(2,1)}, u32[]{:S(2)}, u32[]{:S(2)}) collective-permute-start(bf16[4,2,128,1408]{3,2,1,0:T(8,128)(2,1)S(1)} %fusion.37), channel_id=1, source_target_pairs={{0,2},{2,0},{4,6},{6,4},{8,10},{10,8},{12,14},{14,12},{16,18},{18,... | collective-permute-start | bytes 8650760 | tf_op jit(solution)/shard_map/ppermute | solution.py:36
  328.6 29.8 %collective-permute-start.23 = (bf16[256,1024]{1,0:T(8,128)(2,1)}, bf16[256,1024]{1,0:T(8,128)(2,1)}, u32[]{:S(2)}, u32[]{:S(2)}) collective-permute-start(bf16[256,1024]{1,0:T(8,128)(2,1)} %get-tuple-element.278), channel_id=1, source_target_pairs={{0,1},{1,0},{2,3},{3,2},{4,5},{5,4},{6,7},{7,6},{8,9},{9,8},{10,11... | collective-permute-start | bytes 1572872 | tf_op jit(solution)/shard_map/ppermute | solution.py:50
  330.1 28.3 %collective-permute-start.26 = (bf16[256,1024]{1,0:T(8,128)(2,1)}, bf16[256,1024]{1,0:T(8,128)(2,1)}, u32[]{:S(2)}, u32[]{:S(2)}) collective-permute-start(bf16[256,1024]{1,0:T(8,128)(2,1)} %get-tuple-element.279), channel_id=1, source_target_pairs={{0,1},{1,0},{2,3},{3,2},{4,5},{5,4},{6,7},{7,6},{8,9},{9,8},{10,11... | collective-permute-start | bytes 1572872 | tf_op jit(solution)/shard_map/ppermute | solution.py:50
  357.3 33.7 %collective-permute-start.30 = (bf16[4,128,1408]{2,1,0:T(8,128)(2,1)}, bf16[4,128,1408]{2,1,0:T(8,128)(2,1)}, u32[]{:S(2)}, u32[]{:S(2)}) collective-permute-start(bf16[4,128,1408]{2,1,0:T(8,128)(2,1)} %fusion.59), channel_id=1, source_target_pairs={{0,4},{2,6},{4,0},{6,2},{8,12},{10,14},{12,8},{14,10},{16,20},{18,... | collective-permute-start | bytes 4325384 | tf_op jit(solution)/shard_map/ppermute | solution.py:41
  366.0 21.4 %collective-permute-start.29 = (bf16[48,3072]{1,0:T(8,128)(2,1)S(1)}, bf16[48,3072]{1,0:T(8,128)(2,1)S(1)}, u32[]{:S(2)}, u32[]{:S(2)}) collective-permute-start(bf16[48,3072]{1,0:T(8,128)(2,1)S(1)} %get-tuple-element.272), channel_id=1, source_target_pairs={{0,8},{2,10},{4,12},{6,14},{8,16},{10,18},{12,20},{14,22},{16,24},... | collective-permute-start | bytes 884744 | tf_op jit(solution)/shard_map/ppermute | solution.py:46
  369.8 19.6 %collective-permute-start.28 = (bf16[48,3072]{1,0:T(8,128)(2,1)S(1)}, bf16[48,3072]{1,0:T(8,128)(2,1)S(1)}, u32[]{:S(2)}, u32[]{:S(2)}) collective-permute-start(bf16[48,3072]{1,0:T(8,128)(2,1)S(1)} %get-tuple-element.273), channel_id=1, source_target_pairs={{0,16},{2,18},{4,20},{6,22},{8,24},{10,26},{12,28},{14,30},{16,0},... | collective-permute-start | bytes 884744 | tf_op jit(solution)/shard_map/ppermute | solution.py:46
  369.8 19.6 %collective-permute-start.27 = (bf16[48,3072]{1,0:T(8,128)(2,1)S(1)}, bf16[48,3072]{1,0:T(8,128)(2,1)S(1)}, u32[]{:S(2)}, u32[]{:S(2)}) collective-permute-start(bf16[48,3072]{1,0:T(8,128)(2,1)S(1)} %get-tuple-element.274), channel_id=1, source_target_pairs={{0,24},{2,26},{4,28},{6,30},{8,0},{10,2},{12,4},{14,6},{16,8},{18,... | collective-permute-start | bytes 884744 | tf_op jit(solution)/shard_map/ppermute | solution.py:46
  410.1 27.2 %collective-permute-start.35 = (bf16[48,3072]{1,0:T(8,128)(2,1)S(1)}, bf16[48,3072]{1,0:T(8,128)(2,1)}, u32[]{:S(2)}, u32[]{:S(2)}) collective-permute-start(bf16[48,3072]{1,0:T(8,128)(2,1)S(1)} %get-tuple-element.103), channel_id=1, source_target_pairs={{0,1},{1,0},{2,3},{3,2},{4,5},{5,4},{6,7},{7,6},{8,9},{9,8},{10,11... | collective-permute-start | bytes 884744 | tf_op jit(solution)/shard_map/ppermute | solution.py:50
  412.7 42.2 %collective-permute-start.34 = (bf16[128,1408]{1,0:T(8,128)(2,1)}, bf16[128,1408]{1,0:T(8,128)(2,1)}, u32[]{:S(2)}, u32[]{:S(2)}) collective-permute-start(bf16[128,1408]{1,0:T(8,128)(2,1)} %get-tuple-element.259), channel_id=1, source_target_pairs={{0,8},{2,10},{4,12},{6,14},{8,16},{10,18},{12,20},{14,22},{16,24},... | collective-permute-start | bytes 1081352 | tf_op jit(solution)/shard_map/ppermute | solution.py:46
  419.2 35.7 %collective-permute-start.33 = (bf16[128,1408]{1,0:T(8,128)(2,1)}, bf16[128,1408]{1,0:T(8,128)(2,1)}, u32[]{:S(2)}, u32[]{:S(2)}) collective-permute-start(bf16[128,1408]{1,0:T(8,128)(2,1)} %get-tuple-element.260), channel_id=1, source_target_pairs={{0,16},{2,18},{4,20},{6,22},{8,24},{10,26},{12,28},{14,30},{16,0},... | collective-permute-start | bytes 1081352 | tf_op jit(solution)/shard_map/ppermute | solution.py:46
  420.5 34.3 %collective-permute-start.32 = (bf16[128,1408]{1,0:T(8,128)(2,1)}, bf16[128,1408]{1,0:T(8,128)(2,1)}, u32[]{:S(2)}, u32[]{:S(2)}) collective-permute-start(bf16[128,1408]{1,0:T(8,128)(2,1)} %get-tuple-element.261), channel_id=1, source_target_pairs={{0,24},{2,26},{4,28},{6,30},{8,0},{10,2},{12,4},{14,6},{16,8},{18,... | collective-permute-start | bytes 1081352 | tf_op jit(solution)/shard_map/ppermute | solution.py:46
  463.7 26.5 %collective-permute-start.44 = (bf16[128,2816]{1,0:T(8,128)(2,1)}, bf16[128,2816]{1,0:T(8,128)(2,1)}, u32[]{:S(2)}, u32[]{:S(2)}) collective-permute-start(bf16[128,2816]{1,0:T(8,128)(2,1)} %maximum_maximum_fusion), channel_id=1, source_target_pairs={{0,1},{1,0},{2,3},{3,2},{4,5},{5,4},{6,7},{7,6},{8,9},{9,8},{10,11... | collective-permute-start | bytes 2162696 | tf_op jit(solution)/shard_map/ppermute | solution.py:50
  (112 other events, 1025.6 us)
Sparse Core Ops, SparseCore 0:
  10.8 112.1 all-gather.2
  125.9 81.9 all-gather.4
  237.9 121.4 reduce-scatter.2
  364.8 94.2 reduce-scatter.4

commit v5 on v4

--- a/solution.py
+++ b/solution.py
@@ -193,7 +193,7 @@
 
 
 def conv_backward_kernel(window_ref, flipped_ref, codes_ref, weight_ref, turned_ref, pooled_ref, share_in_ref,
-                         grad_ref, table_ref, share_ref, scores_ref, spread_ref, letters):
+                         grad_ref, table_ref, share_ref, scores_ref, spread_ref, letters, narrow):
     rows = window_ref.shape[0]
     words = rows // letters
     channels = weight_ref.shape[1]
@@ -205,18 +205,29 @@
         grad_ref[...] = jnp.zeros_like(grad_ref)
         table_ref[...] = jnp.zeros_like(table_ref)
 
-    def one_tile(index, _):
-        c = pl.multiple_of(index * tile, tile)
-        scores_ref[...] = jnp.dot(window_ref[...], weight_ref[:, pl.ds(c, tile)], preferred_element_type=jnp.float32)
+    fewer = letters - narrow + 1
+
+    @pl.when(pl.program_id(0) == 0)
+    def _():
+        share_ref[fewer * words:, tile:] = jnp.zeros((rows - fewer * words, channels - tile), jnp.bfloat16)
+
+    def one_tile(c, count):
+        scores_ref[: count * words] = jnp.dot(
+            window_ref[: count * words], weight_ref[:, pl.ds(c, tile)], preferred_element_type=jnp.float32
+        )
         for r in range(0, words, 16):
             top = pooled_ref[r:r + 16, pl.ds(c, tile)]
             part = share_in_ref[r:r + 16, pl.ds(c, tile)]
-            for p in range(letters):
+            for p in range(count):
                 hit = scores_ref[p * words + r:p * words + r + 16] == top
                 share_ref[p * words + r:p * words + r + 16, pl.ds(c, tile)] = jnp.where(hit, part, 0.0).astype(jnp.bfloat16)
+
+    def later_tile(index, _):
+        one_tile(pl.multiple_of(index * tile, tile), fewer)
         return 0
 
-    lax.fori_loop(0, channels // tile, one_tile, 0)
+    one_tile(0, letters)
+    lax.fori_loop(1, channels // tile, later_tile, 0)
     grad_ref[...] += jnp.dot(flipped_ref[...], share_ref[...], preferred_element_type=jnp.float32)
     scores_ref[:, :LANES] = jnp.dot(share_ref[...], turned_ref[...], preferred_element_type=jnp.float32)
     slot = lax.broadcasted_iota(jnp.int32, (words, LANES), 1) // 16
@@ -267,7 +278,7 @@
     )(spread, lens, weight)
 
 
-def conv_backward(window, flipped, codes, weight, turned, pooled, share, vocab, block, first, steps):
+def conv_backward(window, flipped, codes, weight, turned, pooled, share, vocab, block, first, steps, narrow):
     words, channels = pooled.shape
     rows = window.shape[0] // (words // block)
     letters = rows // block
@@ -275,7 +286,7 @@
     vocab = -(-vocab // 16) * 16
 
     def kernel(*refs):
-        conv_backward_kernel(*refs, letters=letters)
+        conv_backward_kernel(*refs, letters=letters, narrow=narrow)
 
     return pl.pallas_call(
         kernel,
@@ -631,9 +642,14 @@
             block,
             first,
             count,
+            narrow,
         )
 
     cuts = steps // 2
+    edges = [0]
+    for kernel in kernels:
+        edges.append(edges[-1] + kernel.shape[1])
+    narrow = min(width for width in range(1, WIDTHS + 1) if edges[width] > 512)
     backs = [back(0, 0, cuts, attention_quarter, joint_half, highway_rows)]
     attention_sum = scatter_outer(attention_quarter, grad_pooled, backs[0])
     joint_quarter = scatter_middle(joint_half, (), backs[0])

time: 536 us -> 536 us (level)
  transfers between devices with their start and end apart: 55 -> 55, of which waited for: 20 -> 21; matrix products, arithmetic and copies ran while one was open for 35% -> 35% of each run, Pallas kernels for 20% -> 20%
where the time goes in v5:
time: 536 us; the launch traced here: 528 us
  Pallas kernels  104 us (19%)
  matrix products  103 us (19%)
  waiting for transfers between devices  94.8 us (18%)
  local copies, waits for them, and re-layouts  72.1 us (13%)
  starting transfers between devices  72 us (13%)
  other arithmetic  65.3 us (12%)
  between operations  16.9 us (3%)
    ppermute x16, waiting for transfers between devices, seq_swap(): return lax.ppermute(value, 'seq', [(0, 1), (1, 0)])  65.3 us
    pallas_call x4, Pallas kernels, conv_backward(): pl.pallas_call(kernel, grid=(steps,), in_specs=[pl.BlockSpec((rows, LANES...  59.4 us
    ppermute x18, starting transfers between devices, outer_shift(): lax.ppermute(value, 'dp', [(spot, (spot - 4 * steps) % size) for spot in...  45.9 us
    pallas_call x2, Pallas kernels, conv_forward(): pl.pallas_call(conv_forward_kernel, grid=(steps,), in_specs=[pl.BlockSpec...  42.3 us
    ppermute x18, waiting for transfers between devices, outer_shift(): lax.ppermute(value, 'dp', [(spot, (spot - 4 * steps) % size) for spot in...  20.1 us
    ppermute x16, starting transfers between devices, seq_swap(): return lax.ppermute(value, 'seq', [(0, 1), (1, 0)])  18.4 us
    unnamed x188, local copies, waits for them, and re-layouts  13.2 us
    dot_general x2, matrix products, body(): jnp.dot(hidden0_all, highway_parts[part], preferred_element_type=f32)  13 us
  transfers between devices with their start and end apart: 55, of which 21 were waited for; matrix products, arithmetic and copies ran while one was open for 35% of the time, Pallas kernels for 20%

profile of v5, /device:TPU:0, one launch (start us, length us, event | category | flops | bytes accessed | tf_op | source)
XLA Modules:
  0.0 527.9 jit_solution(15192651441383995718)
XLA Ops:
  21.8 4.4 convolution_convert_fusion.1
  26.2 21.2 %conv_forward.2 = (f32[256,1024]{1,0:T(8,128)}, f32[256,1024]{1,0:T(8,128)}, bf16[12800,128]{1,0:T(8,128)(2,1)}, bf16[128,12800]{1,0:T(8,128)(2,1)}) custom-call(bf16[50,256,128]{2,1,0:T(8,128)(2,1)} %bitcast.369, s32[256,1]{1,0:T(8,128)} %copy.240.lens_ref, bf16[128,1024]{1,0:T(8,128)(2,1)} %copy.241.weight_ref.refs_3_), custom_call_target="tpu_custom_call" | custom-call | flops 3355443200 | bytes 65536000 | tf_op jit(solution)/shard_map/conv_forward/pallas_call | solution.py:250
  53.0 4.1 collective-permute-done.2
  57.2 13.4 %collective-permute-done.3 = bf16[64,768]{1,0:T(8,128)(2,1)S(1)} collective-permute-done((bf16[64,768]{1,0:T(8,128)(2,1)S(1)}, bf16[64,768]{1,0:T(8,128)(2,1)S(1)}, u32[]{:S(2)}, u32[]{:S(2)}) %collective-permute-start.3) | collective-permute-done | bytes 98336 | tf_op jit(solution)/shard_map/ppermute | solution.py:46
  72.1 5.5 %collective-permute-start.12 = (bf16[48,3072]{1,0:T(8,128)(2,1)S(1)}, bf16[48,3072]{1,0:T(8,128)(2,1)}, u32[]{:S(2)}, u32[]{:S(2)}) collective-permute-start(bf16[48,3072]{1,0:T(8,128)(2,1)S(1)} %pad_maximum_fusion.14), channel_id=1, source_target_pairs={{0,16},{2,18},{4,20},{6,22},{8,24},{10,26},{12,28},{14,30},{16,0},... | collective-permute-start | bytes 884744 | tf_op jit(solution)/shard_map/ppermute | solution.py:46
  82.9 4.4 convolution_convert_fusion
  87.3 21.2 %conv_forward.3 = (f32[256,1024]{1,0:T(8,128)}, f32[256,1024]{1,0:T(8,128)}, bf16[12800,128]{1,0:T(8,128)(2,1)}, bf16[128,12800]{1,0:T(8,128)(2,1)}) custom-call(bf16[50,256,128]{2,1,0:T(8,128)(2,1)} %bitcast.368, s32[256,1]{1,0:T(8,128)} %slice.408.lens_ref, bf16[128,1024]{1,0:T(8,128)(2,1)} %copy.241.weight_ref.refs_3_), custom_call_target="tpu_custom_call" | custom-call | flops 3355443200 | bytes 65536000 | tf_op jit(solution)/shard_map/conv_forward/pallas_call | solution.py:250
  120.8 16.2 %collective-permute-done.6 = bf16[256,1024]{1,0:T(8,128)(2,1)S(1)} collective-permute-done((bf16[256,1024]{1,0:T(8,128)(2,1)S(1)}, bf16[256,1024]{1,0:T(8,128)(2,1)S(1)}, u32[]{:S(2)}, u32[]{:S(2)}) %collective-permute-start.6) | collective-permute-done | bytes 524320 | tf_op jit(solution)/shard_map/ppermute | solution.py:50
  140.0 5.8 %fusion.15 = f32[512,1024]{1,0:T(8,128)S(1)} fusion(bf16[2048,2048]{0,1:T(8,128)(2,1)} %all-gather.3.cloned.1.call-done, bf16[256,2048]{1,0:T(8,128)(2,1)} %copy-done.62, bf16[256,2048]{1,0:T(8,128)(2,1)} %copy-done.65), kind=kOutput, calls=%fused_computation.35 | convolution fusion | flops 2151677952 | bytes 8388608 | tf_op jit(solution)/shard_map/dot_general | solution.py:467
  145.9 7.2 %fusion.41 = (bf16[512,1024]{1,0:T(8,128)(2,1)S(1)}, f32[512,1024]{1,0:T(8,128)}) fusion(f32[512,1024]{1,0:T(8,128)S(1)} %fusion.15, f32[256,1024]{1,0:T(8,128)S(1)} %copy-done.30, f32[256,1024]{1,0:T(8,128)S(1)} %copy-done.32, f32[1024]{0:T(1024)S(1)} %bitcast.363, f32[1024]{0:T(1024)S(1)} %bitcast.365, ...), kind=kOutput, calls=%fused_computation.79 | convolution fusion | flops 2157969408 | bytes 13639680 | tf_op jit(solution)/shard_map/dot_general | solution.py:467
  157.9 9.4 %collective-permute-done.10 = bf16[256,768]{1,0:T(8,128)(2,1)S(1)} collective-permute-done((bf16[256,768]{1,0:T(8,128)(2,1)S(1)}, bf16[256,768]{1,0:T(8,128)(2,1)S(1)}, u32[]{:S(2)}, u32[]{:S(2)}) %collective-permute-start.10) | collective-permute-done | bytes 393248 | tf_op jit(solution)/shard_map/ppermute | solution.py:50
  174.1 8.6 %collective-permute-done.18 = bf16[256,768]{1,0:T(8,128)(2,1)S(1)} collective-permute-done((bf16[256,768]{1,0:T(8,128)(2,1)S(1)}, bf16[256,768]{1,0:T(8,128)(2,1)S(1)}, u32[]{:S(2)}, u32[]{:S(2)}) %collective-permute-start.18) | collective-permute-done | bytes 393248 | tf_op jit(solution)/shard_map/ppermute | solution.py:50
  183.0 6.6 %collective-permute-done.17 = bf16[256,768]{1,0:T(8,128)(2,1)} collective-permute-done((bf16[256,768]{1,0:T(8,128)(2,1)}, bf16[256,768]{1,0:T(8,128)(2,1)}, u32[]{:S(2)}, u32[]{:S(2)}) %collective-permute-start.17) | collective-permute-done | bytes 393248 | tf_op jit(solution)/shard_map/ppermute | solution.py:50
  192.0 6.2 %fusion.169 = (f32[12,256]{1,0:T(8,128)}, f32[12,256,512]{2,1,0:T(8,128)}) fusion(pred[512]{0:T(512)(128)(4,1)} %fusion.139, bf16[256,12,64]{0,2,1:T(8,128)(2,1)S(1)} %bitcast.330, bf16[512,12,64]{0,2,1:T(8,128)(2,1)S(1)} %bitcast.320), kind=kOutput, calls=%fused_computation.396 | convolution fusion | flops 207618560 | bytes 7483904 | tf_op jit(solution)/shard_map/sub | solution.py:498
  207.9 9.7 %multiply_convert_fusion.1 = (bf16[256,3072]{1,0:T(8,128)(2,1)S(1)}, f32[256,3072]{1,0:T(8,128)S(1)}, f32[256,3072]{1,0:T(8,128)S(1)}) fusion(bf16[768,6144]{1,0:T(8,128)(2,1)} %all-gather.5.cloned.1.call-done, f32[256,768]{1,0:T(8,128)S(1)} %get-tuple-element.305, f32[768]{0:T(1024)S(1)} %convert_element_type.362, f32[768]{0:T(1024)S(1)} %convert_element_type.361, ...), kind=kOutput, calls=%fused_computation.44 | convolution fusion | flops 1260060672 | bytes 13377536 | tf_op jit(solution)/shard_map/dot_general | solution.py:512
  243.3 4.2 fusion.56
  257.4 5.7 %collective-permute-done.20 = bf16[256,768]{0,1:T(8,128)(2,1)S(1)} collective-permute-done((bf16[256,768]{0,1:T(8,128)(2,1)S(1)}, bf16[256,768]{0,1:T(8,128)(2,1)S(1)}, u32[]{:S(2)}, u32[]{:S(2)}) %collective-permute-start.20) | collective-permute-done | bytes 393248 | tf_op jit(solution)/shard_map/ppermute | solution.py:50
  263.2 7.7 %collective-permute-done.19 = bf16[256,768]{0,1:T(8,128)(2,1)S(1)} collective-permute-done((bf16[256,768]{0,1:T(8,128)(2,1)S(1)}, bf16[256,768]{0,1:T(8,128)(2,1)S(1)}, u32[]{:S(2)}, u32[]{:S(2)}) %collective-permute-start.19) | collective-permute-done | bytes 393248 | tf_op jit(solution)/shard_map/ppermute | solution.py:50
  284.3 8.9 %collective-permute-done.21 = bf16[256,768]{1,0:T(8,128)(2,1)S(1)} collective-permute-done((bf16[256,768]{1,0:T(8,128)(2,1)S(1)}, bf16[256,768]{1,0:T(8,128)(2,1)S(1)}, u32[]{:S(2)}, u32[]{:S(2)}) %collective-permute-start.21) | collective-permute-done | bytes 393248 | tf_op jit(solution)/shard_map/ppermute | solution.py:50
  293.3 5.8 %convert_add_fusion.1 = f32[4,2,48,3072]{3,2,1,0:T(8,128)} fusion(bf16[4,2,48,3072]{3,2,1,0:T(8,128)(2,1)} %collective-permute-done.22, bf16[4,2,2,48,3072]{4,3,2,1,0:T(8,128)(2,1)} %bitcast.301, s32[]{:T(128)S(6)} %select_n.658), kind=kLoop, calls=%fused_computation.25 | loop fusion | flops 3538944 | bytes 9437188 | tf_op jit(solution)/shard_map/add | solution.py:96
  304.0 7.1 %convert_reduce_fusion = (f32[1024]{0:T(1024)S(1)}, bf16[512,1024]{1,0:T(8,128)(2,1)}, f32[1024]{0:T(1024)S(1)}, bf16[512,1024]{1,0:T(8,128)(2,1)}, f32[512,1024]{1,0:T(8,128)}) fusion(f32[512,1024]{1,0:T(8,128)} %get-tuple-element.301, f32[256,1024]{1,0:T(8,128)S(1)} %copy-done.31, f32[256,1024]{1,0:T(8,128)} %get-tuple-element.299, ...), kind=kOutput, calls=%fused_computation.87 | convolution fusion | flops 815265792 | bytes 12857344 | tf_op jit(solution)/shard_map/td,fd->tf/dot_general | solution.py:586
  314.1 4.4 convolution_convert_fusion.6
  319.7 4.9 fusion.13
  336.8 4.4 convolution_convert_fusion.5
  341.2 5.4 %pad_maximum_fusion = bf16[16,152,1024]{2,1,0:T(8,128)(2,1)} fusion(bf16[16,24,1024]{2,1,0:T(8,128)(2,1)S(1)} %reshape.489, bf16[16,128,1024]{2,1,0:T(8,128)(2,1)} %bitcast.318), kind=kLoop, calls=%fused_computation.21 | loop fusion | flops 9961472 | bytes 9961472 | tf_op jit(solution)/shard_map/concatenate | solution.py:619
  372.3 14.9 %conv_backward.4 = (f32[128,1024]{1,0:T(8,128)}, f32[272,128]{1,0:T(8,128)}) custom-call(bf16[12800,128]{1,0:T(8,128)(2,1)} %get-tuple-element.71.refs_0_, bf16[128,12800]{1,0:T(8,128)(2,1)} %get-tuple-element.72.refs_1_, s32[4,1,3200]{2,1,0:T(1,128)} %reshape.513.refs_2_, bf16[128,1024]{1,0:T(8,128)(2,1)} %copy.241.weight_ref.refs_3_, ...), custom_call_target="tpu_custom_call" | custom-call | flops 5033164800 | bytes 52428800 | tf_op jit(solution)/shard_map/conv_backward/pallas_call | solution.py:291
  391.0 4.2 fusion.151
  395.2 14.7 %conv_backward.5 = (f32[128,1024]{1,0:T(8,128)}, f32[272,128]{1,0:T(8,128)}) custom-call(bf16[12800,128]{1,0:T(8,128)(2,1)} %get-tuple-element.71.refs_0_, bf16[128,12800]{1,0:T(8,128)(2,1)} %get-tuple-element.72.refs_1_, s32[4,1,3200]{2,1,0:T(1,128)} %reshape.513.refs_2_, bf16[128,1024]{1,0:T(8,128)(2,1)} %copy.241.weight_ref.refs_3_, ...), custom_call_target="tpu_custom_call" | custom-call | flops 5033164800 | bytes 52428800 | tf_op jit(solution)/shard_map/conv_backward/pallas_call | solution.py:291
  412.4 6.6 %collective-permute-start.34 = (bf16[128,1408]{1,0:T(8,128)(2,1)}, bf16[128,1408]{1,0:T(8,128)(2,1)}, u32[]{:S(2)}, u32[]{:S(2)}) collective-permute-start(bf16[128,1408]{1,0:T(8,128)(2,1)} %get-tuple-element.259), channel_id=1, source_target_pairs={{0,8},{2,10},{4,12},{6,14},{8,16},{10,18},{12,20},{14,22},{16,24},... | collective-permute-start | bytes 1081352 | tf_op jit(solution)/shard_map/ppermute | solution.py:46
  421.9 15.0 %conv_backward.6 = (f32[128,1024]{1,0:T(8,128)}, f32[272,128]{1,0:T(8,128)}) custom-call(bf16[12800,128]{1,0:T(8,128)(2,1)} %get-tuple-element.87.refs_0_, bf16[128,12800]{1,0:T(8,128)(2,1)} %get-tuple-element.88.refs_1_, s32[4,1,3200]{2,1,0:T(1,128)} %reshape.514.refs_2_, bf16[128,1024]{1,0:T(8,128)(2,1)} %copy.241.weight_ref.refs_3_, ...), custom_call_target="tpu_custom_call" | custom-call | flops 5033164800 | bytes 52428800 | tf_op jit(solution)/shard_map/conv_backward/pallas_call | solution.py:291
  439.6 14.9 %conv_backward.7 = (f32[128,1024]{1,0:T(8,128)}, f32[272,128]{1,0:T(8,128)}) custom-call(bf16[12800,128]{1,0:T(8,128)(2,1)} %get-tuple-element.87.refs_0_, bf16[128,12800]{1,0:T(8,128)(2,1)} %get-tuple-element.88.refs_1_, s32[4,1,3200]{2,1,0:T(1,128)} %reshape.514.refs_2_, bf16[128,1024]{1,0:T(8,128)(2,1)} %copy.241.weight_ref.refs_3_, ...), custom_call_target="tpu_custom_call" | custom-call | flops 5033164800 | bytes 52428800 | tf_op jit(solution)/shard_map/conv_backward/pallas_call | solution.py:291
  467.4 10.0 %collective-permute-start.38 = (bf16[8,1024]{1,0:T(8,128)(2,1)}, bf16[8,1024]{1,0:T(8,128)(2,1)}, u32[]{:S(2)}, u32[]{:S(2)}) collective-permute-start(bf16[8,1024]{1,0:T(8,128)(2,1)} %get-tuple-element.291), channel_id=1, source_target_pairs={{0,24},{2,26},{4,28},{6,30},{8,0},{10,2},{12,4},{14,6},{16,8},{18,... | collective-permute-start | bytes 49160 | tf_op jit(solution)/shard_map/ppermute | solution.py:46
  (558 shorter events, 228.6 us)
Async XLA Ops:
  7.2 132.7 %all-gather.3.cloned.1.call-start = ((), (), s32[]{:S(2)}) async-start(), calls=%async_computation.2 | async-start | bytes 8912896 | tf_op jit(solution)/shard_map/all_gather | solution.py:422
  9.8 198.1 %all-gather.5.cloned.1.call-start = ((), (), s32[]{:S(2)}) async-start(), calls=%async_computation.3 | async-start | bytes 10027008 | tf_op jit(solution)/shard_map/all_gather | solution.py:449
  9.9 38.2 %collective-permute-start.1 = (bf16[64,768]{1,0:T(8,128)(2,1)S(1)}, bf16[64,768]{1,0:T(8,128)(2,1)S(1)}, u32[]{:S(2)}, u32[]{:S(2)}) collective-permute-start(bf16[64,768]{1,0:T(8,128)(2,1)S(1)} %constant_dynamic-slice_fusion.2), channel_id=1, source_target_pairs={{0,2},{2,0},{4,6},{6,4},{8,10},{10,8},{12,14},{14,12},{16,18},{18,... | collective-permute-start | bytes 294920 | tf_op jit(solution)/shard_map/ppermute | solution.py:36
  10.6 60.0 %collective-permute-start = (s32[256,51]{1,0:T(8,128)S(1)}, s32[256,51]{1,0:T(8,128)S(1)}, u32[]{:S(2)}, u32[]{:S(2)}) collective-permute-start(s32[256,51]{1,0:T(8,128)S(1)} %copy.242), channel_id=1, source_target_pairs={{0,1},{1,0},{2,3},{3,2},{4,5},{5,4},{6,7},{7,6},{8,9},{9,8},{10,11... | collective-permute-start | bytes 156680 | tf_op jit(solution)/shard_map/ppermute | solution.py:50
  47.4 317.2 %reduce-scatter.3.cloned.1.call-start = ((), (), s32[]{:S(2)}) async-start(), calls=%async_computation.4 | async-start | bytes 10027008 | tf_op jit(solution)/shard_map/reduce_scatter | solution.py:540
  51.9 18.7 %collective-permute-start.3 = (bf16[64,768]{1,0:T(8,128)(2,1)S(1)}, bf16[64,768]{1,0:T(8,128)(2,1)S(1)}, u32[]{:S(2)}, u32[]{:S(2)}) collective-permute-start(bf16[64,768]{1,0:T(8,128)(2,1)S(1)} %get-tuple-element.252), channel_id=1, source_target_pairs={{0,16},{2,18},{4,20},{6,22},{8,24},{10,26},{12,28},{14,30},{16,0},... | collective-permute-start | bytes 294920 | tf_op jit(solution)/shard_map/ppermute | solution.py:46
  52.0 18.6 %collective-permute-start.4 = (bf16[64,768]{1,0:T(8,128)(2,1)S(1)}, bf16[64,768]{1,0:T(8,128)(2,1)S(1)}, u32[]{:S(2)}, u32[]{:S(2)}) collective-permute-start(bf16[64,768]{1,0:T(8,128)(2,1)S(1)} %get-tuple-element.252), channel_id=1, source_target_pairs={{0,8},{2,10},{4,12},{6,14},{8,16},{10,18},{12,20},{14,22},{16,24},... | collective-permute-start | bytes 294920 | tf_op jit(solution)/shard_map/ppermute | solution.py:46
  72.1 43.8 %collective-permute-start.13 = (bf16[48,3072]{1,0:T(8,128)(2,1)S(1)}, bf16[48,3072]{1,0:T(8,128)(2,1)}, u32[]{:S(2)}, u32[]{:S(2)}) collective-permute-start(bf16[48,3072]{1,0:T(8,128)(2,1)S(1)} %pad_maximum_fusion.14), channel_id=1, source_target_pairs={{0,8},{2,10},{4,12},{6,14},{8,16},{10,18},{12,20},{14,22},{16,24},... | collective-permute-start | bytes 884744 | tf_op jit(solution)/shard_map/ppermute | solution.py:46
  72.1 41.2 %collective-permute-start.12 = (bf16[48,3072]{1,0:T(8,128)(2,1)S(1)}, bf16[48,3072]{1,0:T(8,128)(2,1)}, u32[]{:S(2)}, u32[]{:S(2)}) collective-permute-start(bf16[48,3072]{1,0:T(8,128)(2,1)S(1)} %pad_maximum_fusion.14), channel_id=1, source_target_pairs={{0,16},{2,18},{4,20},{6,22},{8,24},{10,26},{12,28},{14,30},{16,0},... | collective-permute-start | bytes 884744 | tf_op jit(solution)/shard_map/ppermute | solution.py:46
  77.6 34.2 %collective-permute-start.11 = (bf16[48,3072]{1,0:T(8,128)(2,1)S(1)}, bf16[48,3072]{1,0:T(8,128)(2,1)}, u32[]{:S(2)}, u32[]{:S(2)}) collective-permute-start(bf16[48,3072]{1,0:T(8,128)(2,1)S(1)} %pad_maximum_fusion.14), channel_id=1, source_target_pairs={{0,24},{2,26},{4,28},{6,30},{8,0},{10,2},{12,4},{14,6},{16,8},{18,... | collective-permute-start | bytes 884744 | tf_op jit(solution)/shard_map/ppermute | solution.py:46
  80.9 38.3 %collective-permute-start.8 = (bf16[4,64,768]{2,1,0:T(8,128)(2,1)S(1)}, bf16[4,64,768]{2,1,0:T(8,128)(2,1)}, u32[]{:S(2)}, u32[]{:S(2)}) collective-permute-start(bf16[4,64,768]{2,1,0:T(8,128)(2,1)S(1)} %bitcast_dynamic-update-slice_fusion.16), channel_id=1, source_target_pairs={{0,2},{2,0},{4,6},{6,4},{8,10},{10,8},{12,14},{14,12},{16,18},{18,... | collective-permute-start | bytes 1179656 | tf_op jit(solution)/shard_map/ppermute | solution.py:36
  80.9 36.8 %collective-permute-start.7 = (bf16[4,64,768]{2,1,0:T(8,128)(2,1)S(1)}, bf16[4,64,768]{2,1,0:T(8,128)(2,1)}, u32[]{:S(2)}, u32[]{:S(2)}) collective-permute-start(bf16[4,64,768]{2,1,0:T(8,128)(2,1)S(1)} %bitcast_dynamic-update-slice_fusion.16), channel_id=1, source_target_pairs={{0,4},{2,6},{4,0},{6,2},{8,12},{10,14},{12,8},{14,10},{16,20},{18,... | collective-permute-start | bytes 1179656 | tf_op jit(solution)/shard_map/ppermute | solution.py:41
  111.7 26.1 %collective-permute-start.5 = (bf16[256,1024]{1,0:T(8,128)(2,1)S(1)}, bf16[256,1024]{1,0:T(8,128)(2,1)S(1)}, u32[]{:S(2)}, u32[]{:S(2)}) collective-permute-start(bf16[256,1024]{1,0:T(8,128)(2,1)S(1)} %get-tuple-element.249), channel_id=1, source_target_pairs={{0,1},{1,0},{2,3},{3,2},{4,5},{5,4},{6,7},{7,6},{8,9},{9,8},{10,11... | collective-permute-start | bytes 1572872 | tf_op jit(solution)/shard_map/ppermute | solution.py:50
  113.3 23.7 %collective-permute-start.6 = (bf16[256,1024]{1,0:T(8,128)(2,1)S(1)}, bf16[256,1024]{1,0:T(8,128)(2,1)S(1)}, u32[]{:S(2)}, u32[]{:S(2)}) collective-permute-start(bf16[256,1024]{1,0:T(8,128)(2,1)S(1)} %get-tuple-element.298), channel_id=1, source_target_pairs={{0,1},{1,0},{2,3},{3,2},{4,5},{5,4},{6,7},{7,6},{8,9},{9,8},{10,11... | collective-permute-start | bytes 1572872 | tf_op jit(solution)/shard_map/ppermute | solution.py:50
  116.9 39.6 %collective-permute-start.15 = (bf16[4,48,3072]{2,1,0:T(8,128)(2,1)S(1)}, bf16[4,48,3072]{2,1,0:T(8,128)(2,1)}, u32[]{:S(2)}, u32[]{:S(2)}) collective-permute-start(bf16[4,48,3072]{2,1,0:T(8,128)(2,1)S(1)} %bitcast_dynamic-update-slice_fusion.12), channel_id=1, source_target_pairs={{0,2},{2,0},{4,6},{6,4},{8,10},{10,8},{12,14},{14,12},{16,18},{18,... | collective-permute-start | bytes 3538952 | tf_op jit(solution)/shard_map/ppermute | solution.py:36
  117.7 35.4 %collective-permute-start.14 = (bf16[4,48,3072]{2,1,0:T(8,128)(2,1)S(1)}, bf16[4,48,3072]{2,1,0:T(8,128)(2,1)}, u32[]{:S(2)}, u32[]{:S(2)}) collective-permute-start(bf16[4,48,3072]{2,1,0:T(8,128)(2,1)S(1)} %bitcast_dynamic-update-slice_fusion.12), channel_id=1, source_target_pairs={{0,4},{2,6},{4,0},{6,2},{8,12},{10,14},{12,8},{14,10},{16,20},{18,... | collective-permute-start | bytes 3538952 | tf_op jit(solution)/shard_map/ppermute | solution.py:41
  119.3 19.6 %collective-permute-start.9 = (bf16[4,64,768]{2,1,0:T(8,128)(2,1)}, bf16[4,64,768]{2,1,0:T(8,128)(2,1)S(1)}, u32[]{:S(2)}, u32[]{:S(2)}) collective-permute-start(bf16[4,64,768]{2,1,0:T(8,128)(2,1)} %collective-permute-done.7), channel_id=1, source_target_pairs={{0,2},{2,0},{4,6},{6,4},{8,10},{10,8},{12,14},{14,12},{16,18},{18,... | collective-permute-start | bytes 1179656 | tf_op jit(solution)/shard_map/ppermute | solution.py:36
  171.1 18.6 %collective-permute-start.17 = (bf16[256,768]{1,0:T(8,128)(2,1)}, bf16[256,768]{1,0:T(8,128)(2,1)}, u32[]{:S(2)}, u32[]{:S(2)}) collective-permute-start(bf16[256,768]{1,0:T(8,128)(2,1)} %get-tuple-element.277), channel_id=1, source_target_pairs={{0,1},{1,0},{2,3},{3,2},{4,5},{5,4},{6,7},{7,6},{8,9},{9,8},{10,11... | collective-permute-start | bytes 1179656 | tf_op jit(solution)/shard_map/ppermute | solution.py:50
  237.8 222.4 %reduce-scatter.5.cloned.1.call-start = ((), (), s32[]{:S(2)}) async-start(), calls=%async_computation.5 | async-start | bytes 5292032 | tf_op jit(solution)/shard_map/reduce_scatter | solution.py:622
  314.0 37.2 %collective-permute-start.24 = (bf16[4,48,3072]{2,1,0:T(8,128)(2,1)}, bf16[4,48,3072]{2,1,0:T(8,128)(2,1)S(1)}, u32[]{:S(2)}, u32[]{:S(2)}) collective-permute-start(bf16[4,48,3072]{2,1,0:T(8,128)(2,1)} %fusion.74), channel_id=1, source_target_pairs={{0,4},{2,6},{4,0},{6,2},{8,12},{10,14},{12,8},{14,10},{16,20},{18,... | collective-permute-start | bytes 3538952 | tf_op jit(solution)/shard_map/ppermute | solution.py:41
  318.8 34.6 %collective-permute-start.25 = (bf16[4,2,128,1408]{3,2,1,0:T(8,128)(2,1)S(1)}, bf16[4,2,128,1408]{3,2,1,0:T(8,128)(2,1)}, u32[]{:S(2)}, u32[]{:S(2)}) collective-permute-start(bf16[4,2,128,1408]{3,2,1,0:T(8,128)(2,1)S(1)} %fusion.37), channel_id=1, source_target_pairs={{0,2},{2,0},{4,6},{6,4},{8,10},{10,8},{12,14},{14,12},{16,18},{18,... | collective-permute-start | bytes 8650760 | tf_op jit(solution)/shard_map/ppermute | solution.py:36
  328.6 29.8 %collective-permute-start.23 = (bf16[256,1024]{1,0:T(8,128)(2,1)}, bf16[256,1024]{1,0:T(8,128)(2,1)}, u32[]{:S(2)}, u32[]{:S(2)}) collective-permute-start(bf16[256,1024]{1,0:T(8,128)(2,1)} %get-tuple-element.278), channel_id=1, source_target_pairs={{0,1},{1,0},{2,3},{3,2},{4,5},{5,4},{6,7},{7,6},{8,9},{9,8},{10,11... | collective-permute-start | bytes 1572872 | tf_op jit(solution)/shard_map/ppermute | solution.py:50
  330.1 28.3 %collective-permute-start.26 = (bf16[256,1024]{1,0:T(8,128)(2,1)}, bf16[256,1024]{1,0:T(8,128)(2,1)}, u32[]{:S(2)}, u32[]{:S(2)}) collective-permute-start(bf16[256,1024]{1,0:T(8,128)(2,1)} %get-tuple-element.279), channel_id=1, source_target_pairs={{0,1},{1,0},{2,3},{3,2},{4,5},{5,4},{6,7},{7,6},{8,9},{9,8},{10,11... | collective-permute-start | bytes 1572872 | tf_op jit(solution)/shard_map/ppermute | solution.py:50
  357.3 33.7 %collective-permute-start.30 = (bf16[4,128,1408]{2,1,0:T(8,128)(2,1)}, bf16[4,128,1408]{2,1,0:T(8,128)(2,1)}, u32[]{:S(2)}, u32[]{:S(2)}) collective-permute-start(bf16[4,128,1408]{2,1,0:T(8,128)(2,1)} %fusion.59), channel_id=1, source_target_pairs={{0,4},{2,6},{4,0},{6,2},{8,12},{10,14},{12,8},{14,10},{16,20},{18,... | collective-permute-start | bytes 4325384 | tf_op jit(solution)/shard_map/ppermute | solution.py:41
  366.0 21.2 %collective-permute-start.29 = (bf16[48,3072]{1,0:T(8,128)(2,1)S(1)}, bf16[48,3072]{1,0:T(8,128)(2,1)S(1)}, u32[]{:S(2)}, u32[]{:S(2)}) collective-permute-start(bf16[48,3072]{1,0:T(8,128)(2,1)S(1)} %get-tuple-element.272), channel_id=1, source_target_pairs={{0,8},{2,10},{4,12},{6,14},{8,16},{10,18},{12,20},{14,22},{16,24},... | collective-permute-start | bytes 884744 | tf_op jit(solution)/shard_map/ppermute | solution.py:46
  369.8 19.6 %collective-permute-start.28 = (bf16[48,3072]{1,0:T(8,128)(2,1)S(1)}, bf16[48,3072]{1,0:T(8,128)(2,1)S(1)}, u32[]{:S(2)}, u32[]{:S(2)}) collective-permute-start(bf16[48,3072]{1,0:T(8,128)(2,1)S(1)} %get-tuple-element.273), channel_id=1, source_target_pairs={{0,16},{2,18},{4,20},{6,22},{8,24},{10,26},{12,28},{14,30},{16,0},... | collective-permute-start | bytes 884744 | tf_op jit(solution)/shard_map/ppermute | solution.py:46
  369.8 19.6 %collective-permute-start.27 = (bf16[48,3072]{1,0:T(8,128)(2,1)S(1)}, bf16[48,3072]{1,0:T(8,128)(2,1)S(1)}, u32[]{:S(2)}, u32[]{:S(2)}) collective-permute-start(bf16[48,3072]{1,0:T(8,128)(2,1)S(1)} %get-tuple-element.274), channel_id=1, source_target_pairs={{0,24},{2,26},{4,28},{6,30},{8,0},{10,2},{12,4},{14,6},{16,8},{18,... | collective-permute-start | bytes 884744 | tf_op jit(solution)/shard_map/ppermute | solution.py:46
  409.9 27.0 %collective-permute-start.35 = (bf16[48,3072]{1,0:T(8,128)(2,1)S(1)}, bf16[48,3072]{1,0:T(8,128)(2,1)}, u32[]{:S(2)}, u32[]{:S(2)}) collective-permute-start(bf16[48,3072]{1,0:T(8,128)(2,1)S(1)} %get-tuple-element.103), channel_id=1, source_target_pairs={{0,1},{1,0},{2,3},{3,2},{4,5},{5,4},{6,7},{7,6},{8,9},{9,8},{10,11... | collective-permute-start | bytes 884744 | tf_op jit(solution)/shard_map/ppermute | solution.py:50
  412.4 42.0 %collective-permute-start.34 = (bf16[128,1408]{1,0:T(8,128)(2,1)}, bf16[128,1408]{1,0:T(8,128)(2,1)}, u32[]{:S(2)}, u32[]{:S(2)}) collective-permute-start(bf16[128,1408]{1,0:T(8,128)(2,1)} %get-tuple-element.259), channel_id=1, source_target_pairs={{0,8},{2,10},{4,12},{6,14},{8,16},{10,18},{12,20},{14,22},{16,24},... | collective-permute-start | bytes 1081352 | tf_op jit(solution)/shard_map/ppermute | solution.py:46
  419.0 35.5 %collective-permute-start.33 = (bf16[128,1408]{1,0:T(8,128)(2,1)}, bf16[128,1408]{1,0:T(8,128)(2,1)}, u32[]{:S(2)}, u32[]{:S(2)}) collective-permute-start(bf16[128,1408]{1,0:T(8,128)(2,1)} %get-tuple-element.260), channel_id=1, source_target_pairs={{0,16},{2,18},{4,20},{6,22},{8,24},{10,26},{12,28},{14,30},{16,0},... | collective-permute-start | bytes 1081352 | tf_op jit(solution)/shard_map/ppermute | solution.py:46
  420.3 34.1 %collective-permute-start.32 = (bf16[128,1408]{1,0:T(8,128)(2,1)}, bf16[128,1408]{1,0:T(8,128)(2,1)}, u32[]{:S(2)}, u32[]{:S(2)}) collective-permute-start(bf16[128,1408]{1,0:T(8,128)(2,1)} %get-tuple-element.261), channel_id=1, source_target_pairs={{0,24},{2,26},{4,28},{6,30},{8,0},{10,2},{12,4},{14,6},{16,8},{18,... | collective-permute-start | bytes 1081352 | tf_op jit(solution)/shard_map/ppermute | solution.py:46
  464.3 25.8 %collective-permute-start.44 = (bf16[128,2816]{1,0:T(8,128)(2,1)}, bf16[128,2816]{1,0:T(8,128)(2,1)}, u32[]{:S(2)}, u32[]{:S(2)}) collective-permute-start(bf16[128,2816]{1,0:T(8,128)(2,1)} %maximum_maximum_fusion), channel_id=1, source_target_pairs={{0,1},{1,0},{2,3},{3,2},{4,5},{5,4},{6,7},{7,6},{8,9},{9,8},{10,11... | collective-permute-start | bytes 2162696 | tf_op jit(solution)/shard_map/ppermute | solution.py:50
  (112 other events, 1026.2 us)
Sparse Core Ops, SparseCore 0:
  10.8 112.1 all-gather.2
  125.9 81.9 all-gather.4
  237.9 121.4 reduce-scatter.2
  364.8 95.3 reduce-scatter.4
